TPU v7x, 128 devices: a whole 4x4x4 slice. The times are simulated.
128 devices in a mesh: fsdp: 4 (over y_lo, core), ctx: 8 (over y_hi, z), tp: 4 (over x).
Axes of the slice: x: 4, y: 4 (y_hi: 2, y_lo: 2; y = y_hi * 2 + y_lo), z: 4, core: 2. Of those that a mesh axis runs over, the one named last changes fastest.
Arguments:
- layer_input: bfloat16 [16, 2048, 768], P('fsdp', 'ctx'), may hold values from -6 to 6
- segment_ids: int32 [16, 2048], P('fsdp', 'ctx'), may hold values from 0 to 3, never falling along the last dimension, each value on 1 to 1280 neighbouring positions
- proj_weight: bfloat16 [3, 768, 768], P(None, 'fsdp', 'tp'), may hold values from -0.21875 to 0.21875
- proj_bias: bfloat16 [2, 768], P(None, 'tp'), may hold values from -3 to 3
- out_weight: bfloat16 [768, 768], P('tp', 'fsdp'), may hold values from -2.5 to 2.5
- out_bias: bfloat16 [768], P('fsdp'), may hold values from -3 to 3
- first_gain: bfloat16 [768], P('fsdp'), may hold values from 0.099609375 to 1.8984375
- first_shift: bfloat16 [768], P('fsdp'), may hold values from -2 to 2
- up_weight: bfloat16 [768, 3072], P('fsdp', 'tp'), may hold values from -0.21875 to 0.21875
- up_bias: bfloat16 [3072], P('tp'), may hold values from -3 to 3
- down_weight: bfloat16 [3072, 768], P('tp', 'fsdp'), may hold values from -0.15625 to 0.15625
- down_bias: bfloat16 [768], P('fsdp'), may hold values from -2 to 2
- second_gain: bfloat16 [768], P('fsdp'), may hold values from 0.099609375 to 1.8984375
- second_shift: bfloat16 [768], P('fsdp'), may hold values from -2 to 2
- cotangent: bfloat16 [16, 2048, 768], P('fsdp', 'ctx'), may hold values from -6 to 6
Outputs:
- layer_output: bfloat16 [16, 2048, 768], P('fsdp', 'ctx')
- input_grad: float32 [16, 2048, 768], P('fsdp', 'ctx')
- proj_grad: float32 [3, 768, 768], P(None, ('fsdp', 'ctx'), 'tp')
- proj_bias_grad: float32 [2, 768], P(None, 'tp')
- out_grad: float32 [768, 768], P('tp', ('fsdp', 'ctx'))
- out_bias_grad: float32 [768], P(('fsdp', 'ctx'))
- first_gain_grad: float32 [768], P(('fsdp', 'ctx'))
- first_shift_grad: float32 [768], P(('fsdp', 'ctx'))
- up_grad: float32 [768, 3072], P(('fsdp', 'ctx'), 'tp')
- up_bias_grad: float32 [3072], P('tp')
- down_grad: float32 [3072, 768], P('tp', ('fsdp', 'ctx'))
- down_bias_grad: float32 [768], P(('fsdp', 'ctx'))
- second_gain_grad: float32 [768], P(('fsdp', 'ctx'))
- second_shift_grad: float32 [768], P(('fsdp', 'ctx'))
Inputs may be any that keep to these rules, and one draw needn't show every extreme that they name: `segment_ids`: ids never fall along a sequence; every document spans 1 to 1280 positions, and one in each sequence spans exactly 1280.
All inputs are finite; a program needn't handle non-finite values.
Results may differ from a plain program's by a relative error of at most 0.039.
Values may be sent and summed in bfloat16 or wider, within the bound.
A program may use at most 192 MiB of HBM per device.

v0:
```python
import jax
import jax.numpy as jnp
from jax import lax
from jax.sharding import PartitionSpec as P

HEAD_DIM = 64


norm_eps = 1e-12
masked_score = -1e30


def turned_gather(arrays, axis, dims):
    turned = [jnp.moveaxis(a, dim, 0) for a, dim in zip(arrays, dims)]
    widths = [t[0].size for t in turned]
    both = jnp.concatenate([t.reshape(-1, w) for t, w in zip(turned, widths)], axis=1)
    out = lax.all_gather(both, axis, axis=0, tiled=True)
    pieces = jnp.split(out, [sum(widths[:k]) for k in range(1, len(widths))], axis=1)
    return tuple(
        (
            jnp.moveaxis(b.reshape(-1, *t.shape[1:]), 0, dim)
            for b, t, dim in zip(pieces, turned, dims)
        )
    )


def sent_together(arrays, axis, dim, along):
    ends, at = ([], 0)
    for a in arrays[:-1]:
        at += a.shape[along]
        ends.append(at)
    both = jnp.concatenate(arrays, axis=along)
    return tuple(jnp.split(lax.all_gather(both, axis, axis=dim, tiled=True), ends, axis=along))


def rows_for(lines, count):
    spare = -len(lines) % count
    return jnp.pad(lines, [(0, spare)] + [(0, 0)] * (lines.ndim - 1))


def sum_by_parts(x, axis):
    lines = x.reshape(-1, *x.shape[1:][-1:])
    padded = rows_for(lines, lax.axis_size(axis))
    own = lax.psum_scatter(padded, axis, scatter_dimension=0, tiled=True)
    whole = lax.all_gather(own, axis, axis=0, tiled=True)
    return whole[: len(lines)].reshape(x.shape)


def cut_along(x, dim, count):
    shape = x.shape
    pieces = x.reshape(*shape[:dim], count, shape[dim] // count, *shape[dim + 1 :])
    return jnp.moveaxis(pieces, dim, 0)


def sum_together(arrays, axis, dims):
    count = lax.axis_size(axis)
    pieces = [cut_along(a, dim, count) for a, dim in zip(arrays, dims)]
    lines = jnp.concatenate([b.reshape(count, -1) for b in pieces], axis=1)
    width = max(16, -(-lines.shape[1] // 1024) * 8)
    lines = jnp.pad(lines, ((0, 0), (0, width * 128 - lines.shape[1]))).reshape(-1, 128)
    flat, at, outs = (lax.psum_scatter(lines, axis, tiled=True).reshape(-1), 0, [])
    for b in pieces:
        part = b[0]
        outs.append(flat[at : at + part.size].reshape(part.shape))
        at += part.size
    return tuple(outs)


def sent_to_all(x, axis):
    count = lax.axis_size(axis)
    return lax.all_to_all(jnp.broadcast_to(x[None], (count, *x.shape)), axis, 0, 0, tiled=True)


def of_everyone(x, axis):
    return sent_to_all(x, axis).sum(axis=0)


def packed_total(arrays, axis):
    ends = [0]
    for a in arrays:
        ends.append(ends[-1] + a.size)
    subtotal = of_everyone(jnp.concatenate([a.ravel() for a in arrays]), axis)
    return tuple((subtotal[b:e].reshape(a.shape) for a, b, e in zip(arrays, ends, ends[1:])))


def layer_norm(values_in, gain, shift):
    centre = jnp.mean(values_in, axis=-1, keepdims=True)
    centred = values_in - centre
    spread = jnp.mean(centred * centred, axis=-1, keepdims=True)
    return centred * lax.rsqrt(spread + norm_eps) * gain + shift


def gelu_exact(values_in):
    return jax.nn.gelu(values_in, approximate=False)


def doc_scores(queries, key_rows, query_docs, key_docs):
    raw_scores = jnp.einsum(
        "sqhd,skhd->shqk", queries, key_rows, preferred_element_type=jnp.float32
    ) * HEAD_DIM ** (-0.5)
    same_doc = query_docs[:, None, :, None] == key_docs[:, None, None, :]
    return (raw_scores, same_doc)


def whole_attention(queries, key_rows, value_rows, query_docs, key_docs):
    raw_scores, same_doc = doc_scores(queries, key_rows, query_docs, key_docs)
    row_high = jnp.max(jnp.where(same_doc, raw_scores, masked_score), axis=-1, keepdims=True)
    exp_terms = jnp.where(same_doc, jnp.exp(raw_scores - row_high), 0.0)
    row_total = jnp.sum(exp_terms, axis=-1, keepdims=True)
    attn_probs = (exp_terms / row_total).astype(jnp.bfloat16)
    attended = jnp.einsum(
        "shqk,skhd->sqhd", attn_probs, value_rows, preferred_element_type=jnp.float32
    )
    return (attended, row_high + jnp.log(row_total))


def queries_back(queries, key_rows, value_rows, query_docs, key_docs, log_total, grad_context):
    raw_scores, same_doc = doc_scores(queries, key_rows, query_docs, key_docs)
    attn_probs = jnp.where(same_doc, jnp.exp(raw_scores - log_total), 0.0)
    grad_probs = jnp.einsum(
        "sqhd,skhd->shqk", grad_context, value_rows, preferred_element_type=jnp.float32
    )
    row_delta = jnp.sum(attn_probs * grad_probs, axis=-1, keepdims=True)
    grad_scores = (attn_probs * (grad_probs - row_delta)).astype(jnp.bfloat16)
    grad_queries = jnp.einsum(
        "shqk,skhd->sqhd", grad_scores, key_rows, preferred_element_type=jnp.float32
    ) * HEAD_DIM ** (-0.5)
    return (grad_queries, row_delta)


def keys_back(
    all_queries,
    own_keys,
    own_values,
    all_query_docs,
    own_docs,
    all_log_total,
    all_delta,
    all_grad_context,
):
    raw_scores, same_doc = doc_scores(all_queries, own_keys, all_query_docs, own_docs)
    attn_probs = jnp.where(same_doc, jnp.exp(raw_scores - all_log_total), 0.0)
    probs_low = attn_probs.astype(jnp.bfloat16)
    grad_probs = jnp.einsum(
        "sqhd,skhd->shqk", all_grad_context, own_values, preferred_element_type=jnp.float32
    )
    grad_scores = (attn_probs * (grad_probs - all_delta)).astype(jnp.bfloat16)
    grad_keys = jnp.einsum(
        "shqk,sqhd->skhd", grad_scores, all_queries, preferred_element_type=jnp.float32
    ) * HEAD_DIM ** (-0.5)
    grad_values = jnp.einsum(
        "shqk,sqhd->skhd", probs_low, all_grad_context, preferred_element_type=jnp.float32
    )
    return (grad_keys, grad_values)


def shards(
    layer_input,
    segment_ids,
    proj_weight,
    proj_bias,
    out_weight,
    out_bias,
    first_gain,
    first_shift,
    up_weight,
    up_bias,
    down_weight,
    down_bias,
    second_gain,
    second_shift,
    cotangent,
):
    seq_count, group_len, model_width = layer_input.shape
    local_cols = proj_weight.shape[2]
    head_count = local_cols // HEAD_DIM
    row_count = seq_count * group_len
    (
        proj_full,
        out_full,
        up_full,
        down_full,
        out_shift,
        down_shift,
        gain_one,
        shift_one,
        gain_two,
        shift_two,
    ) = turned_gather(
        (
            proj_weight,
            out_weight,
            up_weight,
            down_weight,
            out_bias,
            down_bias,
            first_gain,
            first_shift,
            second_gain,
            second_shift,
        ),
        "fsdp",
        (1, 1, 0, 1, 0, 0, 0, 0, 0, 0),
    )
    gain_one = gain_one.astype(jnp.float32)
    shift_one = shift_one.astype(jnp.float32)
    gain_two = gain_two.astype(jnp.float32)
    shift_two = shift_two.astype(jnp.float32)
    flat_rows = layer_input.reshape(row_count, model_width)
    bias_pair = proj_bias.astype(jnp.float32)
    proj_pre = jnp.einsum("rd,tdc->trc", flat_rows, proj_full, preferred_element_type=jnp.float32)
    head_shape = (seq_count, group_len, head_count, HEAD_DIM)
    queries = (proj_pre[0] + bias_pair[0]).astype(jnp.bfloat16).reshape(head_shape)
    key_rows = proj_pre[1].astype(jnp.bfloat16).reshape(head_shape)
    value_rows = (proj_pre[2] + bias_pair[1]).astype(jnp.bfloat16).reshape(head_shape)
    all_keys, all_values, all_docs = (
        *sent_together((key_rows, value_rows), "ctx", 1, 0),
        lax.all_gather(segment_ids, "ctx", axis=1, tiled=True),
    )
    attended, log_total = whole_attention(queries, all_keys, all_values, segment_ids, all_docs)
    context = attended.reshape(row_count, local_cols).astype(jnp.bfloat16)
    attn_part = jnp.dot(context, out_full, preferred_element_type=jnp.float32)
    attn_full = lax.psum(attn_part.astype(jnp.bfloat16), "tp").astype(jnp.float32)
    first_sum = flat_rows.astype(jnp.float32) + attn_full + out_shift.astype(jnp.float32)
    first_norm = layer_norm(first_sum, gain_one, shift_one)
    norm_low = first_norm.astype(jnp.bfloat16)
    up_pre = jnp.dot(norm_low, up_full, preferred_element_type=jnp.float32) + up_bias.astype(
        jnp.float32
    )
    activated = gelu_exact(up_pre).astype(jnp.bfloat16)
    ffn_part = jnp.dot(activated, down_full, preferred_element_type=jnp.float32)
    ffn_full = lax.psum(ffn_part.astype(jnp.bfloat16), "tp").astype(jnp.float32)
    second_sum = first_norm + ffn_full + down_shift.astype(jnp.float32)
    second_norm, second_pull = jax.vjp(layer_norm, second_sum, gain_two, shift_two)
    layer_output = second_norm.astype(jnp.bfloat16).reshape(seq_count, group_len, model_width)
    grad_second, grad_gain_two, grad_shift_two = second_pull(
        cotangent.reshape(row_count, model_width).astype(jnp.float32)
    )
    grad_down_bias = jnp.sum(grad_second, axis=0)
    second_low = grad_second.astype(jnp.bfloat16)
    grad_down = jnp.einsum("rf,rd->fd", activated, second_low, preferred_element_type=jnp.float32)
    grad_active = jnp.einsum(
        "rd,fd->rf", second_low, down_full, preferred_element_type=jnp.float32
    ).astype(jnp.bfloat16)
    gelu_value, gelu_pull = jax.vjp(gelu_exact, up_pre)
    grad_up_pre = gelu_pull(grad_active.astype(jnp.float32))[0]
    grad_up_bias = jnp.sum(grad_up_pre, axis=0)
    up_low = grad_up_pre.astype(jnp.bfloat16)
    grad_up = jnp.einsum("rd,rf->df", norm_low, up_low, preferred_element_type=jnp.float32)
    norm_part = jnp.einsum("rf,df->rd", up_low, up_full, preferred_element_type=jnp.float32)
    grad_norm = grad_second + lax.psum(norm_part.astype(jnp.bfloat16), "tp").astype(jnp.float32)
    first_value, first_pull = jax.vjp(layer_norm, first_sum, gain_one, shift_one)
    grad_first, grad_gain_one, grad_shift_one = first_pull(grad_norm)
    grad_out_bias = jnp.sum(grad_first, axis=0)
    first_low = grad_first.astype(jnp.bfloat16)
    grad_out = jnp.einsum("rc,rd->cd", context, first_low, preferred_element_type=jnp.float32)
    grad_context = (
        jnp.einsum("rd,cd->rc", first_low, out_full, preferred_element_type=jnp.float32)
        .astype(jnp.bfloat16)
        .reshape(head_shape)
    )
    back_keys, back_values, back_docs = (all_keys, all_values, all_docs)
    grad_queries, row_delta = queries_back(
        queries, back_keys, back_values, segment_ids, back_docs, log_total, grad_context
    )
    all_queries, all_grad_context, all_query_docs = (
        *sent_together((queries, grad_context), "ctx", 1, 0),
        lax.all_gather(segment_ids, "ctx", axis=1, tiled=True),
    )
    all_log_total, all_delta = sent_together((log_total, row_delta), "ctx", 2, 0)
    grad_keys, grad_values = keys_back(
        all_queries,
        key_rows,
        value_rows,
        all_query_docs,
        segment_ids,
        all_log_total,
        all_delta,
        all_grad_context,
    )
    grad_query_flat = grad_queries.reshape(row_count, local_cols)
    grad_value_flat = grad_values.reshape(row_count, local_cols)
    grad_proj_bias = jnp.stack([jnp.sum(grad_query_flat, axis=0), jnp.sum(grad_value_flat, axis=0)])
    grad_stack = jnp.stack(
        [grad_query_flat, grad_keys.reshape(row_count, local_cols), grad_value_flat]
    ).astype(jnp.bfloat16)
    grad_proj = jnp.einsum("rd,trc->tdc", flat_rows, grad_stack, preferred_element_type=jnp.float32)
    input_part = jnp.einsum(
        "trc,tdc->rd", grad_stack, proj_full, preferred_element_type=jnp.float32
    )
    input_grad = (
        grad_first + sum_by_parts(input_part.astype(jnp.bfloat16), "tp").astype(jnp.float32)
    ).reshape(seq_count, group_len, model_width)
    (
        proj_grad,
        out_grad,
        up_grad,
        down_grad,
        out_bias_grad,
        down_bias_grad,
        first_gain_grad,
        first_shift_grad,
        second_gain_grad,
        second_shift_grad,
    ) = tuple(
        (
            part.astype(jnp.float32)
            for part in sum_together(
                (
                    grad_proj.astype(jnp.bfloat16),
                    grad_out.astype(jnp.bfloat16),
                    grad_up.astype(jnp.bfloat16),
                    grad_down.astype(jnp.bfloat16),
                    grad_out_bias.astype(jnp.bfloat16),
                    grad_down_bias.astype(jnp.bfloat16),
                    grad_gain_one.astype(jnp.bfloat16),
                    grad_shift_one.astype(jnp.bfloat16),
                    grad_gain_two.astype(jnp.bfloat16),
                    grad_shift_two.astype(jnp.bfloat16),
                ),
                ("fsdp", "ctx"),
                (1, 1, 0, 1, 0, 0, 0, 0, 0, 0),
            )
        )
    )
    proj_bias_grad, up_bias_grad = packed_total((grad_proj_bias, grad_up_bias), ("fsdp", "ctx"))
    return (
        layer_output,
        input_grad,
        proj_grad,
        proj_bias_grad,
        out_grad,
        out_bias_grad,
        first_gain_grad,
        first_shift_grad,
        up_grad,
        up_bias_grad,
        down_grad,
        down_bias_grad,
        second_gain_grad,
        second_shift_grad,
    )


def solution(mesh):
    placed = (
        P("fsdp", "ctx", None),
        P("fsdp", "ctx"),
        P(None, "fsdp", "tp"),
        P(None, "tp"),
        P("tp", "fsdp"),
        P("fsdp"),
        P("fsdp"),
        P("fsdp"),
        P("fsdp", "tp"),
        P("tp"),
        P("tp", "fsdp"),
        P("fsdp"),
        P("fsdp"),
        P("fsdp"),
        P("fsdp", "ctx", None),
    )
    return jax.shard_map(
        shards,
        mesh=mesh,
        in_specs=placed,
        out_specs=(
            P("fsdp", "ctx", None),
            P("fsdp", "ctx", None),
            P(None, ("fsdp", "ctx"), "tp"),
            P(None, "tp"),
            P("tp", ("fsdp", "ctx")),
            P(("fsdp", "ctx")),
            P(("fsdp", "ctx")),
            P(("fsdp", "ctx")),
            P(("fsdp", "ctx"), "tp"),
            P("tp"),
            P("tp", ("fsdp", "ctx")),
            P(("fsdp", "ctx")),
            P(("fsdp", "ctx")),
            P(("fsdp", "ctx")),
        ),
        check_vma=False,
    )
```

profile of v0, /device:TPU:1, one launch (start us, length us, event | category | flops | bytes accessed | tf_op | source)
XLA Modules:
  0.0 778.3 jit_solution(16677096041173922460)
XLA Ops:
  14.1 3.2 concatenate.18
  17.5 46.3 %all-gather.5.cloned.1.call-done = bf16[768,2310]{1,0:T(8,128)(2,1)} async-done(((bf16[192,2310]{1,0:T(8,128)(2,1)}), bf16[768,2310]{1,0:T(8,128)(2,1)}) %all-gather.5.cloned.1.call-update) | async-done | bytes 3548176 | tf_op jit(solution)/shard_map/all_gather | solution.py:17
  70.7 28.1 %all_gather.21 = s32[4,2048]{1,0:T(4,128)S(1)} all-gather(s32[4,256]{1,0:T(4,128)S(1)} %copy-done.34), channel_id=1, replica_groups=mesh['fsdp'=4,'ctx'=8,'tp'=4] {'ctx'}, dimensions={1}, use_global_device_ids=true | all-gather | bytes 36864 | tf_op jit(solution)/shard_map/all_gather | solution.py:218
  100.2 2.1 squeeze.8
  102.5 62.1 %all-gather.7.cloned.1.call-done = bf16[8,2048,3,64]{1,3,2,0:T(8,128)(2,1)} async-done(((bf16[8,256,3,64]{1,3,2,0:T(8,128)(2,1)}), bf16[8,2048,3,64]{1,3,2,0:T(8,128)(2,1)}) %all-gather.7.cloned.1.call-update) | async-done | bytes 6291472 | tf_op jit(solution)/shard_map/all_gather | solution.py:33
  164.5 12.8 %select_reduce_fusion = (f32[4,3,256]{2,1,0:T(4,128)S(1)}, f32[4,3,256,2048]{3,2,1,0:T(8,128)}) fusion(pred[4,256,2048]{2,1,0:T(8,128)(4,1)S(1)} %broadcast_compare_fusion.1, bf16[4,256,3,64]{1,3,2,0:T(8,128)(2,1)S(1)} %fusion.49, bf16[8,2048,3,64]{1,3,2,0:T(8,128)(2,1)} %all-gather.7.cloned.1.call-done), kind=kOutput, calls=%fused_computation.7 | convolution fusion | flops 824177664 | bytes 30814208 | tf_op jit(solution)/shard_map/sqhd,skhd->shqk/dot_general | solution.py:98
  177.3 12.0 %fusion = f32[4,3,256]{2,1,0:T(4,128)S(1)} fusion(f32[4,3,256,2048]{3,2,1,0:T(8,128)} %get-tuple-element.114, f32[4,3,256]{2,1,0:T(4,128)S(1)} %get-tuple-element.113, pred[4,256,2048]{2,1,0:T(8,128)(4,1)S(1)} %broadcast_compare_fusion.1), kind=kLoop, calls=%fused_computation.8 | loop fusion | flops 25162752 | bytes 27287552 | tf_op jit(solution)/shard_map/reduce_sum | solution.py:109
  189.3 13.3 %fusion.42 = bf16[4,256,3,64]{1,3,2,0:T(8,128)(2,1)S(1)} fusion(bf16[8,2048,3,64]{1,3,2,0:T(8,128)(2,1)} %all-gather.7.cloned.1.call-done, f32[4,3,256,2048]{3,2,1,0:T(8,128)} %get-tuple-element.114, f32[4,3,256]{2,1,0:T(4,128)S(1)} %fusion, f32[4,3,256]{2,1,0:T(4,128)S(1)} %get-tuple-element.113, pred[4,256,2048]{2,1,0:T(8,128)(4,1)S(1)} %broadcast_compare_fusion.1), kind=kOutput, calls=%fused_computation.90 | convolution fusion | flops 836960256 | bytes 33972224 | tf_op jit(solution)/shard_map/shqk,skhd->sqhd/dot_general | solution.py:111
  203.8 3.0 convolution_convert_fusion.3
  207.2 2.4 convert_reduce_fusion.1
  209.6 45.8 %all-reduce.7.cloned.1.call-done = bf16[1024,768]{1,0:T(8,128)(2,1)} async-done(((bf16[1024,768]{1,0:T(8,128)(2,1)}), bf16[1024,768]{1,0:T(8,128)(2,1)}) %all-reduce.7.cloned.1.call-update) | async-done | bytes 1572880 | tf_op jit(solution)/shard_map/psum | solution.py:223
  255.5 2.1 fusion.31
  257.6 2.4 multiply_reduce_fusion.4
  260.1 9.6 %multiply_convert_fusion.4 = (bf16[1024,768]{1,0:T(8,128)(2,1)S(1)}, f32[1024,768]{1,0:T(8,128)}, f32[1024,768]{1,0:T(8,128)}) fusion(f32[768]{0:T(1024)S(1)} %convert_element_type.279, bf16[768,2310]{1,0:T(8,128)(2,1)S(1)} %copy-done.21, f32[1024,768]{1,0:T(8,128)S(1)} %get-tuple-element.93, f32[768]{0:T(1024)S(1)} %get-tuple-element.78, ...), kind=kOutput, calls=%fused_computation.49 | convolution fusion | flops 1263009792 | bytes 12206080 | tf_op jit(solution)/shard_map/dot_general | solution.py:227
  270.9 2.6 convolution_convert_fusion.2
  273.8 50.3 %all-reduce.9.cloned.1.call-done = bf16[1024,768]{1,0:T(8,128)(2,1)} async-done(((bf16[1024,768]{1,0:T(8,128)(2,1)}), bf16[1024,768]{1,0:T(8,128)(2,1)}) %all-reduce.9.cloned.1.call-update) | async-done | bytes 1572880 | tf_op jit(solution)/shard_map/psum | solution.py:232
  324.2 2.4 fusion.73
  327.9 1.8 fusion.19
  329.8 2.6 fusion.72
  333.3 3.1 fusion.79
  337.6 2.6 convolution_convert_fusion
  340.3 50.6 %all-reduce.11.cloned.1.call-done = bf16[1024,768]{1,0:T(8,128)(2,1)} async-done(((bf16[1024,768]{1,0:T(8,128)(2,1)}), bf16[1024,768]{1,0:T(8,128)(2,1)}) %all-reduce.11.cloned.1.call-update) | async-done | bytes 1572880 | tf_op jit(solution)/shard_map/psum | solution.py:251
  390.9 4.4 multiply_reduce_fusion.1
  395.3 1.6 fusion.71
  396.9 1.6 copy-done.4
  398.5 2.8 convolution_convert_fusion.7
  402.7 2.0 pad_maximum_fusion.1
  405.2 1.7 reduce_sum.205
  407.6 4.9 broadcast_compare_fusion
  413.2 4.2 convolution_convert_fusion.5
  417.4 2.6 reshape_reshape.3
  420.0 21.4 %multiply_reduce_fusion = (f32[4,3,256]{2,1,0:T(4,128)S(1)}, f32[4,3,256,2048]{3,2,1,0:T(8,128)}) fusion(f32[4,3,256,2048]{3,2,1,0:T(8,128)} %get-tuple-element.114, f32[4,3,256]{2,1,0:T(4,128)S(1)} %log_add_fusion, pred[4,256,2048]{2,1,0:T(8,128)(4,1)} %copy-done.1, bf16[8,2048,3,64]{1,3,2,0:T(8,128)(2,1)} %all-gather.7.cloned.1.call-done, ...), kind=kOutput, calls=%fused_computation.3 | convolution fusion | flops 836760576 | bytes 55992320 | tf_op jit(solution)/shard_map/sqhd,skhd->shqk/dot_general | solution.py:120
  441.5 19.5 %fusion.77 = (f32[3,64]{1,0:T(4,128)}, bf16[4,256,3,64]{1,3,2,0:T(8,128)(2,1)S(1)}) fusion(bf16[8,2048,3,64]{1,3,2,0:T(8,128)(2,1)S(1)} %bitcast.94, f32[4,3,256,2048]{3,2,1,0:T(8,128)} %get-tuple-element.117, f32[4,3,256,2048]{3,2,1,0:T(8,128)} %get-tuple-element.114, f32[4,3,256]{2,1,0:T(4,128)S(1)} %get-tuple-element.116, ...), kind=kOutput, calls=%fused_computation.166 | convolution fusion | flops 843644736 | bytes 59138816 | tf_op jit(solution)/shard_map/shqk,skhd->sqhd/dot_general | solution.py:125
  461.6 30.1 %all_gather.23 = f32[8,3,2048,1]{2,1,0,3:T(4,128)S(1)} all-gather(f32[8,3,256,1]{2,1,0,3:T(4,128)S(1)} %pad_maximum_fusion.2), channel_id=1, replica_groups=mesh['fsdp'=4,'ctx'=8,'tp'=4] {'ctx'}, dimensions={2}, use_global_device_ids=true | all-gather | bytes 221184 | tf_op jit(solution)/shard_map/all_gather | solution.py:33
  492.5 8.1 %all-gather.9.cloned.1.call-done = bf16[8,2048,3,64]{1,3,2,0:T(8,128)(2,1)} async-done(((bf16[8,256,3,64]{1,3,2,0:T(8,128)(2,1)}), bf16[8,2048,3,64]{1,3,2,0:T(8,128)(2,1)}) %all-gather.9.cloned.1.call-update) | async-done | bytes 6291472 | tf_op jit(solution)/shard_map/all_gather | solution.py:33
  500.5 12.3 %fusion.80 = f32[4,3,2048,256]{3,2,1,0:T(8,128)} fusion(bf16[8,2048,3,64]{1,3,2,0:T(8,128)(2,1)} %all-gather.9.cloned.1.call-done, bf16[4,256,3,64]{1,3,2,0:T(8,128)(2,1)S(1)} %copy-done.18), kind=kOutput, calls=%fused_computation.169 | convolution fusion | flops 805306368 | bytes 31850496 | tf_op jit(solution)/shard_map/sqhd,skhd->shqk/dot_general | solution.py:144
  512.8 10.1 %fusion.66 = f32[4,3,2048,256]{3,2,1,0:T(8,128)} fusion(bf16[8,2048,3,64]{1,3,2,0:T(8,128)(2,1)S(1)} %copy-done, bf16[4,256,3,64]{1,0,3,2:T(4,128)(2,1)S(1)} %copy-done.16), kind=kOutput, calls=%fused_computation.159 | convolution fusion | flops 805306368 | bytes 31850496 | tf_op jit(solution)/shard_map/sqhd,skhd->shqk/dot_general | solution.py:98
  522.9 16.5 %fusion.43 = bf16[4,256,3,64]{1,3,2,0:T(8,128)(2,1)S(1)} fusion(bf16[8,2048,3,64]{1,3,2,0:T(8,128)(2,1)S(1)} %copy-done, f32[4,3,2048,256]{3,2,1,0:T(8,128)} %fusion.80, f32[4,3,2048,256]{3,2,1,0:T(8,128)} %fusion.66, f32[4,3,2048]{2,1,0:T(4,128)S(1)} %get-tuple-element.106, f32[4,3,2048]{2,1,0:T(4,128)S(1)} %get-tuple-element.105, ...), kind=kOutput, calls=%fused_computation.91 | convolution fusion | flops 843448320 | bytes 59310080 | tf_op jit(solution)/shard_map/shqk,sqhd->skhd/dot_general | solution.py:148
  540.1 12.0 %fusion.78 = (f32[3,64]{1,0:T(4,128)}, bf16[4,256,3,64]{1,3,2,0:T(8,128)(2,1)S(1)}) fusion(bf16[8,2048,3,64]{1,3,2,0:T(8,128)(2,1)} %all-gather.9.cloned.1.call-done, f32[4,3,2048,256]{3,2,1,0:T(8,128)} %fusion.66, f32[4,3,2048]{2,1,0:T(4,128)S(1)} %get-tuple-element.105, pred[4,2048,256]{2,1,0:T(8,128)(4,1)S(1)} %copy-done.3), kind=kOutput, calls=%fused_computation.167 | convolution fusion | flops 830865216 | bytes 34046720 | tf_op jit(solution)/shard_map/shqk,sqhd->skhd/dot_general | solution.py:151
  554.3 4.3 bitcast_convert_fusion
  558.8 4.0 convolution_convert_fusion.4
  562.8 6.2 copy.144
  569.1 13.0 %reshape.337 = bf16[32,18432]{1,0:T(8,128)(2,1)} reshape(bf16[32,768,24]{2,1,0:T(8,128)(2,1)} %bitcast.95) | data formatting | bytes 2359296 | tf_op jit(solution)/shard_map/reshape | solution.py:58
  584.7 1.5 copy.143
  586.3 3.4 reshape.335
  591.3 3.8 fusion.33
  595.1 2.3 copy.140
  597.4 2.4 copy.141
  599.8 2.9 reshape.333
  602.7 2.2 constant_dynamic-update-slice_fusion.6
  605.9 2.5 constant_dynamic-update-slice_fusion.4
  609.5 20.9 %all-gather.11.cloned.1.call-done = bf16[1024,768]{1,0:T(8,128)(2,1)} async-done(((bf16[256,768]{1,0:T(8,128)(2,1)}), bf16[1024,768]{1,0:T(8,128)(2,1)}) %all-gather.11.cloned.1.call-update) | async-done | bytes 1572880 | tf_op jit(solution)/shard_map/all_gather | solution.py:45
  630.5 3.5 add_reduce_fusion
  634.1 1.4 dynamic-update-slice.4
  635.5 1.5 dynamic-update-slice.5
  637.0 1.5 dynamic-update-slice.6
  638.5 1.5 dynamic-update-slice.7
  640.0 1.5 dynamic-update-slice.8
  641.5 1.5 dynamic-update-slice.9
  643.0 4.1 pad.4
  647.0 5.2 reshape.338
  653.9 7.7 all-to-all-start
  662.9 6.3 all-to-all-done
  670.6 93.9 %all-reduce.13.cloned.1.call-done = bf16[14080,128]{1,0:T(8,128)(2,1)} async-done(((bf16[14080,128]{1,0:T(8,128)(2,1)}), bf16[14080,128]{1,0:T(8,128)(2,1)}) %all-reduce.13.cloned.1.call-update) | async-done | bytes 3604496
  (204 shorter events, 46.7 us)
Async XLA Ops:
  7.2 10.2 %copy-start.43 = (bf16[2,192]{1,0:T(2,128)(2,1)S(1)}, bf16[2,192]{1,0:T(2,128)(2,1)}, u32[]{:S(2)}) copy-start(bf16[2,192]{1,0:T(2,128)(2,1)} %param.18) | copy-start | bytes 2308
  7.2 56.6 %all-gather.5.cloned.1.call-start = ((), (), s32[]{:S(2)}) async-start(), calls=%async_computation.2 | async-start | bytes 4669440 | tf_op jit(solution)/shard_map/all_gather | solution.py:17
  14.1 51.7 %copy-start.10 = (bf16[4,256,768]{2,1,0:T(8,128)(2,1)S(1)}, bf16[4,256,768]{2,1,0:T(8,128)(2,1)}, u32[]{:S(2)}) copy-start(bf16[4,256,768]{2,1,0:T(8,128)(2,1)} %param.15) | copy-start | bytes 4718596
  17.3 147.2 %all-gather.7.cloned.1.call-start = ((), (), s32[]{:S(2)}) async-start(), calls=%async_computation.3 | async-start | bytes 7077888 | tf_op jit(solution)/shard_map/all_gather | solution.py:33
  65.7 2.2 copy-start.24
  67.9 2.8 copy-start.34
  68.6 2.1 copy-start.15
  68.9 0.8 copy-start.17
  70.6 184.9 %all-reduce.7.cloned.1.call-start = ((), (), s32[]{:S(2)}) async-start(), calls=%async_computation.4 | async-start | bytes 3145728 | tf_op jit(solution)/shard_map/psum | solution.py:223
  98.8 1.3 copy-start.25
  100.2 89.1 %copy-start.1 = (pred[4,256,2048]{2,1,0:T(8,128)(4,1)}, pred[4,256,2048]{2,1,0:T(8,128)(4,1)S(1)}, u32[]{:S(2)}) copy-start(pred[4,256,2048]{2,1,0:T(8,128)(4,1)S(1)} %broadcast_compare_fusion.1) | copy-start | bytes 6291460
  102.4 74.9 %copy-start.23 = (bf16[4,256,3,64]{1,3,2,0:T(8,128)(2,1)}, bf16[4,256,3,64]{1,3,2,0:T(8,128)(2,1)S(1)}, u32[]{:S(2)}) copy-start(bf16[4,256,3,64]{1,3,2,0:T(8,128)(2,1)S(1)} %fusion.49) | copy-start | bytes 1179652
  177.3 12.0 %copy-start.30 = (f32[4,3,256]{2,1,0:T(4,128)}, f32[4,3,256]{2,1,0:T(4,128)S(1)}, u32[]{:S(2)}) copy-start(f32[4,3,256]{2,1,0:T(4,128)S(1)} %get-tuple-element.113) | copy-start | bytes 36868
  189.3 13.4 %copy-start.31 = (f32[4,3,256]{2,1,0:T(4,128)}, f32[4,3,256]{2,1,0:T(4,128)S(1)}, u32[]{:S(2)}) copy-start(f32[4,3,256]{2,1,0:T(4,128)S(1)} %fusion) | copy-start | bytes 36868
  202.7 4.5 copy-start.41
  203.0 52.5 %copy-start.11 = (bf16[4,256,768]{2,1,0:T(8,128)(2,1)S(1)}, bf16[4,256,768]{2,1,0:T(8,128)(2,1)}, u32[]{:S(2)}) copy-start(bf16[4,256,768]{2,1,0:T(8,128)(2,1)} %param.15) | copy-start | bytes 4718596
  203.1 0.8 copy-start.19
  206.9 117.3 %all-reduce.9.cloned.1.call-start = ((), (), s32[]{:S(2)}) async-start(), calls=%async_computation.5 | async-start | bytes 3145728 | tf_op jit(solution)/shard_map/psum | solution.py:232
  209.6 114.5 %copy-start.36 = (f32[768]{0:T(1024)}, f32[768]{0:T(1024)S(1)}, u32[]{:S(2)}) copy-start(f32[768]{0:T(1024)S(1)} %get-tuple-element.78) | copy-start | bytes 9220
  209.6 185.6 %copy-start.26 = (f32[768]{0:T(1024)}, f32[768]{0:T(1024)S(1)}, u32[]{:S(2)}) copy-start(f32[768]{0:T(1024)S(1)} %get-tuple-element.79) | copy-start | bytes 9220
  255.5 2.1 copy-start.12
  257.6 2.5 copy-start.21
  260.1 135.2 %copy-start.27 = (f32[1024]{0:T(1024)}, f32[1024]{0:T(1024)S(1)}, u32[]{:S(2)}) copy-start(f32[1024]{0:T(1024)S(1)} %fusion.55) | copy-start | bytes 12292
  269.8 1.1 copy-start.48
  273.5 117.3 %all-reduce.11.cloned.1.call-start = ((), (), s32[]{:S(2)}) async-start(), calls=%async_computation.6 | async-start | bytes 3145728 | tf_op jit(solution)/shard_map/psum | solution.py:251
  326.5 1.4 copy-start.9
  327.9 4.5 copy-start.46
  329.8 2.7 copy-start.22
  329.8 3.5 copy-start.45
  332.4 4.0 copy-start.6
  332.4 62.8 %copy-start.32 = (f32[1024]{0:T(1024)}, f32[1024]{0:T(1024)S(1)}, u32[]{:S(2)}) copy-start(f32[1024]{0:T(1024)S(1)} %negate_multiply_fusion.2) | copy-start | bytes 12292
  336.4 1.2 copy-start.47
  340.2 160.3 %all-gather.9.cloned.1.call-start = ((), (), s32[]{:S(2)}) async-start(), calls=%async_computation.7 | async-start | bytes 7077888 | tf_op jit(solution)/shard_map/all_gather | solution.py:33
  390.9 4.4 copy-start.7
  390.9 4.4 copy-start.13
  396.9 1.7 copy-start.4
  396.9 1.6 copy-start.28
  404.7 200.9 %reduce-scatter.2.cloned.1.call-start = ((), (), s32[]{:S(2)}) async-start(), calls=%async_computation.8 | async-start | bytes 1966080 | tf_op jit(solution)/shard_map/reduce_scatter | solution.py:44
  417.4 24.1 %slice-start = ((s8[6291456]{0:T(1024)(128)(4,1)}), s8[2097152]{0:T(1024)(128)(4,1)S(1)}, s32[]{:S(2)}) async-start(s8[6291456]{0:T(1024)(128)(4,1)} %bitcast.93), calls=%async_computation.11 | async-start | bytes 4194304
  420.0 21.5 %slice-start.1 = ((s8[6291456]{0:T(1024)(128)(4,1)}), s8[4194304]{0:T(1024)(128)(4,1)S(1)}, s32[]{:S(2)}) async-start(s8[6291456]{0:T(1024)(128)(4,1)} %bitcast.93), calls=%async_computation.12 | async-start | bytes 8388608
  420.0 21.5 %copy-start.2 = (pred[4,256,2048]{2,1,0:T(8,128)(4,1)S(1)}, pred[4,256,2048]{2,1,0:T(8,128)(4,1)}, u32[]{:S(2)}) copy-start(pred[4,256,2048]{2,1,0:T(8,128)(4,1)} %copy-done.1) | copy-start | bytes 6291460
  460.9 39.6 %copy-start.18 = (bf16[4,256,3,64]{1,3,2,0:T(8,128)(2,1)S(1)}, bf16[4,256,3,64]{1,3,2,0:T(8,128)(2,1)}, u32[]{:S(2)}) copy-start(bf16[4,256,3,64]{1,3,2,0:T(8,128)(2,1)} %copy-done.17) | copy-start | bytes 1179652
  492.5 20.4 %copy-start.16 = (bf16[4,256,3,64]{1,0,3,2:T(4,128)(2,1)S(1)}, bf16[4,256,3,64]{1,0,3,2:T(4,128)(2,1)}, u32[]{:S(2)}) copy-start(bf16[4,256,3,64]{1,0,3,2:T(4,128)(2,1)} %copy-done.15) | copy-start | bytes 1179652
  500.5 12.3 %copy-start = (bf16[8,2048,3,64]{1,3,2,0:T(8,128)(2,1)S(1)}, bf16[8,2048,3,64]{1,3,2,0:T(8,128)(2,1)}, u32[]{:S(2)}) copy-start(bf16[8,2048,3,64]{1,3,2,0:T(8,128)(2,1)} %all-gather.9.cloned.1.call-done) | copy-start | bytes 18874372
  512.8 10.1 %copy-start.3 = (pred[4,2048,256]{2,1,0:T(8,128)(4,1)S(1)}, pred[4,2048,256]{2,1,0:T(8,128)(4,1)}, u32[]{:S(2)}) copy-start(pred[4,2048,256]{2,1,0:T(8,128)(4,1)} %broadcast_compare_fusion) | copy-start | bytes 6291460
  554.3 4.6 copy-start.8
  554.3 4.6 copy-start.33
  558.5 71.9 %all-gather.11.cloned.1.call-start = ((), (), s32[]{:S(2)}) async-start(), calls=%async_computation.9 | async-start | bytes 1966080 | tf_op jit(solution)/shard_map/all_gather | solution.py:45
  569.1 13.0 %copy-start.37 = (bf16[768]{0:T(1024)(128)(2,1)S(1)}, bf16[768]{0:T(1024)(128)(2,1)}, u32[]{:S(2)}) copy-start(bf16[768]{0:T(1024)(128)(2,1)} %get-tuple-element.72) | copy-start | bytes 4612
  569.1 13.1 %copy-start.5 = (f32[1024,768]{1,0:T(8,128)S(1)}, f32[1024,768]{1,0:T(8,128)}, u32[]{:S(2)}) copy-start(f32[1024,768]{1,0:T(8,128)} %copy-done.4) | copy-start | bytes 9437188
  569.1 13.1 %copy-start.20 = (bf16[24,8,4,256]{3,1,2,0:T(8,128)(2,1)S(1)}, bf16[24,8,4,256]{3,1,2,0:T(8,128)(2,1)}, u32[]{:S(2)}) copy-start(bf16[24,8,4,256]{3,1,2,0:T(8,128)(2,1)} %copy-done.19) | copy-start | bytes 1179652
  569.1 13.2 %copy-start.29 = (f32[1024]{0:T(1024)S(1)}, f32[1024]{0:T(1024)}, u32[]{:S(2)}) copy-start(f32[1024]{0:T(1024)} %copy-done.28) | copy-start | bytes 12292
  583.6 7.6 copy-start.38
  605.6 158.9 %all-reduce.13.cloned.1.call-start = ((), (), s32[]{:S(2)}) async-start(), calls=%async_computation.10 | async-start | bytes 7208960
  605.9 2.5 copy-start.14
  609.5 31.9 %copy-start.35 = (bf16[32,24]{1,0:T(8,128)(2,1)S(1)}, bf16[32,24]{1,0:T(8,128)(2,1)}, u32[]{:S(2)}) copy-start(bf16[32,24]{1,0:T(8,128)(2,1)} %convert_element_type.320) | copy-start | bytes 4612
  652.2 0.7 copy-start.39
  652.2 0.8 copy-start.42
  652.2 0.9 copy-start.40
  652.2 9.4 %copy-start.44 = (u32[128]{0:T(128)S(1)}, u32[128]{0:T(128)}, u32[]{:S(2)}) copy-start(u32[128]{0:T(128)} %constant.93) | copy-start | bytes 1540
  653.9 15.3 %all-to-all-start = ((f32[32,1,1152]{2,1,0:T(1,128)}), f32[32,1,1152]{2,1,0:T(1,128)S(1)}, u32[]{:S(2)}, u32[]{:S(2)}) async-start(f32[32,1,1152]{2,1,0:T(1,128)} %broadcast_in_dim.87), calls=%async_computation.1 | async-start | bytes 294912 | tf_op jit(solution)/shard_map/all_to_all | solution.py:71
Sparse Core Ops, SparseCore 0:
  17.4 46.3 all-gather.4
  70.7 93.7 all-gather.6
  207.0 48.4 all-reduce.6
  273.6 50.4 all-reduce.8
  340.3 50.4 all-reduce.10
  404.8 95.7 all-gather.8
  558.7 22.9 reduce-scatter.1
  605.7 24.6 all-gather.10
  652.4 112.0 all-reduce.12
where the time goes:
time: 784 us; the launch traced here: 778 us
  waiting for transfers between devices  385 us (49%)
  matrix products  160 us (20%)
  local copies, waits for them, and re-layouts  99.4 us (13%)
  blocking collectives  58.2 us (7%)
  other arithmetic  50.8 us (6%)
  between operations  15.6 us (2%)
  starting transfers between devices  9.47 us (1%)
    unnamed x10, waiting for transfers between devices  94.1 us
    all_gather x2, waiting for transfers between devices, sent_together(): lax.all_gather(both, axis, axis=dim, tiled=True)  70.2 us
    psum x1, waiting for transfers between devices, shards(): lax.psum(norm_part.astype(jnp.bfloat16), 'tp').astype(jnp.float32)  50.6 us
    psum x1, waiting for transfers between devices, shards(): ffn_full = lax.psum(ffn_part.astype(jnp.bfloat16), 'tp').astype(jnp.float32)  50.3 us
    all_gather x1, waiting for transfers between devices, turned_gather(): out = lax.all_gather(both, axis, axis=0, tiled=True)  46.3 us
    psum x1, waiting for transfers between devices, shards(): lax.psum(attn_part.astype(jnp.bfloat16), 'tp').astype(jnp.float32)  45.8 us
    all_gather x1, blocking collectives, sent_together(): lax.all_gather(both, axis, axis=dim, tiled=True)  30.1 us
    all_gather x1, blocking collectives, shards(): lax.all_gather(segment_ids, 'ctx', axis=1, tiled=True)  28.1 us
  transfers between devices with their start and end apart: 10, of which 9 were waited for; matrix products, arithmetic and copies ran while one was open for 15% of the time, Pallas kernels for 0%

commit v1 on v0

v1 whole, which is shorter than its diff:
```python
import functools
import math

import jax
import jax.numpy as jnp
import numpy as np
from jax import lax
from jax.experimental import pallas as pl
from jax.experimental.pallas import tpu as pltpu
from jax.sharding import PartitionSpec as P

HEAD_DIM = 64
NORM_EPS = 1e-12
MESH = pl.DeviceIdType.MESH
bf=jnp.bfloat16; f32=jnp.float32

class Place:
    def __init__(self):
        self.x=lax.axis_index("tp"); f=lax.axis_index("fsdp"); c=lax.axis_index("ctx")
        self.yl=f//2; self.core=f%2; self.yh=c//4; self.z=c%4
        self.y=self.yh*2+self.yl
    def px(self,k):
        q=(self.x+k)%4
        return {"tp":q}, q
    def pz(self,k):
        q=(self.z+k)%4
        return {"ctx":self.yh*4+q}, q
    def py(self,k):
        q=(self.y+k)%4
        return {"fsdp":(q%2)*2+self.core,"ctx":(q//2)*4+self.z}, (q%2,q//2)
    def sib(self):
        return {"fsdp":self.yl*2+1-self.core}

def greet(devs):
    bar=pltpu.get_barrier_semaphore()
    for d in devs: pl.semaphore_signal(bar,inc=1,device_id=d,device_id_type=MESH)
    pl.semaphore_wait(bar,len(devs))

def rcopy(src,dst,ss,rs,dev):
    return pltpu.make_async_remote_copy(src_ref=src,dst_ref=dst,send_sem=ss,recv_sem=rs,device_id=dev,device_id_type=MESH)

def gather_kernel(pk,vec,W,V,ss,rs,ls):
    p=Place(); x,yl,core,yh,z=p.x,p.yl,p.core,p.yh,p.z
    nb={"fsdp":(1-yl)*2+core}
    greet([p.px(k)[0] for k in (1,2,3)]+[p.pz(k)[0] for k in (1,2,3)]+[p.py(k)[0] for k in (1,2,3)]+[nb_dev(p) for nb_dev in (lambda q:q.sib(),)])
    n=[0]; sent=[]
    def sem():
        n[0]+=1; return n[0]-1
    def send(src,dst,dev):
        i=sem(); c=rcopy(src,dst,ss.at[i],rs.at[i],dev); c.start(); sent.append(c); return c
    own=pltpu.make_async_copy(pk,W.at[:,x,yl,core],ls.at[0]); own.start()
    ownv=pltpu.make_async_copy(vec,V.at[x,yl,core],ls.at[1]); ownv.start()
    half=pl.ds(pl.multiple_of(yh*96,8),96); quar=pl.ds(pl.multiple_of(z*48,8),48)
    nbd,_=p.py(1)
    a0=send(pk.at[0],W.at[0,x,yl,core],nb)
    av=send(vec,V.at[x,yl,core],nb)
    a2=send(pk.at[2,quar],W.at[2,x,yl,core,quar],nb)
    b1=[send(pk.at[1,half],W.at[1,x,yl,core,half],p.px(k)[0]) for k in (1,2,3)]
    b2=[send(pk.at[2,quar],W.at[2,x,yl,core,quar],p.px(k)[0]) for k in (1,2,3)]
    b0=[send(pk.at[0],W.at[0,x,yl,core],p.px(k)[0]) for k in (1,2,3)]
    bv=[send(vec,V.at[x,yl,core],p.px(k)[0]) for k in (1,2,3)]
    c1=[send(pk.at[1,half],W.at[1,x,yl,core,half],p.py(k)[0]) for k in (1,3)]
    d=[send(pk.at[j],W.at[j,x,yl,core],p.sib()) for j in range(3)]
    dv=[send(vec,V.at[x,yl,core],p.sib())]
    a2.wait_recv()
    b2n=[send(W.at[2,x,1-yl,core,quar],W.at[2,x,1-yl,core,quar],p.px(k)[0]) for k in (1,2,3)]
    c2=[send(W.at[2,x,1-yl,core,quar],W.at[2,x,1-yl,core,quar],p.pz(k)[0]) for k in (1,2,3)]
    a0.wait_recv(); av.wait_recv()
    b0n=[send(W.at[0,x,1-yl,core],W.at[0,x,1-yl,core],p.px(k)[0]) for k in (1,2,3)]
    bvn=[send(V.at[x,1-yl,core],V.at[x,1-yl,core],p.px(k)[0]) for k in (1,2,3)]
    d.append(send(W.at[0,x,1-yl,core],W.at[0,x,1-yl,core],p.sib()))
    dv.append(send(V.at[x,1-yl,core],V.at[x,1-yl,core],p.sib()))
    c1n=[]; c2n=[]
    for k in (1,2,3):
        t=(x-k+4)%4
        b1[k-1].wait_recv()
        c1n.append([send(W.at[1,t,yl,core,half],W.at[1,t,yl,core,half],p.py(j)[0]) for j in (1,2,3)])
        b2[k-1].wait_recv()
        c2n.append([send(W.at[2,t,yl,core,quar],W.at[2,t,yl,core,quar],p.pz(j)[0]) for j in (1,2,3)])
    for k in (1,2,3):
        t=(x-k+4)%4
        b2n[k-1].wait_recv()
        c2n.append([send(W.at[2,t,1-yl,core,quar],W.at[2,t,1-yl,core,quar],p.pz(j)[0]) for j in (1,2,3)])
    for k in (1,2,3):
        t=(x-k+4)%4
        b0[k-1].wait_recv(); bv[k-1].wait_recv()
        d.append(send(W.at[0,t,yl,core],W.at[0,t,yl,core],p.sib()))
        dv.append(send(V.at[t,yl,core],V.at[t,yl,core],p.sib()))
    for c in c2: c.wait_recv()
    d.append(send(W.at[2,x,1-yl,core],W.at[2,x,1-yl,core],p.sib()))
    for c in c1: c.wait_recv()
    d.append(send(W.at[1,x,1-yl,core],W.at[1,x,1-yl,core],p.sib()))
    for k in (1,2,3):
        t=(x-k+4)%4
        for c in c1n[k-1]: c.wait_recv()
        d.append(send(W.at[1,t],W.at[1,t],p.sib()) if False else send(W.at[1,t,:,core],W.at[1,t,:,core],p.sib()))
        for c in c2n[k-1]: c.wait_recv()
        d.append(send(W.at[2,t,yl,core],W.at[2,t,yl,core],p.sib()))
    for k in (1,2,3):
        t=(x-k+4)%4
        b0n[k-1].wait_recv(); bvn[k-1].wait_recv()
        d.append(send(W.at[0,t,1-yl,core],W.at[0,t,1-yl,core],p.sib()))
        dv.append(send(V.at[t,1-yl,core],V.at[t,1-yl,core],p.sib()))
        for c in c2n[2+k]: c.wait_recv()
        d.append(send(W.at[2,t,1-yl,core],W.at[2,t,1-yl,core],p.sib()))
    for c in d+dv: c.wait_recv()
    for c in sent: c.wait_send()
    own.wait(); ownv.wait()
NS_G=96
def gather_weights(pk,vec,cid):
    return pl.pallas_call(gather_kernel,out_shape=(jax.ShapeDtypeStruct((3,4,2,2,192,768),bf),jax.ShapeDtypeStruct((4,2,2,8,768),bf)),
      in_specs=[pl.BlockSpec(memory_space=pl.ANY)]*2,out_specs=[pl.BlockSpec(memory_space=pl.ANY)]*2,
      scratch_shapes=[pltpu.SemaphoreType.DMA((NS_G,)),pltpu.SemaphoreType.DMA((NS_G,)),pltpu.SemaphoreType.DMA((2,))],
      compiler_params=pltpu.CompilerParams(collective_id=cid,has_side_effects=True))(pk,vec)

DIMS = {"x": (4,), "y": (2, 2), "z": (4,)}
ORDER = ("xyz", "yzx", "zxy")


def shape_of(axes):
    return sum([DIMS[d] for d in "xyz" if d in axes], ())


def split_index(i, shape):
    out = []
    for s in reversed(shape):
        out.insert(0, i % s)
        i = i // s
    return tuple(out)


def pick(ref, axis, q, left):
    at = []
    for d in "xyz":
        if d in left:
            at += list(q if d == "y" else (q,)) if d == axis else [slice(None)] * len(DIMS[d])
    return ref.at[tuple(at)]


def total(dst, first, others, shape):
    count = math.prod(shape)

    @pl.loop(0, count)
    def _(i):
        at = split_index(i, shape)
        a = first[at].astype(f32)
        for o in others:
            a = a + o[at].astype(f32)
        dst[at] = a.astype(dst.dtype)


def reduce_kernel(g0, g1, g2, vin, R, V, acc, cor, *refs):
    s1, r1, s2, r2 = refs[0:3], refs[3:6], refs[6:9], refs[9:12]
    r3, vr, vt, ss, rs, ls = refs[12:]
    p = Place()
    x, yl, core, yh, z = p.x, p.yl, p.core, p.yh, p.z
    peers = {"x": p.px, "y": p.py, "z": p.pz}
    here = {"x": x, "y": (yl, yh), "z": z}
    greet([peers[a](k)[0] for a in "xyz" for k in (1, 2, 3)] + [p.sib()])
    sent = []

    def send(src, dst, dev):
        i = len(sent)
        c = rcopy(src, dst, ss.at[i], rs.at[i], dev)
        c.start()
        sent.append(c)
        return c

    g = [g0, g1, g2]
    turn = (1, 2, 0)
    cv = send(vin, vr.at[0, 0], p.sib())
    cc, ll = {}, {}
    for k in turn:
        cc[k] = send(g[k].at[:, :, 1 - core], cor.at[k], p.sib())
        ll[k] = pltpu.make_async_copy(g[k].at[:, :, core], acc.at[k], ls.at[k])
        ll[k].start()
    cv.wait_recv()
    vt[0] = vin[...] + vr[0, 0]

    def vsend(i, a):
        return [send(vt.at[i], vr.at[i + 1, j - 1], peers[a](j)[0]) for j in (1, 2, 3)]

    def vsum(i, cs):
        for c in cs:
            c.wait_recv()
        return vt[i] + vr[i + 1, 0] + vr[i + 1, 1] + vr[i + 1, 2]

    vx = vsend(0, "x")
    st1, st2, st3 = {}, {}, {}
    for k in turn:
        cc[k].wait_recv()
        ll[k].wait()
        total(acc.at[k], acc.at[k], [cor.at[k]], shape_of("xyz"))
        a = ORDER[k][0]
        st1[k] = [send(pick(acc.at[k], a, peers[a](j)[1], "xyz"), r1[k].at[j - 1], peers[a](j)[0]) for j in (1, 2, 3)]
    vt[1] = vsum(0, vx)
    vy = vsend(1, "y")
    for k in turn:
        a, b, _ = ORDER[k]
        left = [d for d in "xyz" if d != a]
        for c in st1[k]:
            c.wait_recv()
        total(s1[k], pick(acc.at[k], a, here[a], "xyz"), [r1[k].at[j] for j in range(3)], shape_of(left))
        st2[k] = [send(pick(s1[k], b, peers[b](j)[1], left), r2[k].at[j - 1], peers[b](j)[0]) for j in (1, 2, 3)]
    vt[2] = vsum(1, vy)
    vz = vsend(2, "z")
    for k in turn:
        a, b, d = ORDER[k]
        left = [e for e in "xyz" if e != a]
        for c in st2[k]:
            c.wait_recv()
        total(s2[k], pick(s1[k], b, here[b], left), [r2[k].at[j] for j in range(3)], shape_of(d))
        st3[k] = [send(pick(s2[k], d, peers[d](j)[1], d), r3.at[k, j - 1], peers[d](j)[0]) for j in (1, 2, 3)]
    V[...] = vsum(2, vz)
    for k in turn:
        d = ORDER[k][2]
        for c in st3[k]:
            c.wait_recv()
        m = pick(s2[k], d, here[d], d)[...].astype(f32)
        for j in range(3):
            m = m + r3[k, j].astype(f32)
        R[k] = m
    for c in sent:
        c.wait_send()


def reduce_grads(g0, g1, g2, vin, cid):
    vm = pltpu.VMEM
    sh = (4, 2, 2, 2, 4, 24, 768)
    first = [shape_of([d for d in "xyz" if d != o[0]]) for o in ORDER]
    second = [shape_of(o[2]) for o in ORDER]
    scratch = (
        [vm((3, *shape_of("xyz"), 24, 768), bf)] * 2
        + [vm((*s, 24, 768), bf) for s in first]
        + [vm((3, *s, 24, 768), bf) for s in first]
        + [vm((*s, 24, 768), bf) for s in second]
        + [vm((3, *s, 24, 768), bf) for s in second]
        + [vm((3, 3, 24, 768), bf), vm((4, 3) + vin.shape, f32), vm((3,) + vin.shape, f32)]
        + [pltpu.SemaphoreType.DMA((48,)), pltpu.SemaphoreType.DMA((48,)), pltpu.SemaphoreType.DMA((3,))]
    )
    return pl.pallas_call(
        reduce_kernel,
        out_shape=(jax.ShapeDtypeStruct((3, 24, 768), f32), jax.ShapeDtypeStruct(vin.shape, f32)),
        in_specs=[pl.BlockSpec(memory_space=pl.ANY)] * 3 + [pl.BlockSpec(memory_space=vm)],
        out_specs=[pl.BlockSpec(memory_space=vm)] * 2,
        scratch_shapes=scratch,
        compiler_params=pltpu.CompilerParams(collective_id=cid, has_side_effects=True, vmem_limit_bytes=56 << 20),
    )(g0.reshape(sh), g1.reshape(sh), g2.reshape(sh), vin)


SQ = HEAD_DIM ** -0.5
FAR = float(2.0 ** 100)
BLK = 256


def nt(a, b):
    return lax.dot_general(a, b, (((1,), (1,)), ((), ())), preferred_element_type=f32)


def nn(a, b):
    return jnp.dot(a, b, preferred_element_type=f32)


def params(cid=None, mb=48):
    return pltpu.CompilerParams(collective_id=cid, has_side_effects=cid is not None, vmem_limit_bytes=mb << 20)


def qkv_kernel(x, w, b, o):
    r = (nn(x[...], w[0]) + b[0]).astype(bf)
    o[0] = r[:, :384]
    o[1] = jnp.concatenate([r[:, 384:576], r[:, 192:384]], axis=1)


def project(x, w, b):
    return pl.pallas_call(
        qkv_kernel,
        grid=(4,),
        out_shape=jax.ShapeDtypeStruct((8, BLK, 384), bf),
        in_specs=[
            pl.BlockSpec((BLK, 768), lambda t: (0, 0)),
            pl.BlockSpec((1, 768, 768), lambda t: (t, 0, 0)),
            pl.BlockSpec((1, 1, 768), lambda t: (t, 0, 0)),
        ],
        out_specs=pl.BlockSpec((2, BLK, 384), lambda t: (t, 0, 0)),
        compiler_params=params(),
    )(x, w, b)


def swap_kernel(pairs, *refs):
    ins, outs = refs[:pairs], refs[pairs : 2 * pairs]
    ss, rs, ls = refs[2 * pairs :]
    c = lax.axis_index("ctx")
    greet([{"ctx": (c + k) % 8} for k in range(1, 8)])
    sent, own = [], []
    for k in range(1, 8):
        q = (c + k) % 8
        for i in range(pairs):
            src = ins[i].at[q] if ins[i].shape == outs[i].shape else ins[i]
            cp = rcopy(src, outs[i].at[c], ss.at[i, k], rs.at[i, k], {"ctx": q})
            cp.start()
            sent.append(cp)
    for i in range(pairs):
        src = ins[i].at[c] if ins[i].shape == outs[i].shape else ins[i]
        cp = pltpu.make_async_copy(src, outs[i].at[c], ls.at[i])
        cp.start()
        own.append(cp)
    for cp in own + sent:
        cp.wait()


def swap(arrays, outs, cid):
    n = len(arrays)
    sems = [pltpu.SemaphoreType.DMA((n, 8))] * 2 + [pltpu.SemaphoreType.DMA((n,))]
    return pl.pallas_call(
        functools.partial(swap_kernel, n),
        out_shape=tuple(jax.ShapeDtypeStruct(s, a.dtype) for s, a in zip(outs, arrays)),
        in_specs=[pl.BlockSpec(memory_space=pl.ANY)] * n,
        out_specs=[pl.BlockSpec(memory_space=pl.ANY)] * n,
        scratch_shapes=sems,
        compiler_params=params(cid),
    )(*arrays)


def spread(r, aug, qa, ka, h):
    q = r[:, :, h * 192 : h * 192 + 64].reshape(2048, 64)
    k = r[:, :, h * 192 + 64 : h * 192 + 128].reshape(2048, 64)
    qa[h] = jnp.concatenate([q * bf(SQ), aug[:, 64:]], axis=1)
    ka[h] = jnp.concatenate([k, aug[:, :64]], axis=1)


def reach(edge, i, low, high):
    lo, hi = jnp.int32(0), jnp.int32(0)
    for j in range(8):
        lo = lo + (edge[1, j] < edge[0, i]).astype(jnp.int32)
        hi = hi + (edge[0, j] <= edge[1, i]).astype(jnp.int32)
    return lo, hi


def attend_kernel(edge, r, aug, msg, lse, ct, qa, ka, vt):
    par = lax.axis_index("ctx") % 2
    for h in range(2):
        spread(r, aug, qa, ka, h)
        v = r[:, :, h * 192 + 128 : h * 192 + 192].reshape(2048, 64)
        vt[h] = v.astype(f32).T.astype(bf)
    lse[...] = jnp.zeros_like(lse)
    ct[...] = jnp.zeros_like(ct)
    msg[...] = jnp.zeros_like(msg)

    def one(h, i):
        at = pl.ds(pl.multiple_of(i * BLK, BLK), BLK)
        q = qa[h, at]
        lo, hi = reach(edge, i, 0, 8)

        def body(j, carry):
            m, l, acc = carry
            to = pl.ds(pl.multiple_of(j * BLK, BLK), BLK)
            s = nt(ka[h, to], q)
            mj = jnp.maximum(m, jnp.max(s, axis=0, keepdims=True))
            p = jnp.exp(s - mj)
            alpha = jnp.exp(m - mj)
            l = l * alpha + jnp.sum(p, axis=0, keepdims=True)
            acc = acc * alpha + nn(vt[h, :, to], p.astype(bf))
            return mj, l, acc

        m, l, acc = lax.fori_loop(
            lo, hi, body, (jnp.full((1, BLK), -3e38, f32), jnp.zeros((1, BLK), f32), jnp.zeros((64, BLK), f32))
        )
        c = acc / l
        lse[h * 8 + i] = jnp.broadcast_to(m + jnp.log(l), (8, BLK))
        ct[h, :, at] = c
        msg[i, :, h * 64 : h * 64 + 64] = c.T.astype(bf)

    @pl.loop(0, 8)
    def _(i):
        one(0, i)

    @pl.loop(0, 4)
    def _(i):
        one(1, 2 * i + par)


def attend(edge, r, aug):
    vm = pltpu.VMEM
    return pl.pallas_call(
        attend_kernel,
        out_shape=(
            jax.ShapeDtypeStruct((8, BLK, 128), bf),
            jax.ShapeDtypeStruct((16, 8, BLK), f32),
            jax.ShapeDtypeStruct((2, 64, 2048), f32),
        ),
        in_specs=[pl.BlockSpec(memory_space=pltpu.SMEM)] + [pl.BlockSpec(memory_space=vm)] * 2,
        out_specs=[pl.BlockSpec(memory_space=vm)] * 3,
        scratch_shapes=[vm((2, 2048, 128), bf), vm((2, 2048, 128), bf), vm((2, 64, 2048), bf)],
        compiler_params=params(),
    )(edge, r, aug)


def unattend_kernel(edge, r, aug, dc, lse, ct, out, qa, ka, kt, delta, dqt, dk, dv):
    par = lax.axis_index("ctx") % 2
    for h in range(2):
        spread(r, aug, qa, ka, h)
        k = r[:, :, h * 192 + 64 : h * 192 + 128].reshape(2048, 64)
        kt[h] = k.astype(f32).T.astype(bf)
        g = dc[:, :, h * 64 : h * 64 + 64].reshape(2048, 64).astype(f32).T
        d = jnp.sum(g * ct[h], axis=0, keepdims=True)
        for i in range(8):
            delta[h * 8 + i] = jnp.broadcast_to(d[:, i * BLK : i * BLK + BLK], (8, BLK))
    dqt[...] = jnp.zeros_like(dqt)

    def one(h, j):
        to = pl.ds(pl.multiple_of(j * BLK, BLK), BLK)
        lo, hi = reach(edge, j, 0, 8)
        if h == 1:
            lo = (lo - par + 1) // 2
            hi = (hi - par + 1) // 2
        dk[...] = jnp.zeros_like(dk)
        dv[...] = jnp.zeros_like(dv)
        kj = ka[h, to]
        vj = r[j, :, h * 192 + 128 : h * 192 + 192]
        ktj = kt[h, :, to]

        def body(n, _):
            i = n if h == 0 else 2 * n + par
            at = pl.ds(pl.multiple_of(i * BLK, BLK), BLK)
            q = qa[h, at]
            g = dc[i, :, h * 64 : h * 64 + 64]
            p = jnp.exp(nt(kj, q) - lse[h * 8 + i, :1])
            dp = nt(vj, g)
            ds = (p * (dp - delta[h * 8 + i, :1])).astype(bf)
            dv[...] += nn(p.astype(bf), g)
            dk[...] += nn(ds, q)
            dqt[h, :, at] += nn(ktj, ds)
            return 0

        lax.fori_loop(lo, hi, body, 0)
        out[j, :, h * 192 + 64 : h * 192 + 128] = dk[:, :64].astype(bf)
        out[j, :, h * 192 + 128 : h * 192 + 192] = dv[...].astype(bf)

    @pl.loop(0, 8)
    def _(j):
        one(0, j)
        one(1, j)

    for h in range(2):
        dq = (dqt[h] * SQ).T.astype(bf)
        for i in range(8):
            out[i, :, h * 192 : h * 192 + 64] = dq[i * BLK : i * BLK + BLK]


def unattend(edge, r, aug, dc, lse, ct):
    vm = pltpu.VMEM
    return pl.pallas_call(
        unattend_kernel,
        out_shape=jax.ShapeDtypeStruct((8, BLK, 384), bf),
        in_specs=[pl.BlockSpec(memory_space=pltpu.SMEM)] + [pl.BlockSpec(memory_space=vm)] * 5,
        out_specs=pl.BlockSpec(memory_space=vm),
        scratch_shapes=[
            vm((2, 2048, 128), bf),
            vm((2, 2048, 128), bf),
            vm((2, 64, 2048), bf),
            vm((16, 8, BLK), f32),
            vm((2, 64, 2048), f32),
            vm((BLK, 128), f32),
            vm((BLK, 64), f32),
        ],
        compiler_params=params(),
    )(edge, r, aug, dc, lse, ct)


def norm_of(v):
    d = v - jnp.mean(v, axis=-1, keepdims=True)
    s = lax.rsqrt(jnp.mean(d * d, axis=-1, keepdims=True) + NORM_EPS)
    return d * s, s


def norm_back(g, xhat, s, gain):
    e = g * gain
    return s * (e - jnp.mean(e, axis=-1, keepdims=True) - xhat * jnp.mean(e * xhat, axis=-1, keepdims=True))


def down_sum(v):
    return jnp.sum(v, axis=0, keepdims=True)


def rows_kernel(w, cm, x, cot, pv, lo, dh1, gup, gdn, go, dcm, sums, wv, wo, zs, cdf, act, gs, ls, os):
    loads = []
    for k in range(3):
        for t in range(4):
            cp = pltpu.make_async_copy(w.at[k, t], wv.at[k * 4 + t], ls.at[k * 4 + t])
            cp.start()
            loads.append(cp)
    attn = jnp.zeros((BLK, 768), f32)
    for t in range(4):
        loads[t].wait()
        o = wv[t, :, 576:768]
        wo[2 * t] = o[:, :128]
        wo[2 * t + 1] = jnp.concatenate([o[:, 128:], o[:, 64:128]], axis=1)
        attn = attn + nt(cm[2 * t], wo[2 * t]) + nt(cm[2 * t + 1], wo[2 * t + 1])
    h1 = x[...].astype(f32) + attn + pv[0:1]
    xh1, s1 = norm_of(h1)
    y1 = xh1 * pv[2:3] + pv[3:4]
    y1b = y1.astype(bf)
    ffn = jnp.zeros((BLK, 768), f32)
    for t in range(4):
        loads[4 + t].wait()
        z = nn(y1b, wv[4 + t]) + pv[8 + t : 9 + t]
        c = 0.5 * (1.0 + lax.erf(z * (2.0 ** -0.5)))
        zs[t] = z
        cdf[t] = c
        a = (z * c).astype(bf)
        act[t] = a
        loads[8 + t].wait()
        ffn = ffn + nt(a, wv[8 + t])
    xh2, s2 = norm_of(y1 + ffn + pv[1:2])
    lo[...] = (xh2 * pv[4:5] + pv[5:6]).astype(bf)
    g = cot[...].astype(f32)
    sums[4:5] = down_sum(g * xh2)
    sums[5:6] = down_sum(g)
    dh2 = norm_back(g, xh2, s2, pv[4:5])
    sums[1:2] = down_sum(dh2)
    dh2b = dh2.astype(bf)
    dh2t = dh2.T.astype(bf)
    y1t = y1.T.astype(bf)
    dy1 = dh2
    outs = []
    for t in range(4):
        da = nn(dh2b, wv[8 + t]).astype(bf).astype(f32)
        z = zs[t]
        dz = da * (cdf[t] + z * (jnp.exp(-0.5 * z * z) * ((2.0 * math.pi) ** -0.5)))
        sums[8 + t : 9 + t] = down_sum(dz)
        dzb = dz.astype(bf)
        if t >= 1:
            outs[2 * t - 2].wait()
            outs[2 * t - 1].wait()
        gs[0] = nn(dh2t, act[t]).astype(bf)
        cp = pltpu.make_async_copy(gs.at[0], gdn.at[t], os.at[0])
        cp.start()
        outs.append(cp)
        gs[1] = nn(y1t, dzb).astype(bf)
        cp = pltpu.make_async_copy(gs.at[1], gup.at[t], os.at[1])
        cp.start()
        outs.append(cp)
        dy1 = dy1 + nt(dzb, wv[4 + t])
    sums[2:3] = down_sum(dy1 * xh1)
    sums[3:4] = down_sum(dy1)
    d1 = norm_back(dy1, xh1, s1, pv[2:3])
    dh1[...] = d1
    sums[0:1] = down_sum(d1)
    d1b = d1.astype(bf)
    d1t = d1.T.astype(bf)
    for t in range(4):
        ga = nn(d1t, cm[2 * t])
        gb = nn(d1t, cm[2 * t + 1])
        go[t] = jnp.concatenate([ga[:, :64], ga[:, 64:] + gb[:, 64:], gb[:, :64]], axis=1).astype(bf)
        dcm[2 * t] = nn(d1b, wo[2 * t]).astype(bf)
        dcm[2 * t + 1] = nn(d1b, wo[2 * t + 1]).astype(bf)
    outs[6].wait()
    outs[7].wait()


def rows(w, cm, x, cot, pv):
    vm = pltpu.VMEM
    sd = jax.ShapeDtypeStruct
    anywhere = pl.BlockSpec(memory_space=pl.ANY)
    here = pl.BlockSpec(memory_space=vm)
    return pl.pallas_call(
        rows_kernel,
        out_shape=(
            sd((BLK, 768), bf),
            sd((BLK, 768), f32),
            sd((4, 768, 768), bf),
            sd((4, 768, 768), bf),
            sd((4, 768, 192), bf),
            sd((8, BLK, 128), bf),
            sd((16, 768), f32),
        ),
        in_specs=[anywhere] + [here] * 4,
        out_specs=[here, here, anywhere, anywhere, here, here, here],
        scratch_shapes=[
            vm((12, 768, 768), bf),
            vm((8, 768, 128), bf),
            vm((4, BLK, 768), f32),
            vm((4, BLK, 768), f32),
            vm((4, BLK, 768), bf),
            vm((2, 768, 768), bf),
            pltpu.SemaphoreType.DMA((12,)),
            pltpu.SemaphoreType.DMA((2,)),
        ],
        compiler_params=params(mb=56),
    )(w, cm, x, cot, pv)


def last_kernel(d, x, dh1, w, go, g, ig, pb, xt, acc):
    t = pl.program_id(0)

    @pl.when(t == 0)
    def _():
        xt[...] = x[...].astype(f32).T.astype(bf)
        acc[...] = dh1[...]

    a, b = d[0].astype(f32), d[1].astype(f32)
    pre = jnp.concatenate([a[:, :192], a[:, 192:] + b[:, 192:], b[:, :192]], axis=1)
    pb[0] = jnp.broadcast_to(down_sum(pre), (8, 576))
    pre = pre.astype(bf)
    g[0] = jnp.concatenate([nn(xt[...], pre).astype(bf), go[0]], axis=1)
    acc[...] += nt(pre, w[0, :, :576])
    ig[...] = acc[...].astype(bf)


def last(d, x, dh1, w, go):
    sd = jax.ShapeDtypeStruct
    return pl.pallas_call(
        last_kernel,
        grid=(4,),
        out_shape=(sd((4, 768, 768), bf), sd((BLK, 768), bf), sd((4, 8, 576), f32)),
        in_specs=[
            pl.BlockSpec((2, BLK, 384), lambda t: (t, 0, 0)),
            pl.BlockSpec((BLK, 768), lambda t: (0, 0)),
            pl.BlockSpec((BLK, 768), lambda t: (0, 0)),
            pl.BlockSpec((1, 768, 768), lambda t: (t, 0, 0)),
            pl.BlockSpec((1, 768, 192), lambda t: (t, 0, 0)),
        ],
        out_specs=[
            pl.BlockSpec((1, 768, 768), lambda t: (t, 0, 0)),
            pl.BlockSpec((BLK, 768), lambda t: (0, 0)),
            pl.BlockSpec((1, 8, 576), lambda t: (t, 0, 0)),
        ],
        scratch_shapes=[pltpu.VMEM((768, BLK), bf), pltpu.VMEM((BLK, 768), f32)],
        compiler_params=params(),
    )(d, x, dh1, w, go)


def share_kernel(a, o, ss, rs, ls):
    x = lax.axis_index("tp")
    greet([{"tp": (x + k) % 4} for k in (1, 2, 3)])
    sent = []
    for k in (1, 2, 3):
        cp = rcopy(a, o.at[x], ss.at[k], rs.at[k], {"tp": (x + k) % 4})
        cp.start()
        sent.append(cp)
    own = pltpu.make_async_copy(a, o.at[x], ls)
    own.start()
    own.wait()
    for cp in sent:
        cp.wait()


def share(a, cid):
    return pl.pallas_call(
        share_kernel,
        out_shape=jax.ShapeDtypeStruct((4, *a.shape), a.dtype),
        in_specs=[pl.BlockSpec(memory_space=pl.ANY)],
        out_specs=pl.BlockSpec(memory_space=pl.ANY),
        scratch_shapes=[pltpu.SemaphoreType.DMA((4,)), pltpu.SemaphoreType.DMA((4,)), pltpu.SemaphoreType.DMA],
        compiler_params=params(cid),
    )(a)


def shards(
    layer_input,
    segment_ids,
    proj_weight,
    proj_bias,
    out_weight,
    out_bias,
    first_gain,
    first_shift,
    up_weight,
    up_bias,
    down_weight,
    down_bias,
    second_gain,
    second_shift,
    cotangent,
):
    tp = lax.axis_index("tp")
    turn = np.array([0, 2, 1])
    qkv = proj_weight.reshape(3, 192, 3, 64).transpose(1, 2, 0, 3)[:, turn].reshape(192, 576)
    out_turned = out_weight.T.reshape(192, 3, 64)[:, turn].reshape(192, 192)
    pk = jnp.stack([jnp.concatenate([qkv, out_turned], axis=1), up_weight, down_weight.T])
    pb = proj_bias.reshape(2, 3, 64)[:, turn]
    pb = jnp.stack([pb[0], jnp.zeros_like(pb[0]), pb[1]], axis=1).reshape(576)
    vec = jnp.stack(
        [
            up_bias,
            jnp.pad(pb, (0, 192)),
            jnp.concatenate([out_bias, down_bias, first_gain, first_shift]),
            jnp.pad(jnp.concatenate([second_gain, second_shift]), (0, 384)),
        ]
    )
    vec = jnp.pad(vec, ((0, 4), (0, 0)))
    w, v = gather_weights(pk, vec, 1)
    w = w.reshape(3, 4, 768, 768)
    v = v.astype(f32)
    four = v[0, :, :, 2].reshape(4, 4, 192).transpose(1, 0, 2).reshape(4, 768)
    two = v[0, :, :, 3, :384].reshape(4, 2, 192).transpose(1, 0, 2).reshape(2, 768)
    pv = jnp.concatenate([four, two, jnp.zeros((2, 768), f32), v[:, 0, 0, 0], jnp.zeros((4, 768), f32)])
    x = lax.dynamic_index_in_dim(layer_input, tp, 0, keepdims=False)
    cot = lax.dynamic_index_in_dim(cotangent, tp, 0, keepdims=False)
    seg = lax.dynamic_index_in_dim(segment_ids, tp, 0, keepdims=False)
    seg = jnp.pad(seg.reshape(2, 128), ((0, 6), (0, 0)))
    m = project(x, w[0], v[:, 0, 0, 1][:, None])
    r, segs = swap((m, seg), ((8, BLK, 384), (8, 8, 128)), 2)
    segs = segs[:, :2].reshape(8, BLK)
    edge = jnp.stack([segs[:, 0], segs[:, -1]])
    col = segs.reshape(2048, 1)
    lane = lax.broadcasted_iota(jnp.int32, (1, 64), 1)
    same = col == lane
    aug = jnp.concatenate(
        [jnp.where(same | (lane > 3), 0.0, 1.0).astype(bf), jnp.where(same, -FAR, 0.0).astype(bf)], axis=1
    )
    cmsg, lse, ct = attend(edge, r, aug)
    (cm,) = swap((cmsg,), ((8, BLK, 128),), 3)
    lo, dh1, gup, gdn, go, dcm, sums = rows(w, cm, x, cot, pv)
    layer_output = lax.all_gather(lo, "tp", axis=0)
    (dc,) = swap((dcm,), ((8, BLK, 128),), 4)
    dmsg = unattend(edge, r, aug, dc, lse, ct)
    (d,) = swap((dmsg,), ((8, BLK, 384),), 5)
    gpo, ig, pbs = last(d, x, dh1, w[0], go)
    input_grad = share(ig, 6).astype(f32)
    vin = jnp.concatenate([sums[:6].reshape(36, 128), sums[8:12].reshape(24, 128), pbs[:, 0].reshape(18, 128)])
    vin = jnp.pad(vin, ((0, 2), (0, 0)))
    red, vs = reduce_grads(gpo, gup, gdn, vin, 7)
    g0 = red[0]
    gq = g0[:, :576].reshape(24, 3, 3, 64)[:, turn].transpose(2, 0, 1, 3).reshape(3, 24, 192)
    gout = g0[:, 576:].reshape(24, 3, 64)[:, turn].reshape(24, 192).T
    fc = lax.axis_index(("fsdp", "ctx"))
    six = lax.dynamic_index_in_dim(vs[:36].reshape(6, 32, 24), fc, 1, keepdims=False)
    upb = lax.dynamic_index_in_dim(vs[36:60].reshape(4, 768), tp, 0, keepdims=False)
    pbq = lax.dynamic_index_in_dim(vs[60:78].reshape(4, 3, 3, 64), tp, 0, keepdims=False)
    pbg = pbq[turn][:, np.array([0, 2])].transpose(1, 0, 2).reshape(2, 192)
    return (
        layer_output,
        input_grad,
        gq,
        pbg,
        gout,
        six[0],
        six[2],
        six[3],
        red[1],
        upb,
        red[2].T,
        six[1],
        six[4],
        six[5],
    )


def solution(mesh):
    placed = (
        P("fsdp", "ctx", None),
        P("fsdp", "ctx"),
        P(None, "fsdp", "tp"),
        P(None, "tp"),
        P("tp", "fsdp"),
        P("fsdp"),
        P("fsdp"),
        P("fsdp"),
        P("fsdp", "tp"),
        P("tp"),
        P("tp", "fsdp"),
        P("fsdp"),
        P("fsdp"),
        P("fsdp"),
        P("fsdp", "ctx", None),
    )
    return jax.shard_map(
        shards,
        mesh=mesh,
        in_specs=placed,
        out_specs=(
            P("fsdp", "ctx", None),
            P("fsdp", "ctx", None),
            P(None, ("fsdp", "ctx"), "tp"),
            P(None, "tp"),
            P("tp", ("fsdp", "ctx")),
            P(("fsdp", "ctx")),
            P(("fsdp", "ctx")),
            P(("fsdp", "ctx")),
            P(("fsdp", "ctx"), "tp"),
            P("tp"),
            P("tp", ("fsdp", "ctx")),
            P(("fsdp", "ctx")),
            P(("fsdp", "ctx")),
            P(("fsdp", "ctx")),
        ),
        check_vma=False,
    )
```

time: 784 us -> 351 us (0.45)
  waiting for transfers between devices: 385 us -> 0.02 us
  Pallas kernels: 0 us -> 297 us
  matrix products: 160 us -> 0 us
  local copies, waits for them, and re-layouts: 99.4 us -> 32.4 us
  blocking collectives: 58.2 us -> 0 us
  other arithmetic: 50.8 us -> 8.41 us
  starting transfers between devices: 9.47 us -> 0.04 us
    pallas_call x0 -> x12, Pallas kernels: none -> 297 us  [the longest x1 73.6 us: reduce_grads(): pl.pallas_call(reduce_kernel, out_shape=(jax.ShapeDtypeStruct((3, 24, 768...]
    dot_general x20 -> x0, matrix products: 160 us -> none  [the longest x2 22.9 us: doc_scores(): jnp.einsum('sqhd,skhd->shqk', queries, key_rows, preferred_element_type=j...]
    psum x3 -> x0, waiting for transfers between devices: 147 us -> none  [the longest x1 50.6 us: shards(): lax.psum(norm_part.astype(jnp.bfloat16), 'tp').astype(jnp.float32)]
    all_gather x4 -> x1, waiting for transfers between devices: 137 us -> 0.01 us  [shards(): layer_output = lax.all_gather(lo, 'tp', axis=0)]
    unnamed x10 -> x1, waiting for transfers between devices: 94.1 us -> 0.02 us
    all_gather x2 -> x0, blocking collectives: 58.2 us -> none  [the longest x1 30.1 us: sent_together(): lax.all_gather(both, axis, axis=dim, tiled=True)]
    reduce_sum x12 -> x0, other arithmetic: 35.1 us -> none  [the longest x1 12 us: whole_attention(): row_total = jnp.sum(exp_terms, axis=-1, keepdims=True)]
    reshape x17 -> x20, local copies, waits for them, and re-layouts: 38.4 us -> 4 us  [the longest x2 0.89 us: shards(): g0[:, :576].reshape(24, 3, 3, 64)[:, turn].transpose(2, 0, 1, 3)]
  transfers between devices with their start and end apart: 10 -> 1, of which waited for: 9 -> 0; matrix products, arithmetic and copies ran while one was open for 15% -> 4% of each run, Pallas kernels for 0% -> 43%
where the time goes in v1:
time: 351 us; the launch traced here: 352 us
  Pallas kernels  297 us (85%)
  local copies, waits for them, and re-layouts  32.4 us (9%)
  between operations  14.5 us (4%)
  other arithmetic  8.41 us (2%)
    pallas_call x1, Pallas kernels, reduce_grads(): pl.pallas_call(reduce_kernel, out_shape=(jax.ShapeDtypeStruct((3, 24, 768...  73.6 us
    pallas_call x4, Pallas kernels, swap(): pl.pallas_call(functools.partial(swap_kernel, n), out_shape=tuple((jax.Sh...  63 us
    pallas_call x1, Pallas kernels, gather_weights(): pl.pallas_call(gather_kernel, out_shape=(jax.ShapeDtypeStruct((3, 4, 2, 2...  52.9 us
    pallas_call x1, Pallas kernels, attend(): pl.pallas_call(attend_kernel, out_shape=(jax.ShapeDtypeStruct((8, BLK, 12...  28.7 us
    pallas_call x1, Pallas kernels, unattend(): pl.pallas_call(unattend_kernel, out_shape=jax.ShapeDtypeStruct((8, BLK, 3...  28 us
    pallas_call x1, Pallas kernels, rows(): pl.pallas_call(rows_kernel, out_shape=(sd((BLK, 768), bf), sd((BLK, 768),...  21.6 us
    pallas_call x1, Pallas kernels, share(): pl.pallas_call(share_kernel, out_shape=jax.ShapeDtypeStruct((4, *a.shape)...  18.5 us
    unnamed x25, local copies, waits for them, and re-layouts  7.88 us
  transfers between devices with their start and end apart: 1, of which 0 were waited for; matrix products, arithmetic and copies ran while one was open for 4% of the time, Pallas kernels for 43%

profile of v1, /device:TPU:1, one launch (start us, length us, event | category | flops | bytes accessed | tf_op | source)
XLA Modules:
  0.0 352.3 jit_solution(7397009860933905064)
XLA Ops:
  7.3 0.7 pad_clamp_fusion.1
  7.9 0.8 reshape.125
  8.7 0.6 gather_fusion.2
  9.4 0.1 reshape.126
  9.5 0.8 pad_maximum_fusion.3
  10.3 0.8 fusion.10
  11.1 0.7 stack.37
  11.8 1.1 copy.77
  13.0 0.6 gather_fusion
  13.5 0.2 copy.79
  13.7 0.6 gather_fusion.1
  14.3 0.1 copy.80
  14.4 0.1 maximum_bitcast_fusion
  14.5 1.0 pad_maximum_fusion.pk
  15.5 0.6 fusion.7.vec
  16.2 52.9 %shard_map.335 = (bf16[3,4,2,2,192,768]{5,4,3,2,1,0:T(8,128)(2,1)}, bf16[4,2,2,8,768]{4,3,2,1,0:T(8,128)(2,1)}) custom-call(bf16[3,192,768]{2,1,0:T(8,128)(2,1)} %pad_maximum_fusion.pk, bf16[8,768]{1,0:T(8,128)(2,1)} %fusion.7.vec), custom_call_target="tpu_custom_call" | custom-call | tf_op jit(solution)/shard_map/pallas_call | solution.py:111
  69.1 1.1 copy_convert_fusion
  70.3 4.9 %slice.91 = bf16[1,4,2,2,192,768]{5,4,3,2,1,0:T(8,128)(2,1)} slice(bf16[3,4,2,2,192,768]{5,4,3,2,1,0:T(8,128)(2,1)} %get-tuple-element.33), slice={[0:1], [0:4], [0:2], [0:2], [0:192], [0:768]} | slice | bytes 9437184 | tf_op jit(solution)/shard_map/slice | solution.py:702
  75.1 0.7 constant_dynamic-slice_fusion.6
  75.8 1.9 dynamic-slice_bitcast_fusion
  77.7 4.3 %shard_map.336.refs_0_ = bf16[8,256,384]{2,1,0:T(8,128)(2,1)S(1)} custom-call(bf16[256,768]{1,0:T(8,128)(2,1)S(1)} %get-tuple-element.72.x, bf16[4,768,768]{2,1,0:T(8,128)(2,1)} %bitcast.74, f32[4,1,768]{2,1,0:T(1,128)S(1)} %copy.84.b), custom_call_target="tpu_custom_call" | custom-call | tf_op jit(solution)/shard_map/pallas_call | solution.py:275
  82.0 25.2 %shard_map.337 = (bf16[8,256,384]{2,1,0:T(8,128)(2,1)S(1)}, s32[8,8,128]{2,1,0:T(8,128)S(1)}) custom-call(bf16[8,256,384]{2,1,0:T(8,128)(2,1)S(1)} %shard_map.336.refs_0_, s32[8,128]{1,0:T(8,128)S(1)} %pad.23.refs_1_), custom_call_target="tpu_custom_call" | custom-call | tf_op jit(solution)/shard_map/pallas_call | solution.py:314
  107.2 0.1 copy.93
  107.3 0.5 select_convert_fusion.1
  107.8 0.3 pad_maximum_fusion.1.aug
  108.1 28.7 %shard_map.338 = (bf16[8,256,128]{2,1,0:T(8,128)(2,1)S(1)}, f32[16,8,256]{2,1,0:T(8,128)S(1)}, f32[2,64,2048]{2,1,0:T(8,128)S(1)}) custom-call(s32[2,8]{1,0:T(2,128)S(1)} %pad_add_fusion.edge, bf16[8,256,384]{2,1,0:T(8,128)(2,1)S(1)} %get-tuple-element.36.r, bf16[2048,128]{1,0:T(8,128)(2,1)S(1)} %pad_maximum_fusion.1.aug), custom_call_target="tpu_custom_call" | custom-call | tf_op jit(solution)/shard_map/pallas_call | solution.py:384
  136.8 1.0 copy-done.5
  137.8 12.2 %shard_map.339.cm = bf16[8,256,128]{2,1,0:T(8,128)(2,1)S(1)} custom-call(bf16[8,256,128]{2,1,0:T(8,128)(2,1)S(1)} %get-tuple-element.37.refs_0_), custom_call_target="tpu_custom_call" | custom-call | tf_op jit(solution)/shard_map/pallas_call | solution.py:314
  150.1 0.8 copy-done.3
  150.9 0.1 reshape_squeeze.9
  151.0 0.1 reshape.130
  151.1 0.1 reshape_squeeze.10
  151.2 0.1 reshape.131
  151.3 1.3 concatenate.22.pv
  152.5 21.6 %shard_map.340 = (bf16[256,768]{1,0:T(8,128)(2,1)}, f32[256,768]{1,0:T(8,128)}, bf16[4,768,768]{2,1,0:T(8,128)(2,1)}, bf16[4,768,768]{2,1,0:T(8,128)(2,1)}, bf16...) custom-call(bf16[3,4,768,768]{3,2,1,0:T(8,128)(2,1)} %bitcast.76, ...), custom_call_target="tpu_custom_call" | custom-call | tf_op jit(solution)/shard_map/pallas_call | solution.py:566
  174.2 0.7 slice.99
  174.9 0.7 slice.100
  175.7 1.0 copy-done.8
  176.7 9.7 %shard_map.341.dc = bf16[8,256,128]{2,1,0:T(8,128)(2,1)S(1)} custom-call(bf16[8,256,128]{2,1,0:T(8,128)(2,1)S(1)} %copy-done.8), custom_call_target="tpu_custom_call" | custom-call | tf_op jit(solution)/shard_map/pallas_call | solution.py:314
  186.4 1.2 copy-done.6
  187.6 28.0 %shard_map.342.refs_0_ = bf16[8,256,384]{2,1,0:T(8,128)(2,1)S(1)} custom-call(s32[2,8]{1,0:T(2,128)S(1)} %pad_add_fusion.edge, bf16[8,256,384]{2,1,0:T(8,128)(2,1)S(1)} %get-tuple-element.36.r, bf16[2048,128]{1,0:T(8,128)(2,1)S(1)} %pad_maximum_fusion.1.aug, bf16[8,256,128]{2,1,0:T(8,128)(2,1)S(1)} %shard_map.341.dc, ...), custom_call_target="tpu_custom_call" | custom-call | tf_op jit(solution)/shard_map/pallas_call | solution.py:452
  215.6 15.9 %shard_map.343.d = bf16[8,256,384]{2,1,0:T(8,128)(2,1)S(1)} custom-call(bf16[8,256,384]{2,1,0:T(8,128)(2,1)S(1)} %shard_map.342.refs_0_), custom_call_target="tpu_custom_call" | custom-call | tf_op jit(solution)/shard_map/pallas_call | solution.py:314
  231.5 6.4 %shard_map.344 = (bf16[4,768,768]{2,1,0:T(8,128)(2,1)}, bf16[256,768]{1,0:T(8,128)(2,1)S(1)}, f32[4,8,576]{2,1,0:T(8,128)S(1)}) custom-call(bf16[8,256,384]{2,1,0:T(8,128)(2,1)S(1)} %shard_map.343.d, bf16[256,768]{1,0:T(8,128)(2,1)S(1)} %copy-done.2, f32[256,768]{1,0:T(8,128)S(1)} %copy-done.7, bf16[4,768,768]{2,1,0:T(8,128)(2,1)} %bitcast.75, ...), custom_call_target="tpu_custom_call" | custom-call | tf_op jit(solution)/shard_map/pallas_call | solution.py:612
  237.9 0.1 reshape_squeeze.11
  238.0 0.6 select_maximum_fusion.vin
  238.7 73.6 %shard_map.346 = (f32[3,24,768]{2,1,0:T(8,128)}, f32[80,128]{1,0:T(8,128)}) custom-call(bf16[4,2,2,2,4,24,768]{6,5,4,3,2,1,0:T(8,128)(2,1)} %bitcast.79, bf16[4,2,2,2,4,24,768]{6,5,4,3,2,1,0:T(8,128)(2,1)} %bitcast.77, bf16[4,2,2,2,4,24,768]{6,5,4,3,2,1,0:T(8,128)(2,1)} %bitcast.78, f32[80,128]{1,0:T(8,128)} %select_maximum_fusion.vin), custom_call_target="tpu_custom_call" | custom-call | tf_op jit(solution)/shard_map/pallas_call | solution.py:241
  312.3 1.6 slice_bitcast_fusion
  314.0 0.7 slice.106
  314.7 0.7 slice.104
  315.4 0.7 slice.111
  316.2 0.1 reshape.137
  316.3 0.7 gather_fusion.3
  317.0 0.8 reshape.138
  317.9 0.6 gather_fusion.6
  318.5 0.7 reshape.142
  319.2 0.1 reshape.143
  319.4 0.6 gather_fusion.4
  320.0 0.6 gather_fusion.5
  320.5 0.7 reshape.140
  321.2 18.5 %shard_map.345 = bf16[4,256,768]{2,1,0:T(8,128)(2,1)S(1)} custom-call(bf16[256,768]{1,0:T(8,128)(2,1)S(1)} %get-tuple-element.44.a), custom_call_target="tpu_custom_call" | custom-call | tf_op jit(solution)/shard_map/pallas_call | solution.py:649
  339.7 1.9 convert_element_type.23
  341.6 0.6 dynamic-slice_reduce_fusion
  342.2 0.5 fusion.11
  342.8 2.7 copy.102
  (60 shorter events, 0.9 us)
Async XLA Ops:
  7.2 6.5 %copy-start = (bf16[192,192]{1,0:T(8,128)(2,1)S(1)}, bf16[192,192]{1,0:T(8,128)(2,1)}, u32[]{:S(2)}) copy-start(bf16[192,192]{1,0:T(8,128)(2,1)} %param.28) | copy-start | bytes 221188
  7.2 335.6 %all-gather.3.cloned.1.call-start = ((), (), s32[]{:S(2)}) async-start(), calls=%async_computation | async-start | bytes 1966080 | tf_op jit(solution)/shard_map/all_gather | solution.py:715
  12.9 1.6 copy-start.9
  13.0 1.6 copy-start.10
  77.7 4.3 %copy-start.1 = (bf16[256,768]{1,0:T(8,128)(2,1)}, bf16[256,768]{1,0:T(8,128)(2,1)S(1)}, u32[]{:S(2)}) copy-start(bf16[256,768]{1,0:T(8,128)(2,1)S(1)} %get-tuple-element.72.x) | copy-start | bytes 1179652
  136.8 1.0 copy-start.5
  150.1 0.8 copy-start.3
  175.6 1.0 copy-start.8
  186.4 1.2 copy-start.6
  215.6 15.9 %copy-start.2 = (bf16[256,768]{1,0:T(8,128)(2,1)S(1)}, bf16[256,768]{1,0:T(8,128)(2,1)}, u32[]{:S(2)}) copy-start(bf16[256,768]{1,0:T(8,128)(2,1)} %copy-done.1) | copy-start | bytes 1179652
  215.6 15.9 %copy-start.4 = (bf16[4,768,192]{2,1,0:T(8,128)(2,1)S(1)}, bf16[4,768,192]{2,1,0:T(8,128)(2,1)}, u32[]{:S(2)}) copy-start(bf16[4,768,192]{2,1,0:T(8,128)(2,1)} %get-tuple-element.43.go) | copy-start | bytes 3538948
  215.6 15.9 %copy-start.7 = (f32[256,768]{1,0:T(8,128)S(1)}, f32[256,768]{1,0:T(8,128)}, u32[]{:S(2)}) copy-start(f32[256,768]{1,0:T(8,128)} %get-tuple-element.42.dh1) | copy-start | bytes 2359300
Sparse Core Ops, SparseCore 0:
  174.3 31.1 all-gather.2

commit v2 on v0

v2 whole, which is shorter than its diff:
```python
import functools
import math

import jax
import jax.numpy as jnp
from jax import lax
from jax.experimental import pallas as pl
from jax.experimental.pallas import tpu as pltpu
from jax.sharding import PartitionSpec as P

HEAD_DIM = 64
NORM_EPS = 1e-12

MESH = pl.DeviceIdType.MESH
bf=jnp.bfloat16; f32=jnp.float32

class Place:
    def __init__(self):
        self.x=lax.axis_index("tp"); f=lax.axis_index("fsdp"); c=lax.axis_index("ctx")
        self.yl=f//2; self.core=f%2; self.yh=c//4; self.z=c%4
        self.y=self.yh*2+self.yl
    def px(self,k):
        q=(self.x+k)%4
        return {"tp":q}, q
    def pz(self,k):
        q=(self.z+k)%4
        return {"ctx":self.yh*4+q}, q
    def py(self,k):
        q=(self.y+k)%4
        return {"fsdp":(q%2)*2+self.core,"ctx":(q//2)*4+self.z}, (q%2,q//2)
    def sib(self):
        return {"fsdp":self.yl*2+1-self.core}

def greet(devs):
    bar=pltpu.get_barrier_semaphore()
    for d in devs: pl.semaphore_signal(bar,inc=1,device_id=d,device_id_type=MESH)
    pl.semaphore_wait(bar,len(devs))

def rcopy(src,dst,ss,rs,dev):
    return pltpu.make_async_remote_copy(src_ref=src,dst_ref=dst,send_sem=ss,recv_sem=rs,device_id=dev,device_id_type=MESH)


DIMS = {"x": (4,), "y": (2, 2), "z": (4,)}
ORDER = ("xyz", "yzx", "zxy")


def shape_of(axes):
    return sum([DIMS[d] for d in "xyz" if d in axes], ())


def split_index(i, shape):
    out = []
    for s in reversed(shape):
        out.insert(0, i % s)
        i = i // s
    return tuple(out)


def pick(ref, axis, q, left):
    at = []
    for d in "xyz":
        if d in left:
            at += list(q if d == "y" else (q,)) if d == axis else [slice(None)] * len(DIMS[d])
    return ref.at[tuple(at)]


def total(dst, first, others, shape):
    count = math.prod(shape)

    @pl.loop(0, count)
    def _(i):
        at = split_index(i, shape)
        a = first[at].astype(f32)
        for o in others:
            a = a + o[at].astype(f32)
        dst[at] = a.astype(dst.dtype)


SQ = HEAD_DIM ** -0.5
FAR = float(2.0 ** 100)
BLK = 256


def nt(a, b):
    return lax.dot_general(a, b, (((1,), (1,)), ((), ())), preferred_element_type=f32)


def nn(a, b):
    return jnp.dot(a, b, preferred_element_type=f32)


def params(cid=None, mb=48):
    return pltpu.CompilerParams(collective_id=cid, has_side_effects=cid is not None, vmem_limit_bytes=mb << 20)


class Sender:
    def __init__(self, ss, rs):
        self.ss, self.rs, self.all = ss, rs, []

    def __call__(self, src, dst, dev):
        i = len(self.all)
        c = rcopy(src, dst, self.ss.at[i], self.rs.at[i], dev)
        c.start()
        self.all.append(c)
        return c


AXES = (1, 2, 3)


class Spread:
    def __init__(self, p, send, own, to, rx, ry, rz):
        self.p, self.send, self.own, self.to = p, send, own, to
        self.rx, self.ry, self.rz = rx, ry, rz
        self.half = ry[0] + pl.multiple_of(p.yh * (ry[1] // 2), 8), ry[1] // 2
        self.quarter = rz[0] + pl.multiple_of(p.z * (rz[1] // 4), 8), rz[1] // 4

    def rows(self, what):
        a, n = what
        return pl.ds(a if isinstance(a, int) else pl.multiple_of(a, 8), n)

    def out(self, t, yl, what):
        return self.to.at[t, yl, self.p.core, self.rows(what)]

    def pass_on(self, t, yl, what, devs):
        return [self.send(self.out(t, yl, what), self.out(t, yl, what), d) for d in devs]

    def start(self):
        p = self.p
        nb = {"fsdp": (1 - p.yl) * 2 + p.core}
        mine = lambda what: self.own.at[self.rows(what)]
        push = lambda what, devs: [self.send(mine(what), self.out(p.x, p.yl, what), d) for d in devs]
        xs = [p.px(k)[0] for k in AXES]
        self.nz = push(self.quarter, [nb])[0] if self.rz[1] else None
        self.nx = push(self.rx, [nb])[0]
        self.xy = push(self.half, xs)
        self.xz = push(self.quarter, xs)
        self.yy = push(self.half, [p.py(k)[0] for k in (1, 3)])

    def second(self):
        p = self.p
        xs = [p.px(k)[0] for k in AXES]
        ys = [p.py(k)[0] for k in AXES]
        zs = [p.pz(k)[0] for k in AXES]
        self.nz.wait_recv()
        self.xz2 = self.pass_on(p.x, 1 - p.yl, self.quarter, xs)
        self.zz = self.pass_on(p.x, 1 - p.yl, self.quarter, zs)
        self.xx = [self.send(self.own.at[self.rows(self.rx)], self.out(p.x, p.yl, self.rx), d) for d in xs]
        self.nx.wait_recv()
        self.xx2 = self.pass_on(p.x, 1 - p.yl, self.rx, xs)
        for k in AXES:
            t = (p.x + 4 - k) % 4
            self.xy[k - 1].wait_recv()
            self.yy += self.pass_on(t, p.yl, self.half, ys)
            self.xz[k - 1].wait_recv()
            self.zz += self.pass_on(t, p.yl, self.quarter, zs)
        for k in AXES:
            t = (p.x + 4 - k) % 4
            self.xz2[k - 1].wait_recv()
            self.zz += self.pass_on(t, 1 - p.yl, self.quarter, zs)

    def finish(self):
        for c in self.yy + self.zz + self.xx + self.xx2:
            c.wait_recv()


def front_kernel(p0, p1, p2, vec, xs, seg, W, V, R, S, po, m, x, ss, rs, ls):
    p = Place()
    c = lax.axis_index("ctx")
    core, sib = p.core, p.sib()
    ctx = [{"ctx": (c + k) % 8} for k in range(1, 8)]
    greet([p.px(k)[0] for k in AXES] + [p.py(k)[0] for k in (1, 3)] + ctx + [sib])
    send = Sender(ss, rs)
    own = pltpu.make_async_copy(p0, po.at[p.x, p.yl, core], ls.at[0])
    mine = pltpu.make_async_copy(vec, V.at[p.x, p.yl, core], ls.at[1])
    rows = pltpu.make_async_copy(xs.at[p.x], x, ls.at[2])
    up = pltpu.make_async_copy(p1, W.at[1, p.x, p.yl, core], ls.at[4])
    down = pltpu.make_async_copy(p2, W.at[2, p.x, p.yl, core], ls.at[5])
    for cp in (own, mine, rows, up, down):
        cp.start()
    nb = {"fsdp": (1 - p.yl) * 2 + core}
    first = Spread(p, send, p0, po, (0, 64), (64, 64), (128, 64))
    first.start()
    vn = send(vec, V.at[p.x, p.yl, core], nb)
    vx = [send(vec, V.at[p.x, p.yl, core], p.px(k)[0]) for k in AXES]
    sg = [send(seg, S.at[c], d) for d in ctx]
    sgo = pltpu.make_async_copy(seg, S.at[c], ls.at[3])
    sgo.start()
    d0 = [send(p0, po.at[p.x, p.yl, core], sib)]
    dv = [send(vec, V.at[p.x, p.yl, core], sib)]
    first.second()
    vn.wait_recv()
    vx += [send(V.at[p.x, 1 - p.yl, core], V.at[p.x, 1 - p.yl, core], p.px(k)[0]) for k in AXES]
    bulk = [
        Spread(p, send, p1, W.at[1], (0, 96), (96, 64), (160, 32)),
        Spread(p, send, p2, W.at[2], (0, 64), (64, 64), (128, 64)),
    ]
    for b in bulk:
        b.start()
    first.finish()
    for cp in vx:
        cp.wait_recv()
    own.wait()
    mine.wait()
    d0.append(send(po.at[p.x, 1 - p.yl, core], po.at[p.x, 1 - p.yl, core], sib))
    dv.append(send(V.at[p.x, 1 - p.yl, core], V.at[p.x, 1 - p.yl, core], sib))
    for k in AXES:
        t = (p.x + k) % 4
        d0.append(send(po.at[t, :, core], po.at[t, :, core], sib))
        dv.append(send(V.at[t, :, core], V.at[t, :, core], sib))
    for b in bulk:
        b.second()
    for cp in d0 + dv:
        cp.wait_recv()
    rows.wait()
    back = pltpu.make_async_copy(po, W.at[0], ls.at[0])
    back.start()

    @pl.loop(0, 4)
    def _(t):
        b = V[t, 0, 0, 1:2].astype(f32)
        r = (nn(x[...], po[t].reshape(768, 768)) + b).astype(bf)
        m[2 * t] = r[:, :384]
        m[2 * t + 1] = jnp.concatenate([r[:, 384:576], r[:, 192:384]], axis=1)

    sw = [send(m.at[(c + k) % 8], R.at[c], {"ctx": (c + k) % 8}) for k in range(1, 8)]
    swo = pltpu.make_async_copy(m.at[c], R.at[c], ls.at[2])
    swo.start()
    for b in bulk:
        b.finish()
    up.wait()
    down.wait()
    dw = []
    for k in range(4):
        t = (p.x + k) % 4
        dw.append(send(W.at[pl.ds(1, 2), t, :, core], W.at[pl.ds(1, 2), t, :, core], sib))
    for cp in sg + sw + dw:
        cp.wait_recv()
    for cp in send.all:
        cp.wait_send()
    for cp in (back, swo, sgo):
        cp.wait()


def front(p0, p1, p2, vec, xs, seg, cid):
    sd = jax.ShapeDtypeStruct
    vm = pltpu.VMEM
    anywhere, here = pl.BlockSpec(memory_space=pl.ANY), pl.BlockSpec(memory_space=vm)
    count = 192
    return pl.pallas_call(
        front_kernel,
        out_shape=(
            sd((3, 4, 2, 2, 192, 768), bf),
            sd((4, 2, 2, 8, 768), bf),
            sd((8, BLK, 384), bf),
            sd((8, 2, 128), jnp.int32),
        ),
        in_specs=[anywhere] * 6,
        out_specs=[anywhere, here, anywhere, anywhere],
        scratch_shapes=[
            vm((4, 2, 2, 192, 768), bf),
            vm((8, BLK, 384), bf),
            vm((BLK, 768), bf),
            pltpu.SemaphoreType.DMA((count,)),
            pltpu.SemaphoreType.DMA((count,)),
            pltpu.SemaphoreType.DMA((6,)),
        ],
        compiler_params=params(cid),
    )(p0, p1, p2, vec, xs, seg)


LONG = 2048 + BLK
SAFE = 120.0 / SQ
FWD = 8
BWD = 4


def blocks(edge, lst, par, unit):
    n = jnp.int32(0)
    for h in range(2):
        for i in range(8 if h == 0 else 4):
            qi = i if h == 0 else 2 * i + par
            lo, hi = jnp.int32(0), jnp.int32(0)
            for j in range(8):
                lo = lo + (edge[j, 1, 127] < edge[qi, 0, 0]).astype(jnp.int32)
                hi = hi + (edge[j, 0, 0] <= edge[qi, 1, 127]).astype(jnp.int32)

            def put(j, n):
                lst[n] = (h * 8 + qi) * 16 + j
                return n + 1

            n = lax.fori_loop(lo, hi, put, n)
    for k in range(unit - 1):
        lst[n + k] = 8
    return (n + unit - 1) // unit


def triple(code):
    j = code % 16
    i = (code // 16) % 8
    return code // 128, pl.ds(pl.multiple_of(i * BLK, BLK), BLK), pl.ds(pl.multiple_of(j * BLK, BLK), BLK), i


def lanes():
    return lax.broadcasted_iota(jnp.int32, (1, 128), 1)


def three(v, at, lane):
    a = v.astype(bf).astype(f32)
    b = (v - a).astype(bf).astype(f32)
    c = v - a - b
    return jnp.where(lane == at, a, jnp.where(lane == at + 1, b, jnp.where(lane == at + 2, c, 0.0))).astype(bf)


def flat(r, k):
    return r[:, :, 128 * k : 128 * k + 128].reshape(2048, 128)


def turned(v):
    return v.astype(f32).T.astype(bf)


def one_lane(h, lane):
    return lane == (72 if h == 0 else 8)


def doc_rows(docs):
    seg = jnp.concatenate([docs[j, i : i + 1] for j in range(8) for i in range(2)] + [jnp.full((1, BLK), -1)], axis=1)
    row = lax.broadcasted_iota(jnp.int32, (64, 1), 0)
    return seg, jnp.where(((row < 4) & (row != seg)) | ((row >= 8) & (row < 11)), 1.0, 0.0)


def attend_kernel(edge, docs, r, msg, acc, qa, kt, va, top, lst):
    par = lax.axis_index("ctx") % 2
    lane = lanes()
    count = blocks(edge, lst, par, FWD)
    seg, augk = doc_rows(docs)
    row = lax.broadcasted_iota(jnp.int32, (128, 1), 0) - 64
    augq = jnp.where(row == seg[:, :2048], -FAR, 0.0).T.astype(bf)
    augk = augk.astype(bf)
    vv = flat(r, 1)
    safe = jnp.bool_(True)
    for h in range(2):
        qk = flat(r, 2 * h)
        qa[h] = jnp.where(lane < 64, qk * bf(SQ), augq)
        kt[h, :64, :2048] = turned(qk)[64:]
        kt[h, :64, 2048:] = jnp.zeros((64, BLK), bf)
        kt[h, 64:] = augk
        va[h, :2048] = jnp.where((lane < 64) if h == 0 else (lane >= 64), vv, one_lane(h, lane).astype(bf))
        va[h, 2048:] = jnp.zeros((BLK, 128), bf)
        f = qk.astype(f32)
        safe = safe & (jnp.max(jnp.sum(f * f, axis=1, keepdims=True)) < SAFE)
    acc[...] = jnp.zeros_like(acc)

    @pl.when(jnp.logical_not(safe))
    def _():
        top[...] = jnp.full_like(top, -3e38)

        @pl.loop(0, count * FWD)
        def _(n):
            h, at, to, i = triple(lst[n])
            s = jnp.max(nn(qa[h, at], kt[h, :, to]), axis=1, keepdims=True)
            top[h, at] = jnp.maximum(top[h, at], s)

        for h in range(2):
            for i in range(8):
                at = slice(i * BLK, i * BLK + BLK)
                qa[h, at] = qa[h, at] + three(-top[h, at, :1], 72, lane)

    @pl.loop(0, count)
    def _(n):
        got = []
        for u in range(FWD):
            h, at, to, _ = triple(lst[n * FWD + u])
            p = jnp.exp(nn(qa[h, at], kt[h, :, to])).astype(bf)
            got.append((h, at, nn(p, va[h, to])))
        for h, at, o in got:
            acc[h, at] += o

    for i in range(8):
        at = slice(i * BLK, i * BLK + BLK)
        a = acc[0, at] * (1.0 / acc[0, at, 72:73])
        b = acc[1, at] * (1.0 / acc[1, at, 8:9])
        b = jnp.where(par == i % 2, b, 0.0)
        msg[i] = jnp.where(lane < 64, a, b).astype(bf)


def attend(docs, r):
    vm = pltpu.VMEM
    sd = jax.ShapeDtypeStruct
    return pl.pallas_call(
        attend_kernel,
        out_shape=(sd((8, BLK, 128), bf), sd((2, 2048, 128), f32), sd((2, 2048, 128), bf)),
        in_specs=[pl.BlockSpec(memory_space=pltpu.SMEM)] + [pl.BlockSpec(memory_space=vm)] * 2,
        out_specs=[pl.BlockSpec(memory_space=vm)] * 3,
        scratch_shapes=[
            vm((2, 128, LONG), bf),
            vm((2, LONG, 128), bf),
            vm((2, 2048, 128), f32),
            pltpu.SMEM((128,), jnp.int32),
        ],
        compiler_params=params(),
    )(docs, docs, r)


def unattend_kernel(edge, docs, r, dc, acc, qa, out, ka, va, kt, ga, gz, qz, dkv, dqt, lst):
    par = lax.axis_index("ctx") % 2
    lane = lanes()
    count = blocks(edge, lst, par, BWD)
    vv, gg = flat(r, 1), flat(dc, 0)
    tops = doc_rows(docs)[1].T.astype(bf)
    for h in range(2):
        qk = flat(r, 2 * h)
        low = (lane < 64) if h == 0 else (lane >= 64)
        at = 72 if h == 0 else 8
        kt[h, :, :2048] = turned(qk)[64:]
        kt[h, :, 2048:] = jnp.zeros((64, BLK), bf)
        ka[h, :2048] = jnp.concatenate([qk[:, 64:], tops[:2048]], axis=1)
        ka[h, 2048:] = jnp.concatenate([jnp.zeros((BLK, 64), bf), tops[2048:]], axis=1)
        ones = ((lane >= at) & (lane < at + 3)).astype(bf)
        va[h, :2048] = jnp.where(low, vv, ones)
        va[h, 2048:] = jnp.zeros((BLK, 128), bf)
        inv = 1.0 / acc[h, :, at : at + 1]
        g = jnp.where(low, gg.astype(f32), 0.0)
        g = (g * inv).astype(bf)
        delta = jnp.sum(g.astype(f32) * acc[h], axis=1, keepdims=True) * inv
        gz[h] = g
        ga[h] = g + three(-delta, at, lane)
        q = jnp.where(lane < 64, qa[h], bf(0))
        qz[h] = pltpu.roll(q.astype(f32), 64, 1).astype(bf) if h == 0 else q
    dqt[...] = jnp.zeros_like(dqt)
    dkv[...] = jnp.zeros_like(dkv)

    @pl.loop(0, count)
    def _(n):
        got = []
        for u in range(BWD):
            h, at, to, _ = triple(lst[n * BWD + u])
            p = jnp.exp(nt(ka[h, to], qa[h, at]))
            ds = (p * nt(va[h, to], ga[h, at])).astype(bf)
            kv = nn(p.astype(bf), gz[h, at]) + nn(ds, qz[h, at])
            got.append((h, at, to, kv, nn(kt[h, :, to], ds)))
        for h, at, to, kv, dq in got:
            dkv[h, to] += kv
            dqt[h, :, at] += dq

    for i in range(8):
        a = slice(i * BLK, i * BLK + BLK)
        q0, q1 = [jnp.concatenate([(dqt[h, :, a] * SQ).T] * 2, axis=1) for h in range(2)]
        q1 = jnp.where(par == i % 2, q1, 0.0)
        kv0, kv1 = dkv[0, a], dkv[1, a]
        out[i, :, :128] = jnp.where(lane < 64, q0, kv0).astype(bf)
        out[i, :, 128:256] = jnp.where(lane < 64, kv0, kv1).astype(bf)
        out[i, :, 256:] = jnp.where(lane < 64, q1, pltpu.roll(kv1, 64, 1)).astype(bf)


def unattend(docs, r, dc, acc, qa):
    vm = pltpu.VMEM
    return pl.pallas_call(
        unattend_kernel,
        out_shape=jax.ShapeDtypeStruct((8, BLK, 384), bf),
        in_specs=[pl.BlockSpec(memory_space=pltpu.SMEM)] + [pl.BlockSpec(memory_space=vm)] * 5,
        out_specs=pl.BlockSpec(memory_space=vm),
        scratch_shapes=[
            vm((2, LONG, 128), bf),
            vm((2, LONG, 128), bf),
            vm((2, 64, LONG), bf),
            vm((2, 2048, 128), bf),
            vm((2, 2048, 128), bf),
            vm((2, 2048, 128), bf),
            vm((2, LONG, 128), f32),
            vm((2, 64, 2048), f32),
            pltpu.SMEM((128,), jnp.int32),
        ],
        compiler_params=params(),
    )(docs, docs, r, dc, acc, qa)


class Reducer:
    def __init__(self, p, send, order, refs):
        self.p, self.send, self.order = p, send, order
        self.acc, self.cor, self.r1, self.s1, self.r2, self.s2, self.r3 = refs
        self.peers = {"x": p.px, "y": p.py, "z": p.pz}
        self.here = {"x": p.x, "y": (p.yl, p.yh), "z": p.z}
        self.left = [[d for d in "xyz" if d not in order[:n]] for n in range(3)]

    def begin(self, src, sem=None):
        self.c0 = self.send(src.at[:, :, 1 - self.p.core], self.cor, self.p.sib())
        self.own = None
        if sem is not None:
            self.own = pltpu.make_async_copy(src.at[:, :, self.p.core], self.acc, sem)
            self.own.start()

    def scatter(self, src, into, n):
        a = self.order[n]
        return [
            self.send(pick(src, a, self.peers[a](j)[1], self.left[n]), into.at[j - 1], self.peers[a](j)[0]) for j in AXES
        ]

    def first(self):
        self.c0.wait_recv()
        if self.own is not None:
            self.own.wait()
        total(self.acc, self.acc, [self.cor], shape_of("xyz"))
        self.c1 = self.scatter(self.acc, self.r1, 0)

    def gathered(self, copies, out, src, got, n):
        for c in copies:
            c.wait_recv()
        a = self.order[n]
        total(out, pick(src, a, self.here[a], self.left[n]), [got.at[j] for j in range(3)], shape_of(self.left[n + 1]))

    def second(self):
        self.gathered(self.c1, self.s1, self.acc, self.r1, 0)
        self.c2 = self.scatter(self.s1, self.r2, 1)

    def third(self):
        self.gathered(self.c2, self.s2, self.s1, self.r2, 1)
        self.c3 = self.scatter(self.s2, self.r3, 2)

    def result(self):
        for c in self.c3:
            c.wait_recv()
        a = self.order[2]
        m = pick(self.s2, a, self.here[a], self.left[2])[...].astype(f32)
        for j in range(3):
            m = m + self.r3[j].astype(f32)
        return m


def reducer_scratch(order, n):
    vm = pltpu.VMEM
    one, two = shape_of([d for d in "xyz" if d != order[0]]), shape_of(order[2])
    whole = (*shape_of("xyz"), 24, n)
    shapes = [whole, whole, (3, *one, 24, n), (*one, 24, n), (3, *two, 24, n), (*two, 24, n), (3, 24, n)]
    return [vm(s, bf) for s in shapes]


MID = ("yzx", "zyx")


def norm_of(v):
    d = v - jnp.mean(v, axis=-1, keepdims=True)
    s = lax.rsqrt(jnp.mean(d * d, axis=-1, keepdims=True) + NORM_EPS)
    return d * s, s


def norm_back(g, xhat, s, gain):
    e = g * gain
    return s * (e - jnp.mean(e, axis=-1, keepdims=True) - xhat * jnp.mean(e * xhat, axis=-1, keepdims=True))


def down_sum(v):
    return jnp.sum(v, axis=0, keepdims=True)


def store_pieces(g, t, a, b):
    for i in range(32):
        at = (t, i // 16, i // 8 % 2, i // 4 % 2, i % 4)
        piece = g[24 * i : 24 * i + 24].astype(bf)
        a[at] = piece[:, :384]
        b[at] = piece[:, 384:]


def mid_kernel(w, cms, xs, cots, vec, LO, dh1, gup, go, DC, sums, o0, o1, *refs):
    red = [[*refs[3 * i : 3 * i + 3], (o0, o1)[i], None, None, None] for i in range(2)]
    refs = refs[6:]
    cm, wv, wo, zs, cdf, act, gs, ga, gb, lob, dcm, x, cot, ss, rs, ls, os = refs
    p = Place()
    c = lax.axis_index("ctx")
    ctx = [{"ctx": (c + k) % 8} for k in range(1, 8)]
    greet([p.px(k)[0] for k in AXES] + [p.py(k)[0] for k in (1, 3)] + ctx + [p.sib()])
    send = Sender(ss, rs)
    sw = [send(cms.at[(c + k) % 8], cm.at[c], {"ctx": (c + k) % 8}) for k in range(1, 8)]
    swo = pltpu.make_async_copy(cms.at[c], cm.at[c], ls.at[12])
    swo.start()
    ins = [pltpu.make_async_copy(a.at[p.x], b, ls.at[n]) for a, b, n in ((xs, x, 13), (cots, cot, 14))]
    loads = []
    for k in range(3):
        for t in range(4):
            cp = pltpu.make_async_copy(w.at[k, t], wv.at[k * 4 + t], ls.at[k * 4 + t])
            cp.start()
            loads.append(cp)
    for cp in ins:
        cp.start()
    fours = [vec[0, f // 2, f % 2].astype(f32) for f in range(4)]
    pv = [
        jnp.concatenate([f[2 + i // 4 : 3 + i // 4, 192 * (i % 4) : 192 * (i % 4) + 192] for f in fours], axis=1)
        for i in range(6)
    ]
    for t in range(4):
        loads[t].wait()
        o = wv[t, :, 576:768]
        wo[2 * t] = o[:, :128]
        wo[2 * t + 1] = jnp.concatenate([o[:, 128:], o[:, 64:128]], axis=1)
    swo.wait()
    for cp in ins:
        cp.wait()
    for cp in sw:
        cp.wait_recv()
    attn = jnp.zeros((BLK, 768), f32)
    for j in range(8):
        attn = attn + nt(cm[j], wo[j])
    h1 = x[...].astype(f32) + attn + pv[0]
    xh1, s1 = norm_of(h1)
    y1 = xh1 * pv[2] + pv[3]
    y1b = y1.astype(bf)
    ffn = jnp.zeros((BLK, 768), f32)
    for t in range(4):
        loads[4 + t].wait()
        z = nn(y1b, wv[4 + t]) + vec[t, 0, 0, 0:1].astype(f32)
        e = 0.5 * (1.0 + lax.erf(z * (2.0**-0.5)))
        zs[t] = z
        cdf[t] = e
        a = (z * e).astype(bf)
        act[t] = a
        loads[8 + t].wait()
        ffn = ffn + nt(a, wv[8 + t])
    xh2, s2 = norm_of(y1 + ffn + pv[1])
    lob[...] = (xh2 * pv[4] + pv[5]).astype(bf)
    los = [send(lob, LO.at[p.x], p.px(k)[0]) for k in AXES]
    loo = pltpu.make_async_copy(lob, LO.at[p.x], ls.at[12])
    loo.start()
    g = cot[...].astype(f32)
    sums[4:5] = down_sum(g * xh2)
    sums[5:6] = down_sum(g)
    dh2 = norm_back(g, xh2, s2, pv[4])
    sums[1:2] = down_sum(dh2)
    dh2b = dh2.astype(bf)
    dh2t = dh2.T.astype(bf)
    y1t = y1.T.astype(bf)
    for t in range(4):
        store_pieces(nn(dh2t, act[t]), t, ga, gb)
    parts = [Reducer(p, send, o, r) for o, r in zip(MID, red)]
    parts[0].begin(ga, ls.at[0])
    parts[1].begin(gb, ls.at[1])
    dy1 = dh2
    outs = []
    for t in range(4):
        da = nn(dh2b, wv[8 + t]).astype(bf).astype(f32)
        z = zs[t]
        dz = da * (cdf[t] + z * (jnp.exp(-0.5 * z * z) * ((2.0 * math.pi) ** -0.5)))
        sums[8 + t : 9 + t] = down_sum(dz)
        dzb = dz.astype(bf)
        if t >= 2:
            outs[t - 2].wait()
        gs[t % 2] = nn(y1t, dzb).astype(bf)
        cp = pltpu.make_async_copy(gs.at[t % 2], gup.at[t], os.at[t % 2])
        cp.start()
        outs.append(cp)
        dy1 = dy1 + nt(dzb, wv[4 + t])
        if t == 0:
            for part in parts:
                part.first()
    sums[2:3] = down_sum(dy1 * xh1)
    sums[3:4] = down_sum(dy1)
    d1 = norm_back(dy1, xh1, s1, pv[2])
    dh1[...] = d1
    sums[0:1] = down_sum(d1)
    d1b = d1.astype(bf)
    d1t = d1.T.astype(bf)
    for j in range(8):
        dcm[j] = nn(d1b, wo[j]).astype(bf)
    sw = [send(dcm.at[(c + k) % 8], DC.at[c], {"ctx": (c + k) % 8}) for k in range(1, 8)]
    swo = pltpu.make_async_copy(dcm.at[c], DC.at[c], ls.at[2])
    swo.start()
    for t in range(4):
        a, b = nn(d1t, cm[2 * t]), nn(d1t, cm[2 * t + 1])
        go[t] = jnp.concatenate([a[:, :64], a[:, 64:] + b[:, 64:], b[:, :64]], axis=1).astype(bf)
    for part in parts:
        part.gathered(part.c1, part.s1, part.acc, part.r1, 0)
    for cp in los + sw:
        cp.wait_recv()
    for cp in outs[2:] + [swo, loo]:
        cp.wait()
    for cp in send.all:
        cp.wait_send()


def middle(w, cms, xs, cots, vec, cid):
    vm = pltpu.VMEM
    sd = jax.ShapeDtypeStruct
    anywhere, here = pl.BlockSpec(memory_space=pl.ANY), pl.BlockSpec(memory_space=vm)
    left = [shape_of([d for d in "xyz" if d != o[0]]) for o in MID]
    seven = (4, 2, 2, 2, 4, 24)
    return pl.pallas_call(
        mid_kernel,
        out_shape=(
            sd((4, BLK, 768), bf),
            sd((BLK, 768), f32),
            sd((4, 768, 768), bf),
            sd((4, 768, 192), bf),
            sd((8, BLK, 128), bf),
            sd((16, 768), f32),
            sd((*left[0], 24, 384), bf),
            sd((*left[1], 24, 384), bf),
        ),
        in_specs=[anywhere] * 4 + [here],
        out_specs=[anywhere, here, anywhere, here, anywhere, here, here, here],
        scratch_shapes=sum([reducer_scratch(o, 384)[:3] for o in MID], [])
        + [
            vm((8, BLK, 128), bf),
            vm((12, 768, 768), bf),
            vm((8, 768, 128), bf),
            vm((4, BLK, 768), f32),
            vm((4, BLK, 768), f32),
            vm((4, BLK, 768), bf),
            vm((2, 768, 768), bf),
            vm((*seven, 384), bf),
            vm((*seven, 384), bf),
            vm((BLK, 768), bf),
            vm((8, BLK, 128), bf),
            vm((BLK, 768), bf),
            vm((BLK, 768), bf),
            pltpu.SemaphoreType.DMA((40,)),
            pltpu.SemaphoreType.DMA((40,)),
            pltpu.SemaphoreType.DMA((15,)),
            pltpu.SemaphoreType.DMA((2,)),
        ],
        compiler_params=params(cid, 60),
    )(w, cms, xs, cots, vec)


TAIL = ("xyz", "yzx", "zyx")
TAILN = (768, 384, 384)


def tail_kernel(dm, xs, dh1, w, go, gup, vin, n0, n1, R1, R0, R2, V, IG, *refs):
    red, refs = [refs[7 * i : 7 * i + 7] for i in range(3)], refs[21:]
    more, refs = [[None] * 3 + [(n0, n1)[i], *refs[3 * i : 3 * i + 3]] for i in range(2)], refs[6:]
    x, d, wv, ga, gb, igb, igr, acc, vt, vr, ss, rs, ls = refs
    p = Place()
    c = lax.axis_index("ctx")
    core, sib = p.core, p.sib()
    ctx = [{"ctx": (c + k) % 8} for k in range(1, 8)]
    peers = {"x": p.px, "y": p.py, "z": p.pz}
    greet([p.px(k)[0] for k in AXES] + [p.py(k)[0] for k in (1, 3)] + ctx + [sib])
    send = Sender(ss, rs)
    parts = [Reducer(p, send, o, r) for o, r in zip(TAIL, red)]
    parts += [Reducer(p, send, o, r) for o, r in zip(MID, more)]
    parts[0].begin(gup, ls.at[0])
    sw = [send(dm.at[(c + k) % 8], d.at[c], {"ctx": (c + k) % 8}) for k in range(1, 8)]
    swo = pltpu.make_async_copy(dm.at[c], d.at[c], ls.at[1])
    load = pltpu.make_async_copy(w.at[0], wv, ls.at[2])
    swo.start()
    rows = pltpu.make_async_copy(xs.at[p.x], x, ls.at[3])
    rows.start()
    load.start()
    parts[0].first()
    for q in (3, 4):
        parts[q].c2 = parts[q].scatter(parts[q].s1, parts[q].r2, 1)
    rows.wait()
    xt = x[...].astype(f32).T.astype(bf)
    acc[...] = dh1[...]
    swo.wait()
    load.wait()
    for cp in sw:
        cp.wait_recv()
    vt[0, :60] = vin[:60]
    for t in range(4):
        a, b = d[2 * t].astype(f32), d[2 * t + 1].astype(f32)
        pre = jnp.concatenate([a[:, :192], a[:, 192:] + b[:, 192:], b[:, :192]], axis=1)
        sums = jnp.concatenate([down_sum(pre), jnp.zeros((1, 64), f32)], axis=1)
        for k in range(5):
            vt[0, 60 + 5 * t + k : 61 + 5 * t + k] = sums[:, 128 * k : 128 * k + 128]
        pre = pre.astype(bf)
        g = jnp.concatenate([nn(xt, pre), go[t].astype(f32)], axis=1)
        store_pieces(g, t, ga, gb)
        acc[...] += nt(pre, wv[t, :, :576])
    parts[1].begin(ga, ls.at[0])
    parts[2].begin(gb, ls.at[1])
    igb[...] = acc[...].astype(bf)
    igr[p.x] = igb[...]
    ig = [send(igb, igr.at[p.x], p.px(k)[0]) for k in AXES]
    cv = send(vt.at[0], vr.at[0, 0], sib)
    parts[1].first()
    parts[2].first()
    cv.wait_recv()
    vt[1] = vt[0] + vr[0, 0]

    def vsend(i, a):
        return [send(vt.at[i], vr.at[i, j - 1], peers[a](j)[0]) for j in AXES]

    def vsum(i, cs):
        for cp in cs:
            cp.wait_recv()
        return vt[i] + vr[i, 0] + vr[i, 1] + vr[i, 2]

    v1 = vsend(1, "z")
    for q in (3, 4):
        parts[q].third()
    parts[0].second()
    vt[2] = vsum(1, v1)
    v2 = vsend(2, "y")
    for q in (1, 2):
        parts[q].second()
    vt[3] = vsum(2, v2)
    v3 = vsend(3, "x")
    for q in (0, 1, 2):
        parts[q].third()
    V[...] = vsum(3, v3)
    for cp in ig:
        cp.wait_recv()
    IG[...] = igr[...].astype(f32)
    R1[...] = parts[0].result()
    R2[:, :384] = parts[3].result()
    R2[:, 384:] = parts[4].result()
    R0[:, :384] = parts[1].result()
    R0[:, 384:] = parts[2].result()
    for cp in send.all:
        cp.wait_send()


def finale(dm, xs, dh1, w, go, gup, vin, n0, n1, cid):
    vm = pltpu.VMEM
    sd = jax.ShapeDtypeStruct
    anywhere, here = pl.BlockSpec(memory_space=pl.ANY), pl.BlockSpec(memory_space=vm)
    scratch = sum([reducer_scratch(o, n) for o, n in zip(TAIL, TAILN)], [])
    scratch += sum([reducer_scratch(o, 384)[4:] for o in MID], [])
    seven = (4, 2, 2, 2, 4, 24)
    return pl.pallas_call(
        tail_kernel,
        out_shape=(sd((24, 768), f32), sd((24, 768), f32), sd((24, 768), f32), sd((80, 128), f32), sd((4, BLK, 768), f32)),
        in_specs=[anywhere, anywhere, here, anywhere, here, anywhere, here, here, here],
        out_specs=[here] * 5,
        scratch_shapes=scratch
        + [
            vm((BLK, 768), bf),
            vm((8, BLK, 384), bf),
            vm((4, 768, 768), bf),
            vm((*seven, 384), bf),
            vm((*seven, 384), bf),
            vm((BLK, 768), bf),
            vm((4, BLK, 768), bf),
            vm((BLK, 768), f32),
            vm((4, 80, 128), f32),
            vm((4, 3, 80, 128), f32),
            pltpu.SemaphoreType.DMA((64,)),
            pltpu.SemaphoreType.DMA((64,)),
            pltpu.SemaphoreType.DMA((4,)),
        ],
        compiler_params=params(cid, 60),
    )(dm, xs, dh1, w, go, gup.reshape(*seven, 768), vin, n0, n1)


NINE = ((0, 0), (1, 0), (2, 0), (2, 2), (0, 2), (1, 2), (0, 1), (1, 1), (2, 1))
TURN = (0, 2, 1)


def shards(
    layer_input,
    segment_ids,
    proj_weight,
    proj_bias,
    out_weight,
    out_bias,
    first_gain,
    first_shift,
    up_weight,
    up_bias,
    down_weight,
    down_bias,
    second_gain,
    second_shift,
    cotangent,
):
    tp = lax.axis_index("tp")
    out_t = out_weight.T

    def head(h):
        return slice(64 * h, 64 * h + 64)

    p0 = jnp.concatenate([proj_weight[k, :, head(h)] for k, h in NINE] + [out_t[:, head(h)] for h in TURN], axis=1)
    none = jnp.zeros((64,), bf)
    pb = jnp.concatenate([none if k == 1 else proj_bias[k // 2, head(h)] for k, h in NINE] + [none] * 3)
    vec = jnp.concatenate(
        [up_bias, pb, out_bias, down_bias, first_gain, first_shift, second_gain, second_shift, jnp.zeros((3456,), bf)]
    ).reshape(8, 768)
    seg = lax.dynamic_index_in_dim(segment_ids, tp, 0, keepdims=False).reshape(2, 128)
    w, vec, r, docs = front(p0, up_weight, down_weight.T, vec, layer_input, seg, 1)
    w = w.reshape(3, 4, 768, 768)
    cmsg, acc, qa = attend(docs, r)
    layer_output, dh1, gup, go, dc, sums, n0, n1 = middle(w, cmsg, layer_input, cotangent, vec, 2)
    dmsg = unattend(docs, r, dc, acc, qa)
    vin = jnp.concatenate([sums[:6].reshape(36, 128), sums[8:12].reshape(24, 128), jnp.zeros((20, 128), f32)])
    r1, r0, r2, vs, input_grad = finale(dmsg, layer_input, dh1, w, go, gup, vin, n0, n1, 3)
    at = {kh: i for i, kh in enumerate(NINE)}
    proj = jnp.stack([jnp.concatenate([r0[:, head(at[k, h])] for h in range(3)], axis=1) for k in range(3)])
    out_grad = jnp.concatenate([r0[:, head(9 + TURN[h])] for h in range(3)], axis=1).T
    fc = lax.axis_index(("fsdp", "ctx"))
    six = lax.dynamic_index_in_dim(vs[:36].reshape(6, 32, 24), fc, 1, keepdims=False)
    upb = lax.dynamic_index_in_dim(vs[36:60].reshape(4, 768), tp, 0, keepdims=False)
    pbs = lax.dynamic_index_in_dim(vs[60:80].reshape(4, 640), tp, 0, keepdims=False)
    pbg = jnp.stack([jnp.concatenate([pbs[head(at[k, h])] for h in range(3)]) for k in (0, 2)])
    return (
        layer_output,
        input_grad,
        proj,
        pbg,
        out_grad,
        six[0],
        six[2],
        six[3],
        r1,
        upb,
        r2.T,
        six[1],
        six[4],
        six[5],
    )


def solution(mesh):
    placed = (
        P("fsdp", "ctx", None),
        P("fsdp", "ctx"),
        P(None, "fsdp", "tp"),
        P(None, "tp"),
        P("tp", "fsdp"),
        P("fsdp"),
        P("fsdp"),
        P("fsdp"),
        P("fsdp", "tp"),
        P("tp"),
        P("tp", "fsdp"),
        P("fsdp"),
        P("fsdp"),
        P("fsdp"),
        P("fsdp", "ctx", None),
    )
    return jax.shard_map(
        shards,
        mesh=mesh,
        in_specs=placed,
        out_specs=(
            P("fsdp", "ctx", None),
            P("fsdp", "ctx", None),
            P(None, ("fsdp", "ctx"), "tp"),
            P(None, "tp"),
            P("tp", ("fsdp", "ctx")),
            P(("fsdp", "ctx")),
            P(("fsdp", "ctx")),
            P(("fsdp", "ctx")),
            P(("fsdp", "ctx"), "tp"),
            P("tp"),
            P("tp", ("fsdp", "ctx")),
            P(("fsdp", "ctx")),
            P(("fsdp", "ctx")),
            P(("fsdp", "ctx")),
        ),
        check_vma=False,
    )
```

time: 784 us -> 267 us (0.34)
  waiting for transfers between devices: 385 us -> 0 us
  Pallas kernels: 0 us -> 245 us
  matrix products: 160 us -> 0 us
  local copies, waits for them, and re-layouts: 99.4 us -> 20.5 us
  blocking collectives: 58.2 us -> 0 us
  other arithmetic: 50.8 us -> 2.86 us
  between operations: 15.6 us -> 0.97 us
  starting transfers between devices: 9.47 us -> 0 us
    pallas_call x0 -> x5, Pallas kernels: none -> 245 us  [the longest x1 77.8 us: finale(): pl.pallas_call(tail_kernel, out_shape=(sd((24, 768), f32), sd((24, 768),...]
    dot_general x20 -> x0, matrix products: 160 us -> none  [the longest x2 22.9 us: doc_scores(): jnp.einsum('sqhd,skhd->shqk', queries, key_rows, preferred_element_type=j...]
    psum x3 -> x0, waiting for transfers between devices: 147 us -> none  [the longest x1 50.6 us: shards(): lax.psum(norm_part.astype(jnp.bfloat16), 'tp').astype(jnp.float32)]
    all_gather x4 -> x0, waiting for transfers between devices: 137 us -> none  [the longest x2 70.2 us: sent_together(): lax.all_gather(both, axis, axis=dim, tiled=True)]
    unnamed x10 -> x0, waiting for transfers between devices: 94.1 us -> none
    all_gather x2 -> x0, blocking collectives: 58.2 us -> none  [the longest x1 30.1 us: sent_together(): lax.all_gather(both, axis, axis=dim, tiled=True)]
    reshape x17 -> x6, local copies, waits for them, and re-layouts: 38.4 us -> 0.18 us  [the longest x1 0.1 us: shards(): vs[:36].reshape(6, 32, 24)]
    reduce_sum x12 -> x0, other arithmetic: 35.1 us -> none  [the longest x1 12 us: whole_attention(): row_total = jnp.sum(exp_terms, axis=-1, keepdims=True)]
  transfers between devices with their start and end apart: 10 -> 0, of which waited for: 9 -> 0; matrix products, arithmetic and copies ran while one was open for 15% -> 0% of each run, Pallas kernels for 0% -> 0%
where the time goes in v2:
time: 267 us; the launch traced here: 269 us
  Pallas kernels  245 us (92%)
  local copies, waits for them, and re-layouts  20.5 us (8%)
  other arithmetic  2.86 us (1%)
    pallas_call x1, Pallas kernels, finale(): pl.pallas_call(tail_kernel, out_shape=(sd((24, 768), f32), sd((24, 768),...  77.8 us
    pallas_call x1, Pallas kernels, front(): pl.pallas_call(front_kernel, out_shape=(sd((3, 4, 2, 2, 192, 768), bf), s...  71 us
    pallas_call x1, Pallas kernels, middle(): pl.pallas_call(mid_kernel, out_shape=(sd((4, BLK, 768), bf), sd((BLK, 768...  67.3 us
    pallas_call x1, Pallas kernels, unattend(): pl.pallas_call(unattend_kernel, out_shape=jax.ShapeDtypeStruct((8, BLK, 3...  20.2 us
    unnamed x47, local copies, waits for them, and re-layouts  12.6 us
    pallas_call x1, Pallas kernels, attend(): pl.pallas_call(attend_kernel, out_shape=(sd((8, BLK, 128), bf), sd((2, 20...  8.53 us

profile of v2, /device:TPU:1, one launch (start us, length us, event | category | flops | bytes accessed | tf_op | source)
XLA Modules:
  0.0 269.1 jit_solution(7845417066800664620)
XLA Ops:
  0.6 0.0 copy-start
  0.7 0.0 copy-start.13
  0.7 0.0 copy-start.15
  0.7 0.0 copy-start.17
  0.7 0.0 copy-start.18
  0.7 0.0 copy-start.14
  0.7 0.0 copy-start.16
  0.7 0.0 copy-start.19
  0.7 0.0 copy-start.20
  0.7 0.0 copy-start.1
  0.8 1.2 slice_bitcast_fusion
  2.0 1.0 copy.30
  3.0 0.1 fusion.7
  3.1 0.2 concatenate.30.p0
  3.3 0.0 copy-done.13
  3.3 0.1 slice_bitcast_fusion.9
  3.4 0.0 copy-done.15
  3.4 0.0 copy-done.17
  3.4 0.0 copy-done.18
  3.4 0.0 copy-done.14
  3.4 0.0 copy-done.16
  3.5 0.0 copy-done.19
  3.5 0.0 copy-done.20
  3.5 0.1 concatenate.32
  3.6 0.0 copy-done
  3.6 0.0 copy-done.1
  3.7 0.0 copy-start.6
  3.7 1.0 copy-done.6
  4.6 1.0 copy-done.7
  5.6 71.0 %shard_map.254 = (bf16[3,4,2,2,192,768]{5,4,3,2,1,0:T(8,128)(2,1)}, bf16[4,2,2,8,768]{4,3,2,1,0:T(8,128)(2,1)S(1)}, bf16[8,256,384]{2,1,0:T(8,128)(2,1)S(1)}, s32[8,2,128]{2,1,0:T(2,128)S(1)}) custom-call(bf16[192,768]{1,0:T(8,128)(2,1)S(1)} %concatenate.30.p0, bf16[192,768]{1,0:T(8,128)(2,1)S(1)} %copy-done.6, bf16[192,768]{1,0:T(8,128)(2,1)S(1)} %bitcast.70, ...), custom_call_target="tpu_custom_call" | custom-call | tf_op jit(solution)/shard_map/pallas_call | solution.py:250
  76.6 0.0 copy-start.8
  76.6 8.5 %shard_map.255 = (bf16[8,256,128]{2,1,0:T(8,128)(2,1)S(1)}, f32[2,2048,128]{2,1,0:T(8,128)S(1)}, bf16[2,2048,128]{2,1,0:T(8,128)(2,1)S(1)}) custom-call(s32[8,2,128]{2,1,0:T(2,128)S(1)} %get-tuple-element.35.edge.docs, s32[8,2,128]{2,1,0:T(2,128)S(1)} %get-tuple-element.35.edge.docs, bf16[8,256,384]{2,1,0:T(8,128)(2,1)S(1)} %get-tuple-element.36.r), custom_call_target="tpu_custom_call" | custom-call | tf_op jit(solution)/shard_map/pallas_call | solution.py:391
  85.1 0.0 copy-start.3
  85.1 1.3 copy-done.3
  86.5 0.8 copy-done.4
  87.2 67.3 %shard_map.256 = (bf16[4,256,768]{2,1,0:T(8,128)(2,1)}, f32[256,768]{1,0:T(8,128)}, bf16[4,768,768]{2,1,0:T(8,128)(2,1)}, bf16[4,768,192]{2,1,0:T(8,128)(2,1)}, ...) custom-call(bf16[3,4,768,768]{3,2,1,0:T(8,128)(2,1)} %bitcast.72, ...), custom_call_target="tpu_custom_call" | custom-call | tf_op jit(solution)/shard_map/pallas_call | solution.py:686
  154.5 0.7 slice.183
  155.3 0.7 slice.184
  156.1 0.1 pad.25.clone
  156.1 0.7 maximum_maximum_fusion.vin
  156.8 1.0 copy-done.5
  157.9 20.2 %shard_map.257.dm = bf16[8,256,384]{2,1,0:T(8,128)(2,1)S(1)} custom-call(s32[8,2,128]{2,1,0:T(2,128)S(1)} %get-tuple-element.35.edge.docs, s32[8,2,128]{2,1,0:T(2,128)S(1)} %get-tuple-element.35.edge.docs, bf16[8,256,384]{2,1,0:T(8,128)(2,1)S(1)} %get-tuple-element.36.r, bf16[8,256,128]{2,1,0:T(8,128)(2,1)S(1)} %copy-done.5, f32[2,2048,128]{2,1,0:T(8,128)} %copy-done.3, ...), custom_call_target="tpu_custom_call" | custom-call | tf_op jit(solution)/shard_map/pallas_call | solution.py:459
  178.1 0.0 copy-start.2
  178.1 1.1 copy-done.2
  179.2 77.8 %shard_map.258 = (f32[24,768]{1,0:T(8,128)}, f32[24,768]{1,0:T(8,128)}, f32[24,768]{1,0:T(8,128)}, f32[80,128]{1,0:T(8,128)}, f32[4,256,768]{2,1,0:T(8,128)}) custom-call(bf16[8,256,384]{2,1,0:T(8,128)(2,1)} %copy-done.2, bf16[4,256,768]{2,1,0:T(8,128)(2,1)} %xs.5, f32[256,768]{1,0:T(8,128)} %get-tuple-element.43.dh1, bf16[3,4,768,768]{3,2,1,0:T(8,128)(2,1)} %bitcast.73, ...), custom_call_target="tpu_custom_call" | custom-call | tf_op jit(solution)/shard_map/pallas_call | solution.py:821
  257.1 0.9 fusion.8
  258.0 0.7 maximum_bitcast_fusion.3
  258.7 0.7 slice.194
  259.4 0.1 fusion.1
  259.5 0.1 pad_maximum_fusion.2
  259.6 0.6 pad_maximum_fusion.1
  260.2 0.1 maximum_bitcast_fusion
  260.3 0.1 maximum_bitcast_fusion.2
  260.4 0.6 pad_maximum_fusion
  261.0 0.7 slice.210
  261.7 0.1 reshape.81
  261.8 0.5 fusion
  262.4 0.7 slice.214
  263.1 0.6 dynamic-slice_reduce_fusion
  263.8 1.1 copy.35
  264.9 1.3 copy-done.9
  266.2 1.7 copy.36
  267.9 0.6 copy.37
  268.5 0.6 copy.38
  (21 shorter events, 0.1 us)
Async XLA Ops:
  0.6 3.0 %copy-start = (s32[4,256]{1,0:T(4,128)S(1)}, s32[4,256]{1,0:T(4,128)}, u32[]{:S(2)}) copy-start(s32[4,256]{1,0:T(4,128)} %param.16) | copy-start | bytes 12292
  0.7 2.6 copy-start.13
  0.7 2.7 %copy-start.15 = (bf16[192]{0:T(256)(128)(2,1)S(1)}, bf16[192]{0:T(256)(128)(2,1)}, u32[]{:S(2)}) copy-start(bf16[192]{0:T(256)(128)(2,1)} %param.20) | copy-start | bytes 1156
  0.7 2.7 %copy-start.17 = (bf16[192]{0:T(256)(128)(2,1)S(1)}, bf16[192]{0:T(256)(128)(2,1)}, u32[]{:S(2)}) copy-start(bf16[192]{0:T(256)(128)(2,1)} %param.21) | copy-start | bytes 1156
  0.7 2.7 %copy-start.18 = (bf16[192]{0:T(256)(128)(2,1)S(1)}, bf16[192]{0:T(256)(128)(2,1)}, u32[]{:S(2)}) copy-start(bf16[192]{0:T(256)(128)(2,1)} %param.22) | copy-start | bytes 1156
  0.7 2.7 %copy-start.14 = (bf16[768]{0:T(1024)(128)(2,1)S(1)}, bf16[768]{0:T(1024)(128)(2,1)}, u32[]{:S(2)}) copy-start(bf16[768]{0:T(1024)(128)(2,1)} %param.24) | copy-start | bytes 4612
  0.7 2.7 %copy-start.16 = (bf16[192]{0:T(256)(128)(2,1)S(1)}, bf16[192]{0:T(256)(128)(2,1)}, u32[]{:S(2)}) copy-start(bf16[192]{0:T(256)(128)(2,1)} %param.26) | copy-start | bytes 1156
  0.7 2.7 %copy-start.19 = (bf16[192]{0:T(256)(128)(2,1)S(1)}, bf16[192]{0:T(256)(128)(2,1)}, u32[]{:S(2)}) copy-start(bf16[192]{0:T(256)(128)(2,1)} %param.27) | copy-start | bytes 1156
  0.7 2.7 %copy-start.20 = (bf16[192]{0:T(256)(128)(2,1)S(1)}, bf16[192]{0:T(256)(128)(2,1)}, u32[]{:S(2)}) copy-start(bf16[192]{0:T(256)(128)(2,1)} %param.28) | copy-start | bytes 1156
  0.7 2.9 %copy-start.1 = (bf16[4,256,768]{2,1,0:T(8,128)(2,1)S(1)}, bf16[4,256,768]{2,1,0:T(8,128)(2,1)}, u32[]{:S(2)}) copy-start(bf16[4,256,768]{2,1,0:T(8,128)(2,1)} %xs.5) | copy-start | bytes 4718596
  3.7 1.0 copy-start.6
  4.6 1.0 copy-start.7
  76.6 8.5 %copy-start.8 = (bf16[4,2,2,8,768]{4,3,2,1,0:T(8,128)(2,1)}, bf16[4,2,2,8,768]{4,3,2,1,0:T(8,128)(2,1)S(1)}, u32[]{:S(2)}) copy-start(bf16[4,2,2,8,768]{4,3,2,1,0:T(8,128)(2,1)S(1)} %get-tuple-element.38.vec) | copy-start | bytes 589828
  85.1 1.3 copy-start.3
  86.5 0.8 copy-start.4
  156.8 1.0 copy-start.5
  178.1 1.1 copy-start.2
  179.2 84.5 %copy-start.10 = (bf16[4,256,768]{2,1,0:T(8,128)(2,1)S(1)}, bf16[4,256,768]{2,1,0:T(8,128)(2,1)}, u32[]{:S(2)}) copy-start(bf16[4,256,768]{2,1,0:T(8,128)(2,1)} %get-tuple-element.114) | copy-start | bytes 4718596
  263.7 2.5 copy-start.9
  266.2 1.7 copy-start.12
  266.2 2.3 copy-start.11

commit v3 on v2

--- a/solution.py
+++ b/solution.py
@@ -65,15 +65,26 @@
 
 
 def total(dst, first, others, shape):
-    count = math.prod(shape)
-
-    @pl.loop(0, count)
-    def _(i):
-        at = split_index(i, shape)
-        a = first[at].astype(f32)
-        for o in others:
-            a = a + o[at].astype(f32)
-        dst[at] = a.astype(dst.dtype)
+    outer = shape[: max(0, len(shape) - 2)] if len(shape) != 2 or shape == (4, 4) else ()
+    outer = shape[:1] if shape == (4, 4) else outer
+
+    def block(at):
+        at = at + (Ellipsis,)
+        if len(others) == 1:
+            dst[at] = first[at] + others[0][at]
+        else:
+            a = first[at].astype(f32)
+            for o in others:
+                a = a + o[at].astype(f32)
+            dst[at] = a.astype(dst.dtype)
+
+    if outer:
+
+        @pl.loop(0, math.prod(outer))
+        def _(i):
+            block(split_index(i, outer))
+    else:
+        block(())
 
 
 SQ = HEAD_DIM ** -0.5
@@ -91,6 +102,16 @@
 
 def params(cid=None, mb=48):
     return pltpu.CompilerParams(collective_id=cid, has_side_effects=cid is not None, vmem_limit_bytes=mb << 20)
+
+
+NINE = ((0, 0), (1, 0), (2, 0), (2, 2), (0, 2), (1, 2), (0, 1), (1, 1), (2, 1))
+AT = {kh: i for i, kh in enumerate(NINE)}
+TURN = (0, 2, 1)
+TAILMB, MIDMB, FRONTMB = 48, 50, 48
+
+
+def head(h):
+    return slice(64 * h, 64 * h + 64)
 
 
 class Sender:
@@ -218,7 +239,9 @@
 
     @pl.loop(0, 4)
     def _(t):
-        b = V[t, 0, 0, 1:2].astype(f32)
+        qv = V[t, 0, 0].astype(f32)
+        b = [jnp.zeros((1, 64), f32) if k == 1 else qv[6 + k // 2 : 7 + k // 2, head(h)] for k, h in NINE]
+        b = jnp.concatenate(b + [jnp.zeros((1, 192), f32)], axis=1)
         r = (nn(x[...], po[t].reshape(768, 768)) + b).astype(bf)
         m[2 * t] = r[:, :384]
         m[2 * t + 1] = jnp.concatenate([r[:, 384:576], r[:, 192:384]], axis=1)
@@ -251,11 +274,11 @@
         front_kernel,
         out_shape=(
             sd((3, 4, 2, 2, 192, 768), bf),
-            sd((4, 2, 2, 8, 768), bf),
+            sd((4, 2, 2, 16, 192), bf),
             sd((8, BLK, 384), bf),
             sd((8, 2, 128), jnp.int32),
         ),
-        in_specs=[anywhere] * 6,
+        in_specs=[here] * 3 + [anywhere] * 3,
         out_specs=[anywhere, here, anywhere, anywhere],
         scratch_shapes=[
             vm((4, 2, 2, 192, 768), bf),
@@ -369,11 +392,10 @@
 
     @pl.loop(0, count)
     def _(n):
-        got = []
-        for u in range(FWD):
-            h, at, to, _ = triple(lst[n * FWD + u])
-            p = jnp.exp(nn(qa[h, at], kt[h, :, to])).astype(bf)
-            got.append((h, at, nn(p, va[h, to])))
+        tr = [triple(lst[n * FWD + u]) for u in range(FWD)]
+        ps = [nn(qa[h, at], kt[h, :, to]) for h, at, to, _ in tr]
+        ps = [jnp.exp(p).astype(bf) for p in ps]
+        got = [(h, at, nn(p, va[h, to])) for p, (h, at, to, _) in zip(ps, tr)]
         for h, at, o in got:
             acc[h, at] += o
 
@@ -433,13 +455,15 @@
 
     @pl.loop(0, count)
     def _(n):
-        got = []
-        for u in range(BWD):
-            h, at, to, _ = triple(lst[n * BWD + u])
-            p = jnp.exp(nt(ka[h, to], qa[h, at]))
-            ds = (p * nt(va[h, to], ga[h, at])).astype(bf)
-            kv = nn(p.astype(bf), gz[h, at]) + nn(ds, qz[h, at])
-            got.append((h, at, to, kv, nn(kt[h, :, to], ds)))
+        tr = [triple(lst[n * BWD + u]) for u in range(BWD)]
+        ps = [nt(ka[h, to], qa[h, at]) for h, at, to, _ in tr]
+        dp = [nt(va[h, to], ga[h, at]) for h, at, to, _ in tr]
+        ps = [jnp.exp(p) for p in ps]
+        ds = [(p * d).astype(bf) for p, d in zip(ps, dp)]
+        ps = [p.astype(bf) for p in ps]
+        kv = [nn(p, gz[h, at]) + nn(d, qz[h, at]) for p, d, (h, at, to, _) in zip(ps, ds, tr)]
+        dq = [nn(kt[h, :, to], d) for d, (h, at, to, _) in zip(ds, tr)]
+        got = [(h, at, to, a, b) for a, b, (h, at, to, _) in zip(kv, dq, tr)]
         for h, at, to, kv, dq in got:
             dkv[h, to] += kv
             dqt[h, :, at] += dq
@@ -484,12 +508,15 @@
         self.here = {"x": p.x, "y": (p.yl, p.yh), "z": p.z}
         self.left = [[d for d in "xyz" if d not in order[:n]] for n in range(3)]
 
-    def begin(self, src, sem=None):
-        self.c0 = self.send(src.at[:, :, 1 - self.p.core], self.cor, self.p.sib())
-        self.own = None
-        if sem is not None:
-            self.own = pltpu.make_async_copy(src.at[:, :, self.p.core], self.acc, sem)
-            self.own.start()
+    def begin(self, src, sem):
+        self.c0 = [self.send(src.at[:, :, 1 - self.p.core], self.cor, self.p.sib())]
+        self.own = pltpu.make_async_copy(src.at[:, :, self.p.core], self.acc, sem)
+        self.own.start()
+        self.mine = self.acc
+
+    def begin_at(self, src, t):
+        self.c0 = ([] if t == 0 else self.c0) + [self.send(src.at[t, :, 1 - self.p.core], self.cor.at[t], self.p.sib())]
+        self.own, self.mine = None, src.at[:, :, self.p.core]
 
     def scatter(self, src, into, n):
         a = self.order[n]
@@ -498,10 +525,11 @@
         ]
 
     def first(self):
-        self.c0.wait_recv()
+        for c in self.c0:
+            c.wait_recv()
         if self.own is not None:
             self.own.wait()
-        total(self.acc, self.acc, [self.cor], shape_of("xyz"))
+        total(self.acc, self.mine, [self.cor], shape_of("xyz"))
         self.c1 = self.scatter(self.acc, self.r1, 0)
 
     def gathered(self, copies, out, src, got, n):
@@ -571,6 +599,11 @@
     ctx = [{"ctx": (c + k) % 8} for k in range(1, 8)]
     greet([p.px(k)[0] for k in AXES] + [p.py(k)[0] for k in (1, 3)] + ctx + [p.sib()])
     send = Sender(ss, rs)
+
+    def put(i, row):
+        for k in range(6):
+            sums[6 * i + k : 6 * i + k + 1] = row[:, 128 * k : 128 * k + 128]
+
     sw = [send(cms.at[(c + k) % 8], cm.at[c], {"ctx": (c + k) % 8}) for k in range(1, 8)]
     swo = pltpu.make_async_copy(cms.at[c], cm.at[c], ls.at[12])
     swo.start()
@@ -584,10 +617,7 @@
     for cp in ins:
         cp.start()
     fours = [vec[0, f // 2, f % 2].astype(f32) for f in range(4)]
-    pv = [
-        jnp.concatenate([f[2 + i // 4 : 3 + i // 4, 192 * (i % 4) : 192 * (i % 4) + 192] for f in fours], axis=1)
-        for i in range(6)
-    ]
+    pv = [jnp.concatenate([f[i : i + 1] for f in fours], axis=1) for i in range(6)]
     for t in range(4):
         loads[t].wait()
         o = wv[t, :, 576:768]
@@ -608,7 +638,7 @@
     ffn = jnp.zeros((BLK, 768), f32)
     for t in range(4):
         loads[4 + t].wait()
-        z = nn(y1b, wv[4 + t]) + vec[t, 0, 0, 0:1].astype(f32)
+        z = nn(y1b, wv[4 + t]) + jnp.concatenate([vec[t, 0, 0, 8 + k : 9 + k].astype(f32) for k in range(4)], axis=1)
         e = 0.5 * (1.0 + lax.erf(z * (2.0**-0.5)))
         zs[t] = z
         cdf[t] = e
@@ -622,25 +652,25 @@
     loo = pltpu.make_async_copy(lob, LO.at[p.x], ls.at[12])
     loo.start()
     g = cot[...].astype(f32)
-    sums[4:5] = down_sum(g * xh2)
-    sums[5:6] = down_sum(g)
+    put(4, down_sum(g * xh2))
+    put(5, down_sum(g))
     dh2 = norm_back(g, xh2, s2, pv[4])
-    sums[1:2] = down_sum(dh2)
+    put(1, down_sum(dh2))
     dh2b = dh2.astype(bf)
     dh2t = dh2.T.astype(bf)
     y1t = y1.T.astype(bf)
+    parts = [Reducer(p, send, o, r) for o, r in zip(MID, red)]
     for t in range(4):
         store_pieces(nn(dh2t, act[t]), t, ga, gb)
-    parts = [Reducer(p, send, o, r) for o, r in zip(MID, red)]
-    parts[0].begin(ga, ls.at[0])
-    parts[1].begin(gb, ls.at[1])
+        parts[0].begin_at(ga, t)
+        parts[1].begin_at(gb, t)
     dy1 = dh2
     outs = []
     for t in range(4):
         da = nn(dh2b, wv[8 + t]).astype(bf).astype(f32)
         z = zs[t]
         dz = da * (cdf[t] + z * (jnp.exp(-0.5 * z * z) * ((2.0 * math.pi) ** -0.5)))
-        sums[8 + t : 9 + t] = down_sum(dz)
+        put(6 + t, down_sum(dz))
         dzb = dz.astype(bf)
         if t >= 2:
             outs[t - 2].wait()
@@ -652,11 +682,11 @@
         if t == 0:
             for part in parts:
                 part.first()
-    sums[2:3] = down_sum(dy1 * xh1)
-    sums[3:4] = down_sum(dy1)
+    put(2, down_sum(dy1 * xh1))
+    put(3, down_sum(dy1))
     d1 = norm_back(dy1, xh1, s1, pv[2])
     dh1[...] = d1
-    sums[0:1] = down_sum(d1)
+    put(0, down_sum(d1))
     d1b = d1.astype(bf)
     d1t = d1.T.astype(bf)
     for j in range(8):
@@ -691,7 +721,7 @@
             sd((4, 768, 768), bf),
             sd((4, 768, 192), bf),
             sd((8, BLK, 128), bf),
-            sd((16, 768), f32),
+            sd((60, 128), f32),
             sd((*left[0], 24, 384), bf),
             sd((*left[1], 24, 384), bf),
         ),
@@ -717,7 +747,7 @@
             pltpu.SemaphoreType.DMA((15,)),
             pltpu.SemaphoreType.DMA((2,)),
         ],
-        compiler_params=params(cid, 60),
+        compiler_params=params(cid, MIDMB),
     )(w, cms, xs, cots, vec)
 
 
@@ -728,7 +758,7 @@
 def tail_kernel(dm, xs, dh1, w, go, gup, vin, n0, n1, R1, R0, R2, V, IG, *refs):
     red, refs = [refs[7 * i : 7 * i + 7] for i in range(3)], refs[21:]
     more, refs = [[None] * 3 + [(n0, n1)[i], *refs[3 * i : 3 * i + 3]] for i in range(2)], refs[6:]
-    x, d, wv, ga, gb, igb, igr, acc, vt, vr, ss, rs, ls = refs
+    x, d, wv, ga, gb, igb, acc, vt, vr, ss, rs, ls = refs
     p = Place()
     c = lax.axis_index("ctx")
     core, sib = p.core, p.sib()
@@ -756,7 +786,7 @@
     load.wait()
     for cp in sw:
         cp.wait_recv()
-    vt[0, :60] = vin[:60]
+    vt[0, :60] = vin[...]
     for t in range(4):
         a, b = d[2 * t].astype(f32), d[2 * t + 1].astype(f32)
         pre = jnp.concatenate([a[:, :192], a[:, 192:] + b[:, 192:], b[:, :192]], axis=1)
@@ -766,12 +796,12 @@
         pre = pre.astype(bf)
         g = jnp.concatenate([nn(xt, pre), go[t].astype(f32)], axis=1)
         store_pieces(g, t, ga, gb)
+        parts[1].begin_at(ga, t)
+        parts[2].begin_at(gb, t)
         acc[...] += nt(pre, wv[t, :, :576])
-    parts[1].begin(ga, ls.at[0])
-    parts[2].begin(gb, ls.at[1])
     igb[...] = acc[...].astype(bf)
-    igr[p.x] = igb[...]
-    ig = [send(igb, igr.at[p.x], p.px(k)[0]) for k in AXES]
+    IG[p.x] = igb[...]
+    ig = [send(igb, IG.at[p.x], p.px(k)[0]) for k in AXES]
     cv = send(vt.at[0], vr.at[0, 0], sib)
     parts[1].first()
     parts[2].first()
@@ -801,7 +831,6 @@
     V[...] = vsum(3, v3)
     for cp in ig:
         cp.wait_recv()
-    IG[...] = igr[...].astype(f32)
     R1[...] = parts[0].result()
     R2[:, :384] = parts[3].result()
     R2[:, 384:] = parts[4].result()
@@ -820,7 +849,7 @@
     seven = (4, 2, 2, 2, 4, 24)
     return pl.pallas_call(
         tail_kernel,
-        out_shape=(sd((24, 768), f32), sd((24, 768), f32), sd((24, 768), f32), sd((80, 128), f32), sd((4, BLK, 768), f32)),
+        out_shape=(sd((24, 768), f32), sd((24, 768), f32), sd((24, 768), f32), sd((80, 128), f32), sd((4, BLK, 768), bf)),
         in_specs=[anywhere, anywhere, here, anywhere, here, anywhere, here, here, here],
         out_specs=[here] * 5,
         scratch_shapes=scratch
@@ -831,20 +860,46 @@
             vm((*seven, 384), bf),
             vm((*seven, 384), bf),
             vm((BLK, 768), bf),
-            vm((4, BLK, 768), bf),
             vm((BLK, 768), f32),
             vm((4, 80, 128), f32),
             vm((4, 3, 80, 128), f32),
-            pltpu.SemaphoreType.DMA((64,)),
-            pltpu.SemaphoreType.DMA((64,)),
+            pltpu.SemaphoreType.DMA((80,)),
+            pltpu.SemaphoreType.DMA((80,)),
             pltpu.SemaphoreType.DMA((4,)),
         ],
-        compiler_params=params(cid, 60),
+        compiler_params=params(cid, TAILMB),
     )(dm, xs, dh1, w, go, gup.reshape(*seven, 768), vin, n0, n1)
 
 
-NINE = ((0, 0), (1, 0), (2, 0), (2, 2), (0, 2), (1, 2), (0, 1), (1, 1), (2, 1))
-TURN = (0, 2, 1)
+def finish_kernel(r1, r0, r2, v, g, R1, PG, OG, R2, PB, UB, B0, B1, B2, B3, B4, B5, IG):
+    x, fc = lax.axis_index("tp"), lax.axis_index("fsdp") * 8 + lax.axis_index("ctx")
+    IG[...] = g[...].astype(f32)
+    R1[...] = r1[...]
+    for i, out in enumerate((B0, B1, B2, B3, B4, B5)):
+        row = jnp.concatenate([v[6 * i + k : 6 * i + k + 1] for k in range(6)], axis=1)
+        row = pltpu.roll(jnp.broadcast_to(row, (8, 768)), (768 - 24 * fc) % 768, 1)
+        out[...] = row[:1, :24]
+    UB[...] = jnp.concatenate([v[pl.ds(36 + 6 * x + k, 1)] for k in range(6)], axis=1)
+    b = jnp.concatenate([v[pl.ds(60 + 5 * x + k, 1)] for k in range(5)], axis=1)
+    PB[...] = jnp.concatenate([jnp.concatenate([b[:, head(AT[k, h])] for h in range(3)], axis=1) for k in (0, 2)], axis=0)
+    R2[...] = r2[...].T
+    p = r0[...]
+    for k in range(3):
+        PG[k] = jnp.concatenate([p[:, head(AT[k, h])] for h in range(3)], axis=1)
+    OG[...] = jnp.concatenate([p[:, head(9 + TURN[h])] for h in range(3)], axis=1).T
+
+
+def finish(*args):
+    sd = jax.ShapeDtypeStruct
+    here = pl.BlockSpec(memory_space=pltpu.VMEM)
+    shapes = [(24, 768), (3, 24, 192), (192, 24), (768, 24), (2, 192), (1, 768), *[(1, 24)] * 6, (4, BLK, 768)]
+    return pl.pallas_call(
+        finish_kernel,
+        out_shape=tuple(sd(s, f32) for s in shapes),
+        in_specs=[here] * 5,
+        out_specs=[here] * 13,
+        compiler_params=params(mb=24),
+    )(*args)
 
 
 def shards(
@@ -867,47 +922,22 @@
     tp = lax.axis_index("tp")
     out_t = out_weight.T
 
-    def head(h):
-        return slice(64 * h, 64 * h + 64)
-
     p0 = jnp.concatenate([proj_weight[k, :, head(h)] for k, h in NINE] + [out_t[:, head(h)] for h in TURN], axis=1)
-    none = jnp.zeros((64,), bf)
-    pb = jnp.concatenate([none if k == 1 else proj_bias[k // 2, head(h)] for k, h in NINE] + [none] * 3)
-    vec = jnp.concatenate(
-        [up_bias, pb, out_bias, down_bias, first_gain, first_shift, second_gain, second_shift, jnp.zeros((3456,), bf)]
-    ).reshape(8, 768)
+    rows = [out_bias, down_bias, first_gain, first_shift, second_gain, second_shift, proj_bias[0], proj_bias[1]]
+    row = lax.broadcasted_iota(jnp.int32, (16, 192), 0)
+    vec = jnp.zeros((16, 192), bf)
+    for i, v in enumerate(rows + [up_bias[192 * k : 192 * k + 192] for k in range(4)]):
+        vec = jnp.where(row == i, v[None], vec)
     seg = lax.dynamic_index_in_dim(segment_ids, tp, 0, keepdims=False).reshape(2, 128)
     w, vec, r, docs = front(p0, up_weight, down_weight.T, vec, layer_input, seg, 1)
     w = w.reshape(3, 4, 768, 768)
     cmsg, acc, qa = attend(docs, r)
     layer_output, dh1, gup, go, dc, sums, n0, n1 = middle(w, cmsg, layer_input, cotangent, vec, 2)
     dmsg = unattend(docs, r, dc, acc, qa)
-    vin = jnp.concatenate([sums[:6].reshape(36, 128), sums[8:12].reshape(24, 128), jnp.zeros((20, 128), f32)])
-    r1, r0, r2, vs, input_grad = finale(dmsg, layer_input, dh1, w, go, gup, vin, n0, n1, 3)
-    at = {kh: i for i, kh in enumerate(NINE)}
-    proj = jnp.stack([jnp.concatenate([r0[:, head(at[k, h])] for h in range(3)], axis=1) for k in range(3)])
-    out_grad = jnp.concatenate([r0[:, head(9 + TURN[h])] for h in range(3)], axis=1).T
-    fc = lax.axis_index(("fsdp", "ctx"))
-    six = lax.dynamic_index_in_dim(vs[:36].reshape(6, 32, 24), fc, 1, keepdims=False)
-    upb = lax.dynamic_index_in_dim(vs[36:60].reshape(4, 768), tp, 0, keepdims=False)
-    pbs = lax.dynamic_index_in_dim(vs[60:80].reshape(4, 640), tp, 0, keepdims=False)
-    pbg = jnp.stack([jnp.concatenate([pbs[head(at[k, h])] for h in range(3)]) for k in (0, 2)])
-    return (
-        layer_output,
-        input_grad,
-        proj,
-        pbg,
-        out_grad,
-        six[0],
-        six[2],
-        six[3],
-        r1,
-        upb,
-        r2.T,
-        six[1],
-        six[4],
-        six[5],
-    )
+    done = finale(dmsg, layer_input, dh1, w, go, gup, sums, n0, n1, 3)
+    r1, proj, out_grad, r2, pb, ub, b0, b1, b2, b3, b4, b5, input_grad = finish(*done)
+    ob, db, g1, s1, g2, s2 = [b.reshape(24) for b in (b0, b1, b2, b3, b4, b5)]
+    return (layer_output, input_grad, proj, pb, out_grad, ob, g1, s1, r1, ub.reshape(768), r2, db, g2, s2)
 
 
 def solution(mesh):

time: 267 us -> 236 us (0.88); the launches traced: 269 us -> 235 us
  Pallas kernels: 245 us -> 224 us
  local copies, waits for them, and re-layouts: 20.5 us -> 8.67 us
    pallas_call x1, Pallas kernels: 77.8 us -> 62.9 us  [finale(): pl.pallas_call(tail_kernel, out_shape=(sd((24, 768), f32), sd((24, 768),...]
    pallas_call x1, Pallas kernels: 67.3 us -> 58.6 us  [middle(): pl.pallas_call(mid_kernel, out_shape=(sd((4, BLK, 768), bf), sd((BLK, 768...]
    unnamed x47 -> x16, local copies, waits for them, and re-layouts: 12.6 us -> 5.57 us
    slice x7 -> x2, local copies, waits for them, and re-layouts: 4.67 us -> 1.68 us  [the longest x1 0.91 us: shards(): up_bias[192 * k:192 * k + 192]]
where the time goes in v3:
time: 236 us; the launch traced here: 235 us
  Pallas kernels  224 us (95%)
  local copies, waits for them, and re-layouts  8.67 us (4%)
    pallas_call x1, Pallas kernels, front(): pl.pallas_call(front_kernel, out_shape=(sd((3, 4, 2, 2, 192, 768), bf), s...  70.9 us
    pallas_call x1, Pallas kernels, finale(): pl.pallas_call(tail_kernel, out_shape=(sd((24, 768), f32), sd((24, 768),...  62.9 us
    pallas_call x1, Pallas kernels, middle(): pl.pallas_call(mid_kernel, out_shape=(sd((4, BLK, 768), bf), sd((BLK, 768...  58.6 us
    pallas_call x1, Pallas kernels, unattend(): pl.pallas_call(unattend_kernel, out_shape=jax.ShapeDtypeStruct((8, BLK, 3...  19.6 us
    pallas_call x1, Pallas kernels, attend(): pl.pallas_call(attend_kernel, out_shape=(sd((8, BLK, 128), bf), sd((2, 20...  9.59 us
    unnamed x16, local copies, waits for them, and re-layouts  5.57 us

profile of v3, /device:TPU:1, one launch (start us, length us, event | category | flops | bytes accessed | tf_op | source)
XLA Modules:
  0.0 234.7 jit_solution(1400120709331056630)
XLA Ops:
  0.6 0.0 copy-start
  0.7 0.0 copy-start.1
  0.7 0.0 copy-start.4
  0.7 0.0 copy-start.3
  0.7 0.6 copy-done
  1.3 0.8 slice_reduce_fusion.1
  2.2 0.9 fusion.1
  3.1 0.8 select_select_fusion.vec
  3.9 1.0 copy.29
  4.9 0.1 fusion
  5.0 1.1 slice_bitcast_fusion
  6.1 0.2 concatenate.3.p0
  6.4 0.0 copy-done.1
  6.4 0.0 copy-done.4
  6.4 0.0 copy-done.3
  6.4 70.9 %shard_map.254 = (bf16[3,4,2,2,192,768]{5,4,3,2,1,0:T(8,128)(2,1)}, bf16[4,2,2,16,192]{4,3,2,1,0:T(8,128)(2,1)S(1)}, bf16[8,256,384]{2,1,0:T(8,128)(2,1)S(1)}, s32[8,2,128]{2,1,0:T(2,128)S(1)}) custom-call(bf16[192,768]{1,0:T(8,128)(2,1)S(1)} %concatenate.3.p0, bf16[192,768]{1,0:T(8,128)(2,1)S(1)} %copy-done.3, bf16[192,768]{1,0:T(8,128)(2,1)S(1)} %bitcast.29, ...), custom_call_target="tpu_custom_call" | custom-call | tf_op jit(solution)/shard_map/pallas_call | solution.py:273
  77.3 9.6 %shard_map.255 = (bf16[8,256,128]{2,1,0:T(8,128)(2,1)S(1)}, f32[2,2048,128]{2,1,0:T(8,128)S(1)}, bf16[2,2048,128]{2,1,0:T(8,128)(2,1)S(1)}) custom-call(s32[8,2,128]{2,1,0:T(2,128)S(1)} %get-tuple-element.48.edge.docs, s32[8,2,128]{2,1,0:T(2,128)S(1)} %get-tuple-element.48.edge.docs, bf16[8,256,384]{2,1,0:T(8,128)(2,1)S(1)} %get-tuple-element.49.r), custom_call_target="tpu_custom_call" | custom-call | tf_op jit(solution)/shard_map/pallas_call | solution.py:413
  86.9 0.0 copy-start.2
  86.9 1.3 copy-done.2
  88.2 58.6 %shard_map.256 = (bf16[4,256,768]{2,1,0:T(8,128)(2,1)}, f32[256,768]{1,0:T(8,128)S(1)}, bf16[4,768,768]{2,1,0:T(8,128)(2,1)}, bf16[4,768,192]{2,1,0:T(8,128)(2,1...) custom-call(bf16[3,4,768,768]{3,2,1,0:T(8,128)(2,1)} %bitcast.31, ...), custom_call_target="tpu_custom_call" | custom-call | tf_op jit(solution)/shard_map/pallas_call | solution.py:716
  146.9 19.6 %shard_map.257.dm = bf16[8,256,384]{2,1,0:T(8,128)(2,1)S(1)} custom-call(s32[8,2,128]{2,1,0:T(2,128)S(1)} %get-tuple-element.48.edge.docs, s32[8,2,128]{2,1,0:T(2,128)S(1)} %get-tuple-element.48.edge.docs, bf16[8,256,384]{2,1,0:T(8,128)(2,1)S(1)} %get-tuple-element.49.r, bf16[8,256,128]{2,1,0:T(8,128)(2,1)S(1)} %get-tuple-element.53.dc, ...), custom_call_target="tpu_custom_call" | custom-call | tf_op jit(solution)/shard_map/pallas_call | solution.py:483
  166.5 62.9 %shard_map.258 = (f32[24,768]{1,0:T(8,128)S(1)}, f32[24,768]{1,0:T(8,128)S(1)}, f32[24,768]{1,0:T(8,128)S(1)}, f32[80,128]{1,0:T(8,128)S(1)}, bf16[4,256,768]{2,1,0:T(8,128)(2,1)S(1)}) custom-call(bf16[8,256,384]{2,1,0:T(8,128)(2,1)S(1)} %shard_map.257.dm, bf16[4,256,768]{2,1,0:T(8,128)(2,1)} %xs.5, f32[256,768]{1,0:T(8,128)S(1)} %get-tuple-element.56.dh1, ...), custom_call_target="tpu_custom_call" | custom-call | tf_op jit(solution)/shard_map/pallas_call | solution.py:850
  229.4 0.0 copy-start.5
  229.4 2.1 shard_map.259
  231.5 0.6 reduce.2
  232.1 0.7 copy.30
  232.8 0.8 copy.31
  233.6 0.0 copy-done.5
  233.6 1.1 copy.33
  (7 shorter events, 0.0 us)
Async XLA Ops:
  0.6 0.7 copy-start
  0.7 5.7 %copy-start.1 = (bf16[4,256,768]{2,1,0:T(8,128)(2,1)S(1)}, bf16[4,256,768]{2,1,0:T(8,128)(2,1)}, u32[]{:S(2)}) copy-start(bf16[4,256,768]{2,1,0:T(8,128)(2,1)} %xs.5) | copy-start | bytes 4718596
  0.7 5.7 %copy-start.4 = (bf16[768,192]{0,1:T(8,128)(2,1)S(1)}, bf16[768,192]{0,1:T(8,128)(2,1)}, u32[]{:S(2)}) copy-start(bf16[768,192]{0,1:T(8,128)(2,1)} %param.25) | copy-start | bytes 884740
  0.7 5.7 %copy-start.3 = (bf16[192,768]{1,0:T(8,128)(2,1)S(1)}, bf16[192,768]{1,0:T(8,128)(2,1)}, u32[]{:S(2)}) copy-start(bf16[192,768]{1,0:T(8,128)(2,1)} %p1.1) | copy-start | bytes 884740
  86.9 1.3 copy-start.2
  229.4 4.2 %copy-start.5 = (bf16[4,256,768]{2,1,0:T(8,128)(2,1)S(1)}, bf16[4,256,768]{2,1,0:T(8,128)(2,1)}, u32[]{:S(2)}) copy-start(bf16[4,256,768]{2,1,0:T(8,128)(2,1)} %get-tuple-element.138) | copy-start | bytes 4718596

commit v4 on v3

--- a/solution.py
+++ b/solution.py
@@ -107,7 +107,7 @@
 NINE = ((0, 0), (1, 0), (2, 0), (2, 2), (0, 2), (1, 2), (0, 1), (1, 1), (2, 1))
 AT = {kh: i for i, kh in enumerate(NINE)}
 TURN = (0, 2, 1)
-TAILMB, MIDMB, FRONTMB = 48, 50, 48
+TAILMB, MIDMB, FRONTMB = 48, 50, 60
 
 
 def head(h):
@@ -185,7 +185,9 @@
             c.wait_recv()
 
 
-def front_kernel(p0, p1, p2, vec, xs, seg, W, V, R, S, po, m, x, ss, rs, ls):
+def front_kernel(pw, ow, p1, p2, vec, xs, seg, W, V, R, S, po, m, x, p0, ss, rs, ls):
+    ot = ow[...].astype(f32).T.astype(bf)
+    p0[...] = jnp.concatenate([pw[k, :, head(h)] for k, h in NINE] + [ot[:, head(h)] for h in TURN], axis=1)
     p = Place()
     c = lax.axis_index("ctx")
     core, sib = p.core, p.sib()
@@ -213,8 +215,8 @@
     vn.wait_recv()
     vx += [send(V.at[p.x, 1 - p.yl, core], V.at[p.x, 1 - p.yl, core], p.px(k)[0]) for k in AXES]
     bulk = [
-        Spread(p, send, p1, W.at[1], (0, 96), (96, 64), (160, 32)),
-        Spread(p, send, p2, W.at[2], (0, 64), (64, 64), (128, 64)),
+        Spread(p, send, p1, W.at[1], (0, 32), (32, 96), (128, 64)),
+        Spread(p, send, p2, W.at[2], (0, 64), (64, 96), (160, 32)),
     ]
     for b in bulk:
         b.start()
@@ -265,7 +267,7 @@
         cp.wait()
 
 
-def front(p0, p1, p2, vec, xs, seg, cid):
+def front(pw, ow, p1, p2, vec, xs, seg, cid):
     sd = jax.ShapeDtypeStruct
     vm = pltpu.VMEM
     anywhere, here = pl.BlockSpec(memory_space=pl.ANY), pl.BlockSpec(memory_space=vm)
@@ -278,18 +280,19 @@
             sd((8, BLK, 384), bf),
             sd((8, 2, 128), jnp.int32),
         ),
-        in_specs=[here] * 3 + [anywhere] * 3,
+        in_specs=[here] * 4 + [anywhere] * 3,
         out_specs=[anywhere, here, anywhere, anywhere],
         scratch_shapes=[
             vm((4, 2, 2, 192, 768), bf),
             vm((8, BLK, 384), bf),
             vm((BLK, 768), bf),
+            vm((192, 768), bf),
             pltpu.SemaphoreType.DMA((count,)),
             pltpu.SemaphoreType.DMA((count,)),
             pltpu.SemaphoreType.DMA((6,)),
         ],
-        compiler_params=params(cid),
-    )(p0, p1, p2, vec, xs, seg)
+        compiler_params=params(cid, FRONTMB),
+    )(pw, ow, p1, p2, vec, xs, seg)
 
 
 LONG = 2048 + BLK
@@ -564,7 +567,8 @@
     return [vm(s, bf) for s in shapes]
 
 
-MID = ("yzx", "zyx")
+MID = ("yzx", "zyx", "xyz")
+MIDN = 256
 
 
 def norm_of(v):
@@ -582,18 +586,19 @@
     return jnp.sum(v, axis=0, keepdims=True)
 
 
-def store_pieces(g, t, a, b):
+def store_pieces(g, t, outs):
+    n = 768 // len(outs)
     for i in range(32):
         at = (t, i // 16, i // 8 % 2, i // 4 % 2, i % 4)
         piece = g[24 * i : 24 * i + 24].astype(bf)
-        a[at] = piece[:, :384]
-        b[at] = piece[:, 384:]
-
-
-def mid_kernel(w, cms, xs, cots, vec, LO, dh1, gup, go, DC, sums, o0, o1, *refs):
-    red = [[*refs[3 * i : 3 * i + 3], (o0, o1)[i], None, None, None] for i in range(2)]
-    refs = refs[6:]
-    cm, wv, wo, zs, cdf, act, gs, ga, gb, lob, dcm, x, cot, ss, rs, ls, os = refs
+        for k, out in enumerate(outs):
+            out[at] = piece[:, n * k : n * k + n]
+
+
+def mid_kernel(w, cms, xs, cots, vec, LO, dh1, gup, go, DC, sums, o0, o1, o2, *refs):
+    red = [[*refs[3 * i : 3 * i + 3], (o0, o1, o2)[i], None, None, None] for i in range(3)]
+    refs = refs[9:]
+    cm, wv, wo, zs, cdf, act, gs, ga, gb, gc, lob, dcm, x, cot, ss, rs, ls, os = refs
     p = Place()
     c = lax.axis_index("ctx")
     ctx = [{"ctx": (c + k) % 8} for k in range(1, 8)]
@@ -661,9 +666,9 @@
     y1t = y1.T.astype(bf)
     parts = [Reducer(p, send, o, r) for o, r in zip(MID, red)]
     for t in range(4):
-        store_pieces(nn(dh2t, act[t]), t, ga, gb)
-        parts[0].begin_at(ga, t)
-        parts[1].begin_at(gb, t)
+        store_pieces(nn(dh2t, act[t]), t, (ga, gb, gc))
+        for part, g3 in zip(parts, (ga, gb, gc)):
+            part.begin_at(g3, t)
     dy1 = dh2
     outs = []
     for t in range(4):
@@ -722,12 +727,11 @@
             sd((4, 768, 192), bf),
             sd((8, BLK, 128), bf),
             sd((60, 128), f32),
-            sd((*left[0], 24, 384), bf),
-            sd((*left[1], 24, 384), bf),
+            *[sd((*s, 24, MIDN), bf) for s in left],
         ),
         in_specs=[anywhere] * 4 + [here],
-        out_specs=[anywhere, here, anywhere, here, anywhere, here, here, here],
-        scratch_shapes=sum([reducer_scratch(o, 384)[:3] for o in MID], [])
+        out_specs=[anywhere, here, anywhere, here, anywhere, here, here, here, here],
+        scratch_shapes=sum([reducer_scratch(o, MIDN)[:3] for o in MID], [])
         + [
             vm((8, BLK, 128), bf),
             vm((12, 768, 768), bf),
@@ -736,14 +740,15 @@
             vm((4, BLK, 768), f32),
             vm((4, BLK, 768), bf),
             vm((2, 768, 768), bf),
-            vm((*seven, 384), bf),
-            vm((*seven, 384), bf),
+            vm((*seven, MIDN), bf),
+            vm((*seven, MIDN), bf),
+            vm((*seven, MIDN), bf),
             vm((BLK, 768), bf),
             vm((8, BLK, 128), bf),
             vm((BLK, 768), bf),
             vm((BLK, 768), bf),
-            pltpu.SemaphoreType.DMA((40,)),
-            pltpu.SemaphoreType.DMA((40,)),
+            pltpu.SemaphoreType.DMA((48,)),
+            pltpu.SemaphoreType.DMA((48,)),
             pltpu.SemaphoreType.DMA((15,)),
             pltpu.SemaphoreType.DMA((2,)),
         ],
@@ -755,9 +760,9 @@
 TAILN = (768, 384, 384)
 
 
-def tail_kernel(dm, xs, dh1, w, go, gup, vin, n0, n1, R1, R0, R2, V, IG, *refs):
+def tail_kernel(dm, xs, dh1, w, go, gup, vin, n0, n1, n2, R1, R0, R2, V, IG, *refs):
     red, refs = [refs[7 * i : 7 * i + 7] for i in range(3)], refs[21:]
-    more, refs = [[None] * 3 + [(n0, n1)[i], *refs[3 * i : 3 * i + 3]] for i in range(2)], refs[6:]
+    more, refs = [[None] * 3 + [(n0, n1, n2)[i], *refs[3 * i : 3 * i + 3]] for i in range(3)], refs[9:]
     x, d, wv, ga, gb, igb, acc, vt, vr, ss, rs, ls = refs
     p = Place()
     c = lax.axis_index("ctx")
@@ -777,8 +782,6 @@
     rows.start()
     load.start()
     parts[0].first()
-    for q in (3, 4):
-        parts[q].c2 = parts[q].scatter(parts[q].s1, parts[q].r2, 1)
     rows.wait()
     xt = x[...].astype(f32).T.astype(bf)
     acc[...] = dh1[...]
@@ -786,6 +789,8 @@
     load.wait()
     for cp in sw:
         cp.wait_recv()
+    for q in (3, 4, 5):
+        parts[q].c2 = parts[q].scatter(parts[q].s1, parts[q].r2, 1)
     vt[0, :60] = vin[...]
     for t in range(4):
         a, b = d[2 * t].astype(f32), d[2 * t + 1].astype(f32)
@@ -795,7 +800,7 @@
             vt[0, 60 + 5 * t + k : 61 + 5 * t + k] = sums[:, 128 * k : 128 * k + 128]
         pre = pre.astype(bf)
         g = jnp.concatenate([nn(xt, pre), go[t].astype(f32)], axis=1)
-        store_pieces(g, t, ga, gb)
+        store_pieces(g, t, (ga, gb))
         parts[1].begin_at(ga, t)
         parts[2].begin_at(gb, t)
         acc[...] += nt(pre, wv[t, :, :576])
@@ -817,7 +822,7 @@
         return vt[i] + vr[i, 0] + vr[i, 1] + vr[i, 2]
 
     v1 = vsend(1, "z")
-    for q in (3, 4):
+    for q in (3, 4, 5):
         parts[q].third()
     parts[0].second()
     vt[2] = vsum(1, v1)
@@ -832,25 +837,25 @@
     for cp in ig:
         cp.wait_recv()
     R1[...] = parts[0].result()
-    R2[:, :384] = parts[3].result()
-    R2[:, 384:] = parts[4].result()
+    for q in range(3):
+        R2[:, MIDN * q : MIDN * q + MIDN] = parts[3 + q].result()
     R0[:, :384] = parts[1].result()
     R0[:, 384:] = parts[2].result()
     for cp in send.all:
         cp.wait_send()
 
 
-def finale(dm, xs, dh1, w, go, gup, vin, n0, n1, cid):
+def finale(dm, xs, dh1, w, go, gup, vin, n0, n1, n2, cid):
     vm = pltpu.VMEM
     sd = jax.ShapeDtypeStruct
     anywhere, here = pl.BlockSpec(memory_space=pl.ANY), pl.BlockSpec(memory_space=vm)
     scratch = sum([reducer_scratch(o, n) for o, n in zip(TAIL, TAILN)], [])
-    scratch += sum([reducer_scratch(o, 384)[4:] for o in MID], [])
+    scratch += sum([reducer_scratch(o, MIDN)[4:] for o in MID], [])
     seven = (4, 2, 2, 2, 4, 24)
     return pl.pallas_call(
         tail_kernel,
         out_shape=(sd((24, 768), f32), sd((24, 768), f32), sd((24, 768), f32), sd((80, 128), f32), sd((4, BLK, 768), bf)),
-        in_specs=[anywhere, anywhere, here, anywhere, here, anywhere, here, here, here],
+        in_specs=[anywhere, anywhere, here, anywhere, here, anywhere, here, here, here, here],
         out_specs=[here] * 5,
         scratch_shapes=scratch
         + [
@@ -863,12 +868,12 @@
             vm((BLK, 768), f32),
             vm((4, 80, 128), f32),
             vm((4, 3, 80, 128), f32),
-            pltpu.SemaphoreType.DMA((80,)),
-            pltpu.SemaphoreType.DMA((80,)),
-            pltpu.SemaphoreType.DMA((4,)),
+            pltpu.SemaphoreType.DMA((96,)),
+            pltpu.SemaphoreType.DMA((96,)),
+            pltpu.SemaphoreType.DMA((5,)),
         ],
         compiler_params=params(cid, TAILMB),
-    )(dm, xs, dh1, w, go, gup.reshape(*seven, 768), vin, n0, n1)
+    )(dm, xs, dh1, w, go, gup.reshape(*seven, 768), vin, n0, n1, n2)
 
 
 def finish_kernel(r1, r0, r2, v, g, R1, PG, OG, R2, PB, UB, B0, B1, B2, B3, B4, B5, IG):
@@ -879,20 +884,21 @@
         row = jnp.concatenate([v[6 * i + k : 6 * i + k + 1] for k in range(6)], axis=1)
         row = pltpu.roll(jnp.broadcast_to(row, (8, 768)), (768 - 24 * fc) % 768, 1)
         out[...] = row[:1, :24]
-    UB[...] = jnp.concatenate([v[pl.ds(36 + 6 * x + k, 1)] for k in range(6)], axis=1)
+    for k in range(6):
+        UB[k : k + 1] = v[pl.ds(36 + 6 * x + k, 1)]
     b = jnp.concatenate([v[pl.ds(60 + 5 * x + k, 1)] for k in range(5)], axis=1)
     PB[...] = jnp.concatenate([jnp.concatenate([b[:, head(AT[k, h])] for h in range(3)], axis=1) for k in (0, 2)], axis=0)
-    R2[...] = r2[...].T
+    R2[...] = r2[...]
     p = r0[...]
     for k in range(3):
         PG[k] = jnp.concatenate([p[:, head(AT[k, h])] for h in range(3)], axis=1)
-    OG[...] = jnp.concatenate([p[:, head(9 + TURN[h])] for h in range(3)], axis=1).T
+    OG[...] = jnp.concatenate([p[:, head(9 + TURN[h])] for h in range(3)], axis=1)
 
 
 def finish(*args):
     sd = jax.ShapeDtypeStruct
     here = pl.BlockSpec(memory_space=pltpu.VMEM)
-    shapes = [(24, 768), (3, 24, 192), (192, 24), (768, 24), (2, 192), (1, 768), *[(1, 24)] * 6, (4, BLK, 768)]
+    shapes = [(24, 768), (3, 24, 192), (24, 192), (24, 768), (2, 192), (6, 128), *[(1, 24)] * 6, (4, BLK, 768)]
     return pl.pallas_call(
         finish_kernel,
         out_shape=tuple(sd(s, f32) for s in shapes),
@@ -920,24 +926,21 @@
     cotangent,
 ):
     tp = lax.axis_index("tp")
-    out_t = out_weight.T
-
-    p0 = jnp.concatenate([proj_weight[k, :, head(h)] for k, h in NINE] + [out_t[:, head(h)] for h in TURN], axis=1)
     rows = [out_bias, down_bias, first_gain, first_shift, second_gain, second_shift, proj_bias[0], proj_bias[1]]
     row = lax.broadcasted_iota(jnp.int32, (16, 192), 0)
     vec = jnp.zeros((16, 192), bf)
     for i, v in enumerate(rows + [up_bias[192 * k : 192 * k + 192] for k in range(4)]):
         vec = jnp.where(row == i, v[None], vec)
     seg = lax.dynamic_index_in_dim(segment_ids, tp, 0, keepdims=False).reshape(2, 128)
-    w, vec, r, docs = front(p0, up_weight, down_weight.T, vec, layer_input, seg, 1)
+    w, vec, r, docs = front(proj_weight, out_weight, up_weight, down_weight.T, vec, layer_input, seg, 1)
     w = w.reshape(3, 4, 768, 768)
     cmsg, acc, qa = attend(docs, r)
-    layer_output, dh1, gup, go, dc, sums, n0, n1 = middle(w, cmsg, layer_input, cotangent, vec, 2)
+    layer_output, dh1, gup, go, dc, sums, *firsts = middle(w, cmsg, layer_input, cotangent, vec, 2)
     dmsg = unattend(docs, r, dc, acc, qa)
-    done = finale(dmsg, layer_input, dh1, w, go, gup, sums, n0, n1, 3)
+    done = finale(dmsg, layer_input, dh1, w, go, gup, sums, *firsts, 3)
     r1, proj, out_grad, r2, pb, ub, b0, b1, b2, b3, b4, b5, input_grad = finish(*done)
     ob, db, g1, s1, g2, s2 = [b.reshape(24) for b in (b0, b1, b2, b3, b4, b5)]
-    return (layer_output, input_grad, proj, pb, out_grad, ob, g1, s1, r1, ub.reshape(768), r2, db, g2, s2)
+    return (layer_output, input_grad, proj, pb, out_grad.T, ob, g1, s1, r1, ub.reshape(768), r2.T, db, g2, s2)
 
 
 def solution(mesh):

time: 236 us -> 238 us (level)
  Pallas kernels: 224 us -> 228 us
    pallas_call x1, Pallas kernels: 62.9 us -> 70.2 us  [finale(): pl.pallas_call(tail_kernel, out_shape=(sd((24, 768), f32), sd((24, 768),...]
    pallas_call x1, Pallas kernels: 70.9 us -> 65.4 us  [front(): pl.pallas_call(front_kernel, out_shape=(sd((3, 4, 2, 2, 192, 768), bf), s...]
    pallas_call x1, Pallas kernels: 58.6 us -> 62 us  [middle(): pl.pallas_call(mid_kernel, out_shape=(sd((4, BLK, 768), bf), sd((BLK, 768...]
    unnamed x16 -> x17, local copies, waits for them, and re-layouts: 5.57 us -> 5.4 us
where the time goes in v4:
time: 238 us
  Pallas kernels  228 us (96%)
  local copies, waits for them, and re-layouts  7.65 us (3%)
    pallas_call x1, Pallas kernels, finale(): pl.pallas_call(tail_kernel, out_shape=(sd((24, 768), f32), sd((24, 768),...  70.2 us
    pallas_call x1, Pallas kernels, front(): pl.pallas_call(front_kernel, out_shape=(sd((3, 4, 2, 2, 192, 768), bf), s...  65.4 us
    pallas_call x1, Pallas kernels, middle(): pl.pallas_call(mid_kernel, out_shape=(sd((4, BLK, 768), bf), sd((BLK, 768...  62 us
    pallas_call x1, Pallas kernels, unattend(): pl.pallas_call(unattend_kernel, out_shape=jax.ShapeDtypeStruct((8, BLK, 3...  19 us
    pallas_call x1, Pallas kernels, attend(): pl.pallas_call(attend_kernel, out_shape=(sd((8, BLK, 128), bf), sd((2, 20...  9.57 us
    unnamed x17, local copies, waits for them, and re-layouts  5.4 us

profile of v4, /device:TPU:1, one launch (start us, length us, event | category | flops | bytes accessed | tf_op | source)
XLA Modules:
  0.0 238.0 jit_solution(9794607058900608583)
XLA Ops:
  0.6 0.0 copy-start
  0.7 0.7 copy-done
  1.3 0.6 constant_dynamic-slice_fusion
  1.9 0.8 slice_reduce_fusion.1
  2.7 0.9 fusion
  3.7 1.4 select_select_fusion.vec
  5.1 65.4 %shard_map.254 = (bf16[3,4,2,2,192,768]{5,4,3,2,1,0:T(8,128)(2,1)}, bf16[4,2,2,16,192]{4,3,2,1,0:T(8,128)(2,1)}, bf16[8,256,384]{2,1,0:T(8,128)(2,1)}, s32[8,2,128]{2,1,0:T(2,128)}) custom-call(bf16[3,192,192]{2,1,0:T(8,128)(2,1)} %pw.1, bf16[192,192]{1,0:T(8,128)(2,1)} %ow.1, bf16[192,768]{1,0:T(8,128)(2,1)} %p1.1, bf16[192,768]{1,0:T(8,128)(2,1)} %bitcast.16, ...), custom_call_target="tpu_custom_call" | custom-call | tf_op jit(solution)/shard_map/pallas_call | solution.py:275
  70.5 0.0 copy-start.1
  70.5 1.4 copy-done.1
  71.9 0.0 copy-start.5
  71.9 0.7 copy-done.5
  72.6 0.0 copy-start.4
  72.6 9.6 %shard_map.255 = (bf16[8,256,128]{2,1,0:T(8,128)(2,1)S(1)}, f32[2,2048,128]{2,1,0:T(8,128)S(1)}, bf16[2,2048,128]{2,1,0:T(8,128)(2,1)S(1)}) custom-call(s32[8,2,128]{2,1,0:T(2,128)S(1)} %copy-done.5, s32[8,2,128]{2,1,0:T(2,128)S(1)} %copy-done.5, bf16[8,256,384]{2,1,0:T(8,128)(2,1)S(1)} %copy-done.1), custom_call_target="tpu_custom_call" | custom-call | tf_op jit(solution)/shard_map/pallas_call | solution.py:416
  82.2 0.0 copy-start.3
  82.2 1.3 copy-done.3
  83.5 0.0 copy-done.4
  83.5 0.0 copy-start.2
  83.5 0.0 copy-start.6
  83.5 62.0 %shard_map.256 = (bf16[4,256,768]{2,1,0:T(8,128)(2,1)}, f32[256,768]{1,0:T(8,128)S(1)}, bf16[4,768,768]{2,1,0:T(8,128)(2,1)}, bf16[4,768,192]{2,1,0:T(8,128)(2,1...) custom-call(bf16[3,4,768,768]{3,2,1,0:T(8,128)(2,1)} %bitcast.13, ...), custom_call_target="tpu_custom_call" | custom-call | tf_op jit(solution)/shard_map/pallas_call | solution.py:721
  145.5 0.0 copy-done.2
  145.5 0.0 copy-done.6
  145.5 19.0 %shard_map.257.dm = bf16[8,256,384]{2,1,0:T(8,128)(2,1)S(1)} custom-call(s32[8,2,128]{2,1,0:T(2,128)S(1)} %copy-done.6, s32[8,2,128]{2,1,0:T(2,128)S(1)} %copy-done.6, bf16[8,256,384]{2,1,0:T(8,128)(2,1)S(1)} %copy-done.2, bf16[8,256,128]{2,1,0:T(8,128)(2,1)S(1)} %get-tuple-element.54.dc, f32[2,2048,128]{2,1,0:T(8,128)} %copy-done.3, ...), custom_call_target="tpu_custom_call" | custom-call | tf_op jit(solution)/shard_map/pallas_call | solution.py:486
  164.6 70.2 %shard_map.258 = (f32[24,768]{1,0:T(8,128)S(1)}, f32[24,768]{1,0:T(8,128)S(1)}, f32[24,768]{1,0:T(8,128)S(1)}, f32[80,128]{1,0:T(8,128)S(1)}, bf16[4,256,768]{2,1,0:T(8,128)(2,1)S(1)}) custom-call(bf16[8,256,384]{2,1,0:T(8,128)(2,1)S(1)} %shard_map.257.dm, bf16[4,256,768]{2,1,0:T(8,128)(2,1)} %xs.5, f32[256,768]{1,0:T(8,128)S(1)} %get-tuple-element.57.dh1, ...), custom_call_target="tpu_custom_call" | custom-call | tf_op jit(solution)/shard_map/pallas_call | solution.py:855
  234.7 0.0 copy-start.7
  234.7 2.0 shard_map.259
  236.7 0.2 copy-done.7
  236.8 1.1 copy.30
  (6 shorter events, 0.0 us)
Async XLA Ops:
  0.6 0.7 copy-start
  70.5 1.4 copy-start.1
  71.9 0.7 copy-start.5
  72.6 10.9 %copy-start.4 = (bf16[4,2,2,16,192]{4,3,2,1,0:T(8,128)(2,1)S(1)}, bf16[4,2,2,16,192]{4,3,2,1,0:T(8,128)(2,1)}, u32[]{:S(2)}) copy-start(bf16[4,2,2,16,192]{4,3,2,1,0:T(8,128)(2,1)} %get-tuple-element.52.vec) | copy-start | bytes 294916
  82.2 1.3 copy-start.3
  83.5 62.0 %copy-start.2 = (bf16[8,256,384]{2,1,0:T(8,128)(2,1)S(1)}, bf16[8,256,384]{2,1,0:T(8,128)(2,1)}, u32[]{:S(2)}) copy-start(bf16[8,256,384]{2,1,0:T(8,128)(2,1)} %get-tuple-element.50.r) | copy-start | bytes 4718596
  83.5 62.0 %copy-start.6 = (s32[8,2,128]{2,1,0:T(2,128)S(1)}, s32[8,2,128]{2,1,0:T(2,128)}, u32[]{:S(2)}) copy-start(s32[8,2,128]{2,1,0:T(2,128)} %get-tuple-element.49.edge.docs) | copy-start | bytes 24580
  234.7 2.1 copy-start.7
